TPU v7x, 32 devices: a whole 2x2x4 slice. The times are simulated.
32 devices in a mesh: rep: 16 (over z, x, core), shard: 2 (over y).
Axes of the slice: x: 2, y: 2, z: 4, core: 2. Of those that a mesh axis runs over, the one named last changes fastest.
Arguments:
- patches: bfloat16 [16384, 1280], P(('rep', 'shard')), may hold values from -6 to 6
- lengths: int32 [32, 4], P(('rep', 'shard')), may hold values from 1 to 256, 512 in all within a row
- positions: int32 [2, 16384], P(None, ('rep', 'shard')), may hold values from 0 to 63
- ln1_gain: bfloat16 [1280], P('shard'), may hold values from 0.5 to 1.5
- ln1_bias: bfloat16 [1280], P('shard'), may hold values from -3 to 3
- qkv_weight: bfloat16 [1280, 3840], P('shard'), may hold values from -0.15625 to 0.15625
- qkv_bias: bfloat16 [3840], P('shard'), may hold values from -3 to 3
- proj_weight: bfloat16 [1280, 1280], P('shard'), may hold values from -1.25 to 1.25
- proj_bias: bfloat16 [1280], P('shard'), may hold values from -3 to 3
- ln2_gain: bfloat16 [1280], P('shard'), may hold values from 0.5 to 1.5
- ln2_bias: bfloat16 [1280], P('shard'), may hold values from -3 to 3
- fc1_weight: bfloat16 [1280, 5120], P('shard'), may hold values from -0.15625 to 0.15625
- fc1_bias: bfloat16 [5120], P('shard'), may hold values from -3 to 3
- fc2_weight: bfloat16 [5120, 1280], P('shard'), may hold values from -0.125 to 0.125
- fc2_bias: bfloat16 [1280], P('shard'), may hold values from -3 to 3
- cotangent: bfloat16 [16384, 1280], P(('rep', 'shard')), may hold values from -6 to 6
Outputs:
- layer_out: bfloat16 [16384, 1280], P(('rep', 'shard'))
- d_patches: float32 [16384, 1280], P(('rep', 'shard'))
- d_ln1_gain: float32 [1280], P('shard')
- d_ln1_bias: float32 [1280], P('shard')
- d_qkv_weight: float32 [1280, 3840], P('shard')
- d_qkv_bias: float32 [3840], P('shard')
- d_proj_weight: float32 [1280, 1280], P('shard')
- d_proj_bias: float32 [1280], P('shard')
- d_ln2_gain: float32 [1280], P('shard')
- d_ln2_bias: float32 [1280], P('shard')
- d_fc1_weight: float32 [1280, 5120], P('shard')
- d_fc1_bias: float32 [5120], P('shard')
- d_fc2_weight: float32 [5120, 1280], P('shard')
- d_fc2_bias: float32 [1280], P('shard')
Inputs may be any that keep to these rules, and one draw needn't show every extreme that they name: `lengths`: each row's entries sum to 512; its largest entry is 256.
All inputs are finite; a program needn't handle non-finite values.
Results may differ from a plain program's by a relative error of at most 0.012.
The roundings to bfloat16 on the way count: a program that leaves them out, or rounds other values in their place, can miss the bound.
Values may be sent and summed in bfloat16 or wider, within the bound.
A program may use at most 320 MiB of HBM per device.

v0:
```python
from functools import partial

import jax
import jax.numpy as jnp
from jax import lax
from jax.sharding import PartitionSpec as P

HEADS = 16


norm_eps = 1e-06
quick_slope = 1.702


def apply_layer_norm(matrix):
    center = matrix - jnp.mean(matrix, axis=-1, keepdims=True)
    spread = jnp.mean(center * center, axis=-1, keepdims=True)
    inverse_spread = lax.rsqrt(spread + norm_eps)
    return (center * inverse_spread, inverse_spread)


def norm_gradient_step(normalized_gradient, centered_standard, inverse_spread, norm_gain):
    scaled_rows = normalized_gradient * norm_gain
    return inverse_spread * (
        scaled_rows
        - jnp.mean(scaled_rows, axis=-1, keepdims=True)
        - centered_standard * jnp.mean(scaled_rows * centered_standard, axis=-1, keepdims=True)
    )


def rotary_tables(positions, head_size):
    quarter = head_size // 4
    counter = jnp.arange(quarter, dtype=jnp.float32)
    inverse = jnp.power(jnp.float32(10000.0), -2.0 * counter / (head_size // 2))
    row_angle = positions[0].astype(jnp.float32)[:, None] * inverse[None, :]
    col_angle = positions[1].astype(jnp.float32)[:, None] * inverse[None, :]
    angle = jnp.concatenate([row_angle, col_angle], axis=1)
    angle = jnp.concatenate([angle, angle], axis=1)
    return (jnp.cos(angle), jnp.sin(angle))


def apply_rotary(matrix, cosine, sine):
    half_size = matrix.shape[-1] // 2
    turned = jnp.concatenate([-matrix[..., half_size:], matrix[..., :half_size]], axis=-1)
    return matrix * cosine[:, None, :] + turned * sine[:, None, :]


def rotary_back(grad_rows, cosine, sine):
    half_size = grad_rows.shape[-1] // 2
    sined = grad_rows * sine[:, None, :]
    turned = jnp.concatenate([sined[..., half_size:], -sined[..., :half_size]], axis=-1)
    return grad_rows * cosine[:, None, :] + turned


def masked_scores(queries, keys_rot, ident, score_scale):
    scores = (
        jnp.einsum("qhd,khd->hqk", queries, keys_rot, preferred_element_type=jnp.float32)
        * score_scale
    )
    same_pic = ident[:, None] == ident[None, :]
    return jnp.where(same_pic[None], scores, -1000000000.0)


def attend(pieces, score_scale):
    queries, keys_rot, values_all, ident = pieces
    scores = masked_scores(queries, keys_rot, ident, score_scale)
    top_score = jnp.max(scores, axis=2, keepdims=True)
    exp_scores = jnp.exp(scores - top_score)
    total = jnp.sum(exp_scores, axis=2, keepdims=True)
    probs = (exp_scores / total).astype(jnp.bfloat16)
    attended = jnp.einsum("hqk,khd->qhd", probs, values_all, preferred_element_type=jnp.float32)
    return (attended, (top_score + jnp.log(total))[:, :, 0])


def attend_back(pieces, score_scale):
    queries, keys_rot, values_all, ident, grad_heads, log_total = pieces
    scores = masked_scores(queries, keys_rot, ident, score_scale)
    probs = jnp.exp(scores - log_total[:, :, None])
    grad_probs = jnp.einsum(
        "qhd,khd->hqk", grad_heads, values_all, preferred_element_type=jnp.float32
    )
    inner = jnp.sum(probs * grad_probs, axis=2, keepdims=True)
    grad_scores = (probs * (grad_probs - inner)).astype(jnp.bfloat16)
    grad_query = (
        jnp.einsum("hqk,khd->qhd", grad_scores, keys_rot, preferred_element_type=jnp.float32)
        * score_scale
    )
    grad_key = (
        jnp.einsum("hqk,qhd->khd", grad_scores, queries, preferred_element_type=jnp.float32)
        * score_scale
    )
    grad_value = jnp.einsum(
        "hqk,qhd->khd", probs.astype(jnp.bfloat16), grad_heads, preferred_element_type=jnp.float32
    )
    return (grad_query, grad_key, grad_value)


def row_product(left, right):
    return jnp.einsum("ti,tj->ij", left, right, preferred_element_type=jnp.float32)


def back_product(grad_rows, weight_full):
    return jnp.einsum("tj,ij->ti", grad_rows, weight_full, preferred_element_type=jnp.float32)


def per_device(
    patches,
    lengths,
    positions,
    ln1_gain,
    ln1_bias,
    qkv_weight,
    qkv_bias,
    proj_weight,
    proj_bias,
    ln2_gain,
    ln2_bias,
    fc1_weight,
    fc1_bias,
    fc2_weight,
    fc2_bias,
    cotangent,
):
    pack_count = lengths.shape[0]
    row_count = patches.shape[0]
    length = row_count // pack_count
    model_width = patches.shape[1]
    head_count = HEADS
    head_size = model_width // head_count
    score_scale = head_size ** (-0.5)
    pic_ends = jnp.cumsum(lengths[:, :-1], axis=1)
    slot_index = jnp.arange(length, dtype=jnp.int32)
    idents = jnp.sum((slot_index[None, :, None] >= pic_ends[:, None, :]).astype(jnp.int32), axis=2)
    cosine, sine = rotary_tables(positions, head_size)
    pack_shape = (pack_count, length, head_count, head_size)
    first_norm_gain, first_norm_bias, w_qkv, b_qkv, w_proj, b_proj = (
        lax.all_gather(ln1_gain, "shard", axis=0, tiled=True),
        lax.all_gather(ln1_bias, "shard", axis=0, tiled=True),
        lax.all_gather(qkv_weight, "shard", axis=0, tiled=True),
        lax.all_gather(qkv_bias, "shard", axis=0, tiled=True),
        lax.all_gather(proj_weight, "shard", axis=0, tiled=True),
        lax.all_gather(proj_bias, "shard", axis=0, tiled=True),
    )
    input_rows = patches.astype(jnp.float32)
    first_centered_standard, first_inverse_spread = apply_layer_norm(input_rows)
    first_normalized = (
        first_centered_standard * first_norm_gain.astype(jnp.float32)
        + first_norm_bias.astype(jnp.float32)
    ).astype(jnp.bfloat16)
    qkv_rows = jnp.dot(first_normalized, w_qkv, preferred_element_type=jnp.float32) + b_qkv.astype(
        jnp.float32
    )
    qkv_rows = qkv_rows.reshape(row_count, 3, head_count, head_size)
    queries = apply_rotary(qkv_rows[:, 0], cosine, sine).astype(jnp.bfloat16).reshape(pack_shape)
    keys_rot = apply_rotary(qkv_rows[:, 1], cosine, sine).astype(jnp.bfloat16).reshape(pack_shape)
    values_all = qkv_rows[:, 2].astype(jnp.bfloat16).reshape(pack_shape)
    attended, log_total = lax.map(
        partial(attend, score_scale=score_scale), (queries, keys_rot, values_all, idents)
    )
    heads_out = attended.reshape(row_count, model_width).astype(jnp.bfloat16)
    hidden_rows = (
        input_rows
        + jnp.dot(heads_out, w_proj, preferred_element_type=jnp.float32)
        + b_proj.astype(jnp.float32)
    )
    second_norm_gain, second_norm_bias, w_up, b_up, w_down, b_down = (
        lax.all_gather(ln2_gain, "shard", axis=0, tiled=True),
        lax.all_gather(ln2_bias, "shard", axis=0, tiled=True),
        lax.all_gather(fc1_weight, "shard", axis=0, tiled=True),
        lax.all_gather(fc1_bias, "shard", axis=0, tiled=True),
        lax.all_gather(fc2_weight, "shard", axis=0, tiled=True),
        lax.all_gather(fc2_bias, "shard", axis=0, tiled=True),
    )
    second_centered_standard, second_inverse_spread = apply_layer_norm(hidden_rows)
    second_normalized = (
        second_centered_standard * second_norm_gain.astype(jnp.float32)
        + second_norm_bias.astype(jnp.float32)
    ).astype(jnp.bfloat16)
    up_pre = jnp.dot(second_normalized, w_up, preferred_element_type=jnp.float32) + b_up.astype(
        jnp.float32
    )
    sigmoid_up = 1.0 / (1.0 + jnp.exp(-quick_slope * up_pre))
    activation = (up_pre * sigmoid_up).astype(jnp.bfloat16)
    out_full = (
        hidden_rows
        + jnp.dot(activation, w_down, preferred_element_type=jnp.float32)
        + b_down.astype(jnp.float32)
    )
    layer_out = out_full.astype(jnp.bfloat16)
    second_norm_gain, second_norm_bias, w_up, b_up, w_down, b_down = (
        lax.all_gather(ln2_gain, "shard", axis=0, tiled=True),
        lax.all_gather(ln2_bias, "shard", axis=0, tiled=True),
        lax.all_gather(fc1_weight, "shard", axis=0, tiled=True),
        lax.all_gather(fc1_bias, "shard", axis=0, tiled=True),
        lax.all_gather(fc2_weight, "shard", axis=0, tiled=True),
        lax.all_gather(fc2_bias, "shard", axis=0, tiled=True),
    )
    grad_out = cotangent.astype(jnp.float32)
    d_w_down = row_product(activation, cotangent)
    d_b_down = jnp.sum(grad_out, axis=0)
    grad_act = back_product(cotangent, w_down)
    slope_up = sigmoid_up + quick_slope * up_pre * sigmoid_up * (1.0 - sigmoid_up)
    grad_pre = (grad_act * slope_up).astype(jnp.bfloat16)
    d_w_up = row_product(second_normalized, grad_pre)
    d_b_up = jnp.sum(grad_pre.astype(jnp.float32), axis=0)
    second_normalized_gradient = back_product(grad_pre, w_up)
    second_gain_gradient = jnp.sum(second_normalized_gradient * second_centered_standard, axis=0)
    d_bias_two = jnp.sum(second_normalized_gradient, axis=0)
    grad_hidden = grad_out + norm_gradient_step(
        second_normalized_gradient,
        second_centered_standard,
        second_inverse_spread,
        second_norm_gain.astype(jnp.float32),
    )
    m_gain, m_bias, m_up, m_upb, m_down, m_downb = (
        lax.psum_scatter(second_gain_gradient, "shard", scatter_dimension=0, tiled=True),
        lax.psum_scatter(d_bias_two, "shard", scatter_dimension=0, tiled=True),
        lax.psum_scatter(d_w_up, "shard", scatter_dimension=0, tiled=True),
        lax.psum_scatter(d_b_up, "shard", scatter_dimension=0, tiled=True),
        lax.psum_scatter(d_w_down, "shard", scatter_dimension=0, tiled=True),
        lax.psum_scatter(d_b_down, "shard", scatter_dimension=0, tiled=True),
    )
    m_gain, m_bias, m_up, m_upb, m_down, m_downb = lax.psum(
        (m_gain, m_bias, m_up, m_upb, m_down, m_downb), "rep"
    )
    first_norm_gain, first_norm_bias, w_qkv, b_qkv, w_proj, b_proj = (
        lax.all_gather(ln1_gain, "shard", axis=0, tiled=True),
        lax.all_gather(ln1_bias, "shard", axis=0, tiled=True),
        lax.all_gather(qkv_weight, "shard", axis=0, tiled=True),
        lax.all_gather(qkv_bias, "shard", axis=0, tiled=True),
        lax.all_gather(proj_weight, "shard", axis=0, tiled=True),
        lax.all_gather(proj_bias, "shard", axis=0, tiled=True),
    )
    grad_branch = grad_hidden.astype(jnp.bfloat16)
    d_w_proj = row_product(heads_out, grad_branch)
    d_b_proj = jnp.sum(grad_branch.astype(jnp.float32), axis=0)
    grad_heads = back_product(grad_branch, w_proj).astype(jnp.bfloat16).reshape(pack_shape)
    grad_query, grad_key, grad_value = lax.map(
        partial(attend_back, score_scale=score_scale),
        (queries, keys_rot, values_all, idents, grad_heads, log_total),
    )
    rows_shape = (row_count, head_count, head_size)
    grad_query = rotary_back(grad_query.reshape(rows_shape), cosine, sine)
    grad_key = rotary_back(grad_key.reshape(rows_shape), cosine, sine)
    grad_qkv = (
        jnp.stack([grad_query, grad_key, grad_value.reshape(rows_shape)], axis=1)
        .reshape(row_count, 3 * model_width)
        .astype(jnp.bfloat16)
    )
    d_w_qkv = row_product(first_normalized, grad_qkv)
    d_b_qkv = jnp.sum(grad_qkv.astype(jnp.float32), axis=0)
    first_normalized_gradient = back_product(grad_qkv, w_qkv)
    first_gain_gradient = jnp.sum(first_normalized_gradient * first_centered_standard, axis=0)
    d_bias_one = jnp.sum(first_normalized_gradient, axis=0)
    d_patches = grad_hidden + norm_gradient_step(
        first_normalized_gradient,
        first_centered_standard,
        first_inverse_spread,
        first_norm_gain.astype(jnp.float32),
    )
    a_gain, a_bias, a_qkv, a_qkvb, a_proj, a_projb = (
        lax.psum_scatter(first_gain_gradient, "shard", scatter_dimension=0, tiled=True),
        lax.psum_scatter(d_bias_one, "shard", scatter_dimension=0, tiled=True),
        lax.psum_scatter(d_w_qkv, "shard", scatter_dimension=0, tiled=True),
        lax.psum_scatter(d_b_qkv, "shard", scatter_dimension=0, tiled=True),
        lax.psum_scatter(d_w_proj, "shard", scatter_dimension=0, tiled=True),
        lax.psum_scatter(d_b_proj, "shard", scatter_dimension=0, tiled=True),
    )
    a_gain, a_bias, a_qkv, a_qkvb, a_proj, a_projb = lax.psum(
        (a_gain, a_bias, a_qkv, a_qkvb, a_proj, a_projb), "rep"
    )
    return (
        layer_out,
        d_patches,
        a_gain,
        a_bias,
        a_qkv,
        a_qkvb,
        a_proj,
        a_projb,
        m_gain,
        m_bias,
        m_up,
        m_upb,
        m_down,
        m_downb,
    )


def solution(mesh):
    in_specs = (
        P(("rep", "shard"), None),
        P(("rep", "shard"), None),
        P(None, ("rep", "shard")),
        P("shard"),
        P("shard"),
        P("shard", None),
        P("shard"),
        P("shard", None),
        P("shard"),
        P("shard"),
        P("shard"),
        P("shard", None),
        P("shard"),
        P("shard", None),
        P("shard"),
        P(("rep", "shard"), None),
    )
    out_specs = (
        P(("rep", "shard"), None),
        P(("rep", "shard"), None),
        P("shard"),
        P("shard"),
        P("shard", None),
        P("shard"),
        P("shard", None),
        P("shard"),
        P("shard"),
        P("shard"),
        P("shard", None),
        P("shard"),
        P("shard", None),
        P("shard"),
    )
    return jax.shard_map(
        per_device, mesh=mesh, in_specs=in_specs, out_specs=out_specs, check_vma=False
    )
```

profile of v0, /device:TPU:0, one launch (start us, length us, event | category | flops | bytes accessed | tf_op | source)
XLA Modules:
  0.0 2157.3 jit_solution(15266474193244514854)
XLA Ops:
  10.2 5.3 all-gather.4
  38.3 4.7 all-gather.6
  45.8 89.2 %all-gather.13.cloned.1.call-done = bf16[1280,3840]{1,0:T(8,128)(2,1)} async-done(((bf16[640,3840]{1,0:T(8,128)(2,1)}), bf16[1280,3840]{1,0:T(8,128)(2,1)}) %all-gather.13.cloned.1.call-update) | async-done | bytes 9830416 | tf_op jit(solution)/shard_map/all_gather | solution.py:139
  135.0 11.5 convolution_add_fusion
  146.6 9.2 copy.51
  162.9 7.7 fusion.51
  170.6 8.3 fusion
  178.9 10.5 fusion.32
  189.4 5.9 fusion.52
  195.7 147.2 %all-gather.17.cloned.1.call-done = bf16[1280,5120]{1,0:T(8,128)(2,1)} async-done(((bf16[640,5120]{1,0:T(8,128)(2,1)}), bf16[1280,5120]{1,0:T(8,128)(2,1)}) %all-gather.17.cloned.1.call-update) | async-done | bytes 13107216 | tf_op jit(solution)/shard_map/all_gather | solution.py:169
  342.9 13.6 fusion.47
  356.5 146.1 %all-gather.19.cloned.1.call-done = bf16[5120,1280]{1,0:T(8,128)(2,1)} async-done(((bf16[2560,1280]{1,0:T(8,128)(2,1)}), bf16[5120,1280]{1,0:T(8,128)(2,1)}) %all-gather.19.cloned.1.call-update) | async-done | bytes 13107216 | tf_op jit(solution)/shard_map/all_gather | solution.py:171
  502.6 16.9 convert_reduce_fusion
  519.4 15.0 multiply_reduce_fusion.1
  544.0 5.7 convolution_convert_fusion
  552.5 12.1 multiply_reduce_fusion
  564.6 12.1 multiply_convert_fusion
  583.9 8.7 fusion.29
  595.6 10.0 fusion.43
  605.7 15.4 fusion.48
  621.2 15.4 fusion.46
  637.3 12.7 fusion.21
  650.1 196.3 %reduce-scatter.5.cloned.1.call-done = f32[640,3840]{1,0:T(8,128)} async-done(((f32[1280,3840]{1,0:T(8,128)}), f32[640,3840]{1,0:T(8,128)}) %reduce-scatter.5.cloned.1.call-update) | async-done | bytes 9830416 | tf_op jit(solution)/shard_map/reduce_scatter | solution.py:264
  846.5 293.0 %reduce-scatter.11.cloned.1.call-done = f32[2560,1280]{1,0:T(8,128)} async-done(((f32[5120,1280]{1,0:T(8,128)}), f32[2560,1280]{1,0:T(8,128)}) %reduce-scatter.11.cloned.1.call-update) | async-done | bytes 13107216 | tf_op jit(solution)/shard_map/reduce_scatter | solution.py:220
  1139.5 293.0 %reduce-scatter.9.cloned.1.call-done = f32[640,5120]{1,0:T(8,128)} async-done(((f32[1280,5120]{1,0:T(8,128)}), f32[640,5120]{1,0:T(8,128)}) %reduce-scatter.9.cloned.1.call-update) | async-done | bytes 13107216 | tf_op jit(solution)/shard_map/reduce_scatter | solution.py:218
  1440.1 5.3 fusion.20
  1445.4 15.7 fusion.14
  1467.3 63.9 %all-reduce.8 = (f32[640]{0:T(1024)}, f32[640]{0:T(1024)}, f32[1920]{0:T(1024)}, f32[640]{0:T(1024)}, f32[640]{0:T(1024)}, /*index=5*/f32[640]{0:T(1024)}, f32[2560]{0:T(1024)}, f32[640]{0:T(1024)}) all-reduce(f32[640]{0:T(1024)S(1)} %dynamic-slice.4, f32[640]{0:T(1024)S(1)} %dynamic-slice.6, ...), channel_id=1, replica_groups=mesh['rep'=16,'shard'=2] {'rep'}, use_global_device_ids=true, to_apply=%region_15.16 | all-reduce | flops 8320 | bytes 66560 | tf_op jit(solution)/shard_map/psum | solution.py:269
  1531.3 586.7 %all-reduce.14.cloned.1.call-done = (f32[640,3840]{1,0:T(8,128)}, f32[640,1280]{1,0:T(8,128)}, f32[640,5120]{1,0:T(8,128)}, f32[2560,1280]{1,0:T(8,128)}) async-done(((f32[640,3840]{1,0:T(8,128)}, f32[640,1280]{1,0:T(8,128)}, f32[640,5120]{1,0:T(8,128)}, f32[2560,1280]{1,0:T(8,128)}), (f32[640,3840]{1,0:T(8,128)}, f32[640,1280]{1,0:T(8,128)}, f32[640,5120]{1,0:T(8,128)}, ...) | async-done | bytes 39321616 | tf_op jit(solution)/shard_map/psum | solution.py:269
  2118.0 8.4 copy.73
  2128.2 11.3 copy.75
  2139.5 10.5 copy.76
  (165 shorter events, 72.5 us)
Async XLA Ops:
  7.2 127.8 %all-gather.13.cloned.1.call-start = ((), (), s32[]{:S(2)}) async-start(), calls=%async_computation.4 | async-start | bytes 14745600 | tf_op jit(solution)/shard_map/all_gather | solution.py:139
  7.9 181.4 %all-gather.15.cloned.1.call-start = ((), (), s32[]{:S(2)}) async-start(), calls=%async_computation.5 | async-start | bytes 4915200 | tf_op jit(solution)/shard_map/all_gather | solution.py:141
  8.7 334.2 %all-gather.17.cloned.1.call-start = ((), (), s32[]{:S(2)}) async-start(), calls=%async_computation.6 | async-start | bytes 19660800 | tf_op jit(solution)/shard_map/all_gather | solution.py:169
  9.5 24.0 %copy-start.23 = (bf16[1920]{0:T(1024)(128)(2,1)S(1)}, bf16[1920]{0:T(1024)(128)(2,1)}, u32[]{:S(2)}) copy-start(bf16[1920]{0:T(1024)(128)(2,1)} %param.22) | copy-start | bytes 11524
  9.5 28.8 %copy-start.22 = (bf16[2560]{0:T(1024)(128)(2,1)S(1)}, bf16[2560]{0:T(1024)(128)(2,1)}, u32[]{:S(2)}) copy-start(bf16[2560]{0:T(1024)(128)(2,1)} %param.28) | copy-start | bytes 15364
  9.5 33.6 %copy-start.31 = (s32[1,4]{1,0:T(1,128)S(1)}, s32[1,4]{1,0:T(1,128)}, u32[]{:S(2)}) copy-start(s32[1,4]{1,0:T(1,128)} %param.17) | copy-start | bytes 52
  9.5 33.9 %copy-start.24 = (s32[2,512]{1,0:T(2,128)S(1)}, s32[2,512]{1,0:T(2,128)}, u32[]{:S(2)}) copy-start(s32[2,512]{1,0:T(2,128)} %param.18) | copy-start | bytes 12292
  9.5 35.3 %copy-start.1 = (bf16[512,1280]{1,0:T(8,128)(2,1)S(1)}, bf16[512,1280]{1,0:T(8,128)(2,1)}, u32[]{:S(2)}) copy-start(bf16[512,1280]{1,0:T(8,128)(2,1)} %param.16) | copy-start | bytes 3932164
  9.5 493.1 %all-gather.19.cloned.1.call-start = ((), (), s32[]{:S(2)}) async-start(), calls=%async_computation.7 | async-start | bytes 19660800 | tf_op jit(solution)/shard_map/all_gather | solution.py:171
  10.1 640.1 %reduce-scatter.7.cloned.1.call-start = ((), (), s32[]{:S(2)}) async-start(), calls=%async_computation.9 | async-start | bytes 9830400 | tf_op jit(solution)/shard_map/reduce_scatter | solution.py:266
  20.0 126.6 %copy-start.14 = (f32[1280]{0:T(1024)}, f32[1280]{0:T(1024)S(1)}, u32[]{:S(2)}) copy-start(f32[1280]{0:T(1024)S(1)} %reshape.326) | copy-start | bytes 15364
  28.8 117.7 %copy-start.20 = (f32[1280]{0:T(1024)}, f32[1280]{0:T(1024)S(1)}, u32[]{:S(2)}) copy-start(f32[1280]{0:T(1024)S(1)} %reshape.327) | copy-start | bytes 15364
  45.0 101.5 %copy-start.16 = (f32[512]{0:T(512)}, f32[512]{0:T(512)S(1)}, u32[]{:S(2)}) copy-start(f32[512]{0:T(512)S(1)} %broadcast_multiply_fusion.9) | copy-start | bytes 6148
  45.5 101.0 %copy-start.18 = (f32[512]{0:T(512)}, f32[512]{0:T(512)S(1)}, u32[]{:S(2)}) copy-start(f32[512]{0:T(512)S(1)} %add_rsqrt_fusion.1) | copy-start | bytes 6148
  155.8 4.3 slice-start
  162.9 7.7 copy-start.3
  162.9 7.7 copy-start.6
  519.4 15.0 copy-start.11
  534.4 4.8 copy-start.8
  543.9 302.6 %reduce-scatter.5.cloned.1.call-start = ((), (), s32[]{:S(2)}) async-start(), calls=%async_computation.8 | async-start | bytes 29491200 | tf_op jit(solution)/shard_map/reduce_scatter | solution.py:264
  564.6 12.1 copy-start.7
  592.6 3.0 copy-start.2
  592.6 3.0 copy-start.15
  592.6 3.0 copy-start.17
  592.6 3.0 copy-start.19
  592.7 3.0 copy-start.21
  605.7 533.8 %reduce-scatter.11.cloned.1.call-start = ((), (), s32[]{:S(2)}) async-start(), calls=%async_computation.11 | async-start | bytes 39321600 | tf_op jit(solution)/shard_map/reduce_scatter | solution.py:220
  621.1 811.3 %reduce-scatter.9.cloned.1.call-start = ((), (), s32[]{:S(2)}) async-start(), calls=%async_computation.10 | async-start | bytes 39321600 | tf_op jit(solution)/shard_map/reduce_scatter | solution.py:218
  636.6 824.6 %all-reduce.16.cloned.1.call-start = ((), (), s32[]{:S(2)}) async-start(), calls=%async_computation.13 | async-start | bytes 172032
  650.1 1468.0 %all-reduce.14.cloned.1.call-start = ((), (), s32[]{:S(2)}) async-start(), calls=%async_computation.12 | async-start | bytes 78643200 | tf_op jit(solution)/shard_map/psum | solution.py:269
  1432.4 3.2 copy-start.30
  2118.0 8.5 copy-start.10
  (13 other events, 17.7 us)
Sparse Core Ops, SparseCore 0:
  9.5 125.4 all-gather.12
  136.6 46.4 all-gather.14
  184.6 158.2 all-gather.16
  344.3 158.2 all-gather.18
  544.0 79.9 reduce-scatter.6
  626.2 220.1 reduce-scatter.4
  848.8 290.6 reduce-scatter.10
  1141.8 290.6 reduce-scatter.8
  1436.3 20.8 all-reduce.15
  1461.9 656.1 all-reduce.13
where the time goes:
time: 2170 us; the launch traced here: 2160 us
  waiting for transfers between devices  1750 us (81%)
  matrix products  186 us (9%)
  blocking collectives  101 us (5%)
  local copies, waits for them, and re-layouts  60.9 us (3%)
  other arithmetic  38 us (2%)
    psum x1, waiting for transfers between devices, per_device(): lax.psum((a_gain, a_bias, a_qkv, a_qkvb, a_proj, a_projb), 'rep')  587 us
    reduce_scatter x1, waiting for transfers between devices, per_device(): lax.psum_scatter(d_w_down, 'shard', scatter_dimension=0, tiled=True)  293 us
    reduce_scatter x1, waiting for transfers between devices, per_device(): lax.psum_scatter(d_w_up, 'shard', scatter_dimension=0, tiled=True)  293 us
    reduce_scatter x1, waiting for transfers between devices, per_device(): lax.psum_scatter(d_w_qkv, 'shard', scatter_dimension=0, tiled=True)  196 us
    all_gather x1, waiting for transfers between devices, per_device(): lax.all_gather(fc1_weight, 'shard', axis=0, tiled=True)  147 us
    all_gather x1, waiting for transfers between devices, per_device(): lax.all_gather(fc2_weight, 'shard', axis=0, tiled=True)  146 us
    all_gather x1, waiting for transfers between devices, per_device(): lax.all_gather(qkv_weight, 'shard', axis=0, tiled=True)  89.2 us
    psum x1, blocking collectives, per_device(): lax.psum((a_gain, a_bias, a_qkv, a_qkvb, a_proj, a_projb), 'rep')  63.9 us
  transfers between devices with their start and end apart: 10, of which 7 were waited for; matrix products, arithmetic and copies ran while one was open for 10% of the time, Pallas kernels for 0%

commit v1 on v0

v1 whole, which is shorter than its diff:
```python
from functools import partial

import jax
import jax.numpy as jnp
from jax import lax
from jax.sharding import PartitionSpec as P

HEADS = 16


norm_eps = 1e-06
quick_slope = 1.702


def apply_layer_norm(matrix):
    center = matrix - jnp.mean(matrix, axis=-1, keepdims=True)
    spread = jnp.mean(center * center, axis=-1, keepdims=True)
    inverse_spread = lax.rsqrt(spread + norm_eps)
    return (center * inverse_spread, inverse_spread)


def norm_gradient_step(normalized_gradient, centered_standard, inverse_spread, norm_gain):
    scaled_rows = normalized_gradient * norm_gain
    return inverse_spread * (
        scaled_rows
        - jnp.mean(scaled_rows, axis=-1, keepdims=True)
        - centered_standard * jnp.mean(scaled_rows * centered_standard, axis=-1, keepdims=True)
    )


def rotary_tables(positions, head_size):
    quarter = head_size // 4
    counter = jnp.arange(quarter, dtype=jnp.float32)
    inverse = jnp.power(jnp.float32(10000.0), -2.0 * counter / (head_size // 2))
    row_angle = positions[0].astype(jnp.float32)[:, None] * inverse[None, :]
    col_angle = positions[1].astype(jnp.float32)[:, None] * inverse[None, :]
    angle = jnp.concatenate([row_angle, col_angle], axis=1)
    angle = jnp.concatenate([angle, angle], axis=1)
    return (jnp.cos(angle), jnp.sin(angle))


def apply_rotary(matrix, cosine, sine):
    half_size = matrix.shape[-1] // 2
    turned = jnp.concatenate([-matrix[..., half_size:], matrix[..., :half_size]], axis=-1)
    return matrix * cosine[:, None, :] + turned * sine[:, None, :]


def rotary_back(grad_rows, cosine, sine):
    half_size = grad_rows.shape[-1] // 2
    sined = grad_rows * sine[:, None, :]
    turned = jnp.concatenate([sined[..., half_size:], -sined[..., :half_size]], axis=-1)
    return grad_rows * cosine[:, None, :] + turned


def masked_scores(queries, keys_rot, ident, score_scale):
    scores = (
        jnp.einsum("qhd,khd->hqk", queries, keys_rot, preferred_element_type=jnp.float32)
        * score_scale
    )
    same_pic = ident[:, None] == ident[None, :]
    return jnp.where(same_pic[None], scores, -1000000000.0)


def attend(pieces, score_scale):
    queries, keys_rot, values_all, ident = pieces
    scores = masked_scores(queries, keys_rot, ident, score_scale)
    top_score = jnp.max(scores, axis=2, keepdims=True)
    exp_scores = jnp.exp(scores - top_score)
    total = jnp.sum(exp_scores, axis=2, keepdims=True)
    probs = (exp_scores / total).astype(jnp.bfloat16)
    attended = jnp.einsum("hqk,khd->qhd", probs, values_all, preferred_element_type=jnp.float32)
    return (attended, (top_score + jnp.log(total))[:, :, 0])


def attend_back(pieces, score_scale):
    queries, keys_rot, values_all, ident, grad_heads, log_total = pieces
    scores = masked_scores(queries, keys_rot, ident, score_scale)
    probs = jnp.exp(scores - log_total[:, :, None])
    grad_probs = jnp.einsum(
        "qhd,khd->hqk", grad_heads, values_all, preferred_element_type=jnp.float32
    )
    inner = jnp.sum(probs * grad_probs, axis=2, keepdims=True)
    grad_scores = (probs * (grad_probs - inner)).astype(jnp.bfloat16)
    grad_query = (
        jnp.einsum("hqk,khd->qhd", grad_scores, keys_rot, preferred_element_type=jnp.float32)
        * score_scale
    )
    grad_key = (
        jnp.einsum("hqk,qhd->khd", grad_scores, queries, preferred_element_type=jnp.float32)
        * score_scale
    )
    grad_value = jnp.einsum(
        "hqk,qhd->khd", probs.astype(jnp.bfloat16), grad_heads, preferred_element_type=jnp.float32
    )
    return (grad_query, grad_key, grad_value)


def row_product(left, right):
    return jnp.einsum("ti,tj->ij", left, right, preferred_element_type=jnp.float32)


def back_product(grad_rows, weight_full):
    return jnp.einsum("tj,ij->ti", grad_rows, weight_full, preferred_element_type=jnp.float32)


def add_low(left, right):
    return (left.astype(jnp.float32) + right.astype(jnp.float32)).astype(jnp.bfloat16)


class Links:
    def __init__(self, n_rep, n_shard):
        self.nz, self.ny, self.n_rep = n_rep // 4, n_shard, n_rep
        rep = lax.axis_index("rep")
        self.y = lax.axis_index("shard")
        self.z, self.x, self.c = rep // 4, (rep // 2) % 2, rep % 2

    def swap_core(self, item):
        return lax.ppermute(item, "rep", [(i, i ^ 1) for i in range(self.n_rep)])

    def swap_x(self, item):
        return lax.ppermute(item, "rep", [(i, i ^ 2) for i in range(self.n_rep)])

    def swap_y(self, item):
        return lax.ppermute(item, "shard", [(0, 1), (1, 0)])

    def send_z(self, item, pairs):
        return lax.ppermute(
            item, "rep", [(a * 4 + k, b * 4 + k) for a, b in pairs for k in range(4)]
        )

    def inward(self, step):
        last = self.nz - 1
        return [(step, step + 1), (last - step, last - step - 1)]

    def outward(self, step):
        return [(b, a) for a, b in self.inward(step)]

    def middle(self):
        half = self.nz // 2
        return [(half - 1, half), (half, half - 1)]

    def in_order(self, index, mine, theirs, axis=0):
        first = jnp.concatenate([mine, theirs], axis=axis)
        second = jnp.concatenate([theirs, mine], axis=axis)
        return jnp.where(index == 0, first, second)

    def reduce_z(self, part):
        for step in range(self.nz // 2 - 1):
            part = add_low(part, self.send_z(part, self.inward(step)))
        part = add_low(part, self.send_z(part, self.middle()))
        for step in reversed(range(self.nz // 2 - 1)):
            moved = self.send_z(part, self.outward(step))
            outer = (self.z == step) | (self.z == self.nz - 1 - step)
            part = jnp.where(outer, moved, part)
        return part

    def gather_z(self, part):
        low = self.z < self.nz // 2
        own = part
        for step in range(self.nz // 2 - 1):
            moved = self.send_z(part, self.inward(step))
            part = jnp.where(
                low, jnp.concatenate([moved, own], 0), jnp.concatenate([own, moved], 0)
            )
        part = self.in_order(jnp.where(low, 0, 1), part, self.send_z(part, self.middle()))
        for step in reversed(range(self.nz // 2 - 1)):
            moved = self.send_z(part, self.outward(step))
            outer = (self.z == step) | (self.z == self.nz - 1 - step)
            part = jnp.where(outer, moved, part)
        return part

    def gather_plane(self, weight):
        rows = weight.shape[0] // self.n_rep
        place = ((self.c * 2 + self.x) * self.nz + self.z) * rows
        part = self.swap_y(lax.dynamic_slice_in_dim(weight, place, rows, 0))
        part = self.gather_z(part)
        part = self.in_order(self.x, part, self.swap_x(part))
        return self.in_order(self.c, part, self.swap_core(part))

    def gather_straight(self, weight):
        rows = weight.shape[0] // 2
        part = self.swap_y(lax.dynamic_slice_in_dim(weight, self.c * rows, rows, 0))
        return self.in_order(self.c, part, self.swap_core(part))

    def gather_weight(self, weight, cuts):
        if self.ny != 2:
            return lax.all_gather(weight, "shard", axis=0, tiled=True)
        pieces = []
        for start, stop, plane in cuts:
            block = weight[:, start:stop]
            pieces.append(self.gather_plane(block) if plane else self.gather_straight(block))
        other = jnp.concatenate(pieces, axis=1)
        return self.in_order(self.y, weight, other)

    def gather_vector(self, vector):
        if self.ny != 2:
            return lax.all_gather(vector, "shard", axis=0, tiled=False)
        return self.in_order(self.y, vector[None], self.swap_y(vector)[None])

    def sum_all(self, vector):
        vector = vector + self.swap_core(vector)
        vector = vector + self.swap_x(vector)
        step = 1
        while step < self.nz:
            vector = vector + self.send_z(vector, [(i, i ^ step) for i in range(self.nz)])
            step *= 2
        step = 1
        while step < self.ny:
            vector = vector + lax.ppermute(
                vector, "shard", [(i, i ^ step) for i in range(self.ny)]
            )
            step *= 2
        return vector

    def pick(self, stacked, index):
        return lax.dynamic_index_in_dim(stacked, index, 0, keepdims=False)

    def reduce_part(self, part):
        if self.ny == 2:
            got = self.swap_y(self.pick(part, 1 - self.y))
            part = add_low(self.pick(part, self.y), got)
        else:
            part = lax.psum_scatter(part, "shard", scatter_dimension=0, tiled=False)
        got = self.swap_x(self.pick(part, 1 - self.x))
        part = add_low(self.pick(part, self.x), got)
        part = self.reduce_z(part)
        part = self.in_order(self.x, part[None], self.swap_x(part)[None])
        return part

    def weight_gradient(self, left, right, chunks):
        half = right.shape[1] // 2
        kept = lax.dynamic_slice_in_dim(right, self.c * half, half, 1)
        sent = lax.dynamic_slice_in_dim(right, (1 - self.c) * half, half, 1)
        both_left = jnp.concatenate([left, self.swap_core(left)], axis=0)
        both_right = jnp.concatenate([kept, self.swap_core(sent)], axis=0)
        product = row_product(both_left, both_right).astype(jnp.bfloat16)
        rows = product.shape[0] // (self.ny * 2 * chunks)
        product = product.reshape(self.ny, 2, chunks, rows, half)
        parts = [self.reduce_part(product[:, :, i]) for i in range(chunks)]
        full = []
        for part in parts:
            full.append(self.in_order(self.c, part, self.swap_core(part), axis=2))
        total = jnp.stack(full, axis=1)
        return total.reshape(2 * chunks * rows, 2 * half).astype(jnp.float32)


def per_device(
    patches,
    lengths,
    positions,
    ln1_gain,
    ln1_bias,
    qkv_weight,
    qkv_bias,
    proj_weight,
    proj_bias,
    ln2_gain,
    ln2_bias,
    fc1_weight,
    fc1_bias,
    fc2_weight,
    fc2_bias,
    cotangent,
    n_rep,
    n_shard,
):
    links = Links(n_rep, n_shard)
    pack_count = lengths.shape[0]
    row_count = patches.shape[0]
    length = row_count // pack_count
    model_width = patches.shape[1]
    head_count = HEADS
    head_size = model_width // head_count
    score_scale = head_size ** (-0.5)
    pic_ends = jnp.cumsum(lengths[:, :-1], axis=1)
    slot_index = jnp.arange(length, dtype=jnp.int32)
    idents = jnp.sum((slot_index[None, :, None] >= pic_ends[:, None, :]).astype(jnp.int32), axis=2)
    cosine, sine = rotary_tables(positions, head_size)
    pack_shape = (pack_count, length, head_count, head_size)

    small = [ln1_gain, ln1_bias, qkv_bias, proj_bias, ln2_gain, ln2_bias, fc1_bias, fc2_bias]
    sizes = [item.shape[0] for item in small]
    gathered = links.gather_vector(jnp.concatenate(small))
    spots = [sum(sizes[:i]) for i in range(len(sizes) + 1)]
    (
        first_norm_gain, first_norm_bias, b_qkv, b_proj,
        second_norm_gain, second_norm_bias, b_up, b_down,
    ) = [
        gathered[:, spots[i] : spots[i + 1]].reshape(-1).astype(jnp.float32)
        for i in range(len(sizes))
    ]

    width = model_width
    w_qkv = links.gather_weight(
        qkv_weight,
        [(0, 1024, True), (1024, 2048, True), (2048, 2816, True), (2816, 3840, False)],
    )
    w_proj = links.gather_weight(proj_weight, [(0, 1024, True), (1024, width, False)])
    ff = fc1_weight.shape[1]
    w_up = links.gather_weight(
        fc1_weight, [(0, 1920, True), (1920, 3840, True), (3840, ff, False)]
    )
    w_down = links.gather_weight(
        fc2_weight, [(0, 512, True), (512, 1024, True), (1024, width, False)]
    )

    input_rows = patches.astype(jnp.float32)
    first_centered_standard, first_inverse_spread = apply_layer_norm(input_rows)
    first_normalized = (first_centered_standard * first_norm_gain + first_norm_bias).astype(
        jnp.bfloat16
    )
    qkv_rows = jnp.dot(first_normalized, w_qkv, preferred_element_type=jnp.float32) + b_qkv
    qkv_rows = qkv_rows.reshape(row_count, 3, head_count, head_size)
    queries = apply_rotary(qkv_rows[:, 0], cosine, sine).astype(jnp.bfloat16).reshape(pack_shape)
    keys_rot = apply_rotary(qkv_rows[:, 1], cosine, sine).astype(jnp.bfloat16).reshape(pack_shape)
    values_all = qkv_rows[:, 2].astype(jnp.bfloat16).reshape(pack_shape)
    attended, log_total = lax.map(
        partial(attend, score_scale=score_scale), (queries, keys_rot, values_all, idents)
    )
    heads_out = attended.reshape(row_count, model_width).astype(jnp.bfloat16)
    hidden_rows = (
        input_rows + jnp.dot(heads_out, w_proj, preferred_element_type=jnp.float32) + b_proj
    )
    second_centered_standard, second_inverse_spread = apply_layer_norm(hidden_rows)
    second_normalized = (second_centered_standard * second_norm_gain + second_norm_bias).astype(
        jnp.bfloat16
    )
    up_pre = jnp.dot(second_normalized, w_up, preferred_element_type=jnp.float32) + b_up
    sigmoid_up = 1.0 / (1.0 + jnp.exp(-quick_slope * up_pre))
    activation = (up_pre * sigmoid_up).astype(jnp.bfloat16)

    d_w_down = links.weight_gradient(activation, cotangent, 4)
    out_full = (
        hidden_rows + jnp.dot(activation, w_down, preferred_element_type=jnp.float32) + b_down
    )
    layer_out = out_full.astype(jnp.bfloat16)
    grad_out = cotangent.astype(jnp.float32)
    d_b_down = jnp.sum(grad_out, axis=0)
    grad_act = back_product(cotangent, w_down)
    slope_up = sigmoid_up + quick_slope * up_pre * sigmoid_up * (1.0 - sigmoid_up)
    grad_pre = (grad_act * slope_up).astype(jnp.bfloat16)
    d_w_up = links.weight_gradient(second_normalized, grad_pre, 4)
    d_b_up = jnp.sum(grad_pre.astype(jnp.float32), axis=0)
    second_normalized_gradient = back_product(grad_pre, w_up)
    second_gain_gradient = jnp.sum(second_normalized_gradient * second_centered_standard, axis=0)
    d_bias_two = jnp.sum(second_normalized_gradient, axis=0)
    grad_hidden = grad_out + norm_gradient_step(
        second_normalized_gradient,
        second_centered_standard,
        second_inverse_spread,
        second_norm_gain,
    )
    grad_branch = grad_hidden.astype(jnp.bfloat16)
    d_w_proj = links.weight_gradient(heads_out, grad_branch, 1)
    d_b_proj = jnp.sum(grad_branch.astype(jnp.float32), axis=0)
    grad_heads = back_product(grad_branch, w_proj).astype(jnp.bfloat16).reshape(pack_shape)
    grad_query, grad_key, grad_value = lax.map(
        partial(attend_back, score_scale=score_scale),
        (queries, keys_rot, values_all, idents, grad_heads, log_total),
    )
    rows_shape = (row_count, head_count, head_size)
    grad_query = rotary_back(grad_query.reshape(rows_shape), cosine, sine)
    grad_key = rotary_back(grad_key.reshape(rows_shape), cosine, sine)
    grad_qkv = (
        jnp.stack([grad_query, grad_key, grad_value.reshape(rows_shape)], axis=1)
        .reshape(row_count, 3 * model_width)
        .astype(jnp.bfloat16)
    )
    d_w_qkv = links.weight_gradient(first_normalized, grad_qkv, 4)
    d_b_qkv = jnp.sum(grad_qkv.astype(jnp.float32), axis=0)
    first_normalized_gradient = back_product(grad_qkv, w_qkv)
    first_gain_gradient = jnp.sum(first_normalized_gradient * first_centered_standard, axis=0)
    d_bias_one = jnp.sum(first_normalized_gradient, axis=0)
    d_patches = grad_hidden + norm_gradient_step(
        first_normalized_gradient,
        first_centered_standard,
        first_inverse_spread,
        first_norm_gain,
    )

    def own_parts(vectors):
        lens = [item.shape[0] for item in vectors]
        total = links.sum_all(jnp.concatenate(vectors))
        result, start = [], 0
        for size in lens:
            own = size // n_shard
            result.append(lax.dynamic_slice_in_dim(total, start + links.y * own, own, 0))
            start += size
        return result

    m_gain, m_bias, m_upb, m_downb = own_parts(
        [second_gain_gradient, d_bias_two, d_b_up, d_b_down]
    )
    a_gain, a_bias, a_qkvb, a_projb = own_parts(
        [first_gain_gradient, d_bias_one, d_b_qkv, d_b_proj]
    )
    return (
        layer_out,
        d_patches,
        a_gain,
        a_bias,
        d_w_qkv,
        a_qkvb,
        d_w_proj,
        a_projb,
        m_gain,
        m_bias,
        d_w_up,
        m_upb,
        d_w_down,
        m_downb,
    )


def solution(mesh):
    rows, whole = P(("rep", "shard"), None), P("shard")
    matrix = P("shard", None)
    in_specs = (
        rows,
        rows,
        P(None, ("rep", "shard")),
        whole,
        whole,
        matrix,
        whole,
        matrix,
        whole,
        whole,
        whole,
        matrix,
        whole,
        matrix,
        whole,
        rows,
    )
    out_specs = (
        rows,
        rows,
        whole,
        whole,
        matrix,
        whole,
        matrix,
        whole,
        whole,
        whole,
        matrix,
        whole,
        matrix,
        whole,
    )
    body = partial(per_device, n_rep=mesh.shape["rep"], n_shard=mesh.shape["shard"])
    return jax.shard_map(
        body, mesh=mesh, in_specs=in_specs, out_specs=out_specs, check_vma=False
    )
```

time: 2170 us -> 1220 us (0.56)
  waiting for transfers between devices: 1750 us -> 475 us
  starting transfers between devices: 0.4 us -> 204 us
  other arithmetic: 38 us -> 216 us
  blocking collectives: 101 us -> 0 us
  local copies, waits for them, and re-layouts: 60.9 us -> 99.4 us
  matrix products: 186 us -> 209 us
    reduce_scatter x4 -> x0, waiting for transfers between devices: 782 us -> none  [the longest x1 293 us: per_device(): lax.psum_scatter(d_w_down, 'shard', scatter_dimension=0, tiled=True)]
    psum x1 -> x0, waiting for transfers between devices: 587 us -> none  [per_device(): lax.psum((a_gain, a_bias, a_qkv, a_qkvb, a_proj, a_projb), 'rep')]
    ppermute x0 -> x166, waiting for transfers between devices: none -> 475 us  [the longest x67 254 us: send_z(): lax.ppermute(item, 'rep', [(a * 4 + k, b * 4 + k) for a, b in pairs for k...]
    all_gather x4 -> x0, waiting for transfers between devices: 382 us -> none  [the longest x1 147 us: per_device(): lax.all_gather(fc1_weight, 'shard', axis=0, tiled=True)]
    ppermute x0 -> x166, starting transfers between devices: none -> 204 us  [the longest x67 124 us: send_z(): lax.ppermute(item, 'rep', [(a * 4 + k, b * 4 + k) for a, b in pairs for k...]
    select_n x0 -> x85, other arithmetic: none -> 153 us  [the longest x56 147 us: in_order(): return jnp.where(index == 0, first, second)]
    psum x1 -> x0, blocking collectives: 63.9 us -> none  [per_device(): lax.psum((a_gain, a_bias, a_qkv, a_qkvb, a_proj, a_projb), 'rep')]
    all_gather x8 -> x0, blocking collectives: 36.8 us -> none  [the longest x1 5.32 us: per_device(): lax.all_gather(ln2_gain, 'shard', axis=0, tiled=True)]
  transfers between devices with their start and end apart: 10 -> 166, of which waited for: 7 -> 72; matrix products, arithmetic and copies ran while one was open for 10% -> 41% of each run, Pallas kernels for 0% -> 0%
where the time goes in v1:
time: 1220 us; the launch traced here: 1210 us
  waiting for transfers between devices  475 us (39%)
  other arithmetic  216 us (18%)
  matrix products  209 us (17%)
  starting transfers between devices  204 us (17%)
  local copies, waits for them, and re-layouts  99.4 us (8%)
    ppermute x67, waiting for transfers between devices, send_z(): lax.ppermute(item, 'rep', [(a * 4 + k, b * 4 + k) for a, b in pairs for k...  254 us
    select_n x56, other arithmetic, in_order(): return jnp.where(index == 0, first, second)  147 us
    ppermute x67, starting transfers between devices, send_z(): lax.ppermute(item, 'rep', [(a * 4 + k, b * 4 + k) for a, b in pairs for k...  124 us
    ppermute x36, waiting for transfers between devices, swap_x(): return lax.ppermute(item, 'rep', [(i, i ^ 2) for i in range(self.n_rep)])  123 us
    ppermute x26, waiting for transfers between devices, swap_y(): return lax.ppermute(item, 'shard', [(0, 1), (1, 0)])  92.8 us
    dot_general x4, matrix products, back_product(): jnp.einsum('tj,ij->ti', grad_rows, weight_full, preferred_element_type=jn...  73.3 us
    ppermute x36, starting transfers between devices, swap_x(): return lax.ppermute(item, 'rep', [(i, i ^ 2) for i in range(self.n_rep)])  49.8 us
    dot_general x1, matrix products, per_device(): jnp.dot(activation, w_down, preferred_element_type=jnp.float32)  32.9 us
  transfers between devices with their start and end apart: 166, of which 72 were waited for; matrix products, arithmetic and copies ran while one was open for 41% of the time, Pallas kernels for 0%

profile of v1, /device:TPU:0, one launch (start us, length us, event | category | flops | bytes accessed | tf_op | source)
XLA Modules:
  0.0 1207.0 jit_solution(17493211046808253014)
XLA Ops:
  88.4 12.2 %collective-permute-start.50 = (bf16[160,512]{1,0:T(8,128)(2,1)S(1)}, bf16[160,512]{1,0:T(8,128)(2,1)S(1)}, u32[]{:S(2)}, u32[]{:S(2)}) collective-permute-start(bf16[160,512]{1,0:T(8,128)(2,1)S(1)} %collective-permute-done.49), channel_id=1, source_target_pairs={{0,8},{2,10},{4,12},{6,14},{24,16},{26,18},{28,20},{30,22},{1,9},{... | collective-permute-start | bytes 491528 | tf_op jit(solution)/shard_map/ppermute | solution.py:127
  166.3 13.1 %collective-permute-done.32 = bf16[160,1920]{1,0:T(8,128)(2,1)S(1)} collective-permute-done((bf16[160,1920]{1,0:T(8,128)(2,1)S(1)}, bf16[160,1920]{1,0:T(8,128)(2,1)S(1)}, u32[]{:S(2)}, u32[]{:S(2)}) %collective-permute-start.32) | collective-permute-done | bytes 614432 | tf_op jit(solution)/shard_map/ppermute | solution.py:127
  181.8 11.7 collective-permute-done.52
  193.5 11.0 collective-permute-done.46
  213.0 87.4 %maximum_select_fusion.2 = bf16[1280,3840]{1,0:T(8,128)(2,1)S(1)} fusion(bf16[640,1024]{1,0:T(8,128)(2,1)S(1)} %maximum_select_fusion.20, bf16[640,768]{1,0:T(8,128)(2,1)S(1)} %maximum_select_fusion.31, bf16[640,1024]{1,0:T(8,128)(2,1)S(1)} %maximum_select_fusion.19, bf16[640,1024]{1,0:T(8,128)(2,1)S(1)} %maximum_select_fusion.18, ...), kind=kLoop, calls=%fused_computation.20 | loop fusion | flops 103219200 | bytes 19660800 | tf_op jit(solution)/shard_map/jit(_where)/select_n | solution.py:145
  312.8 9.3 copy.71
  345.0 10.7 fusion.65
  382.5 21.3 %maximum_select_fusion = bf16[1280,5120]{1,0:T(8,128)(2,1)} fusion(bf16[640,1280]{1,0:T(8,128)(2,1)} %maximum_select_fusion.8, bf16[640,1920]{1,0:T(8,128)(2,1)} %maximum_select_fusion.7, bf16[640,1920]{1,0:T(8,128)(2,1)} %maximum_select_fusion.6, bf16[640,5120]{1,0:T(8,128)(2,1)} %param.27, pred[]{:T(512)S(6)} %eq.39), kind=kLoop, calls=%fused_computation.7 | loop fusion | flops 111411200 | bytes 26214400 | tf_op jit(solution)/shard_map/jit(_where)/select_n | solution.py:145
  403.8 16.8 %multiply_convert_fusion.1 = (bf16[512,5120]{1,0:T(8,128)(2,1)}, f32[512,5120]{1,0:T(8,128)}) fusion(f32[5120]{0:T(1024)S(1)} %copy-done.39, bf16[512,1280]{1,0:T(8,128)(2,1)} %add_convert_fusion, bf16[1280,5120]{1,0:T(8,128)(2,1)} %maximum_select_fusion), kind=kOutput, calls=%fused_computation.18 | convolution fusion | flops 6726615040 | bytes 30167040 | tf_op jit(solution)/shard_map/dot_general | solution.py:328
  428.5 33.0 %convert_reduce_fusion = (f32[5120]{0:T(1024)S(1)}, bf16[512,5120]{1,0:T(8,128)(2,1)}) fusion(f32[512,5120]{1,0:T(8,128)} %get-tuple-element.147, f32[5120]{0:T(1024)S(1)} %copy-done.39, bf16[512,1280]{1,0:T(8,128)(2,1)} %param.31, bf16[2560,256]{1,0:T(8,128)(2,1)} %maximum_select_fusion.24, bf16[2560,512]{1,0:T(8,128)(2,1)} %maximum_select_fusion.5, ...), kind=kOutput, calls=%fused_computation.17 | convolution fusion | flops 6856371200 | bytes 30187520 | tf_op jit(solution)/shard_map/tj,ij->ti/dot_general | solution.py:103
  461.5 14.4 %multiply_reduce_fusion.1 = (f32[1280]{0:T(1024)S(1)}, f32[512]{0:T(512)S(1)}, f32[512]{0:T(512)S(1)}, f32[1280]{0:T(1024)S(1)}, f32[512,1280]{1,0:T(8,128)}) fusion(f32[512,1280]{1,0:T(8,128)S(1)} %get-tuple-element.145, f32[512]{0:T(512)S(1)} %add_rsqrt_fusion, f32[512]{0:T(512)S(1)} %broadcast_multiply_fusion.8, f32[1280]{0:T(1024)S(1)} %reshape.1879, ...), kind=kOutput, calls=%fused_computation.92 | convolution fusion | flops 6716781568 | bytes 23616512 | tf_op jit(solution)/shard_map/tj,ij->ti/dot_general | solution.py:103
  481.1 13.5 %convolution_convert_fusion.3 = bf16[512,1280]{1,0:T(8,128)(2,1)} fusion(bf16[512,1280]{1,0:T(8,128)(2,1)S(1)} %get-tuple-element.76, bf16[640,256]{1,0:T(8,128)(2,1)S(1)} %copy-done.33, bf16[640,1024]{1,0:T(8,128)(2,1)S(1)} %copy-done.22, bf16[640,1280]{1,0:T(8,128)(2,1)S(1)} %copy-done.19, pred[]{:T(512)S(6)} %eq.39), kind=kOutput, calls=%fused_computation.54 | convolution fusion | flops 1699676160 | bytes 5898241 | tf_op jit(solution)/shard_map/tj,ij->ti/dot_general | solution.py:103
  506.1 12.0 multiply_reduce_fusion
  519.0 12.0 multiply_convert_fusion
  539.3 12.5 %fusion.35 = (f32[1280]{0:T(1024)S(1)}, f32[512]{0:T(512)S(1)}, f32[512]{0:T(512)S(1)}, f32[1280]{0:T(1024)S(1)}, f32[512,1280]{1,0:T(8,128)}) fusion(bf16[512,1280]{1,0:T(8,128)(2,1)S(1)} %copy-done.2, f32[512]{0:T(512)S(1)} %copy-done.41, f32[512]{0:T(512)S(1)} %copy-done.37, f32[1280]{0:T(1024)S(1)} %copy-done.35, bf16[512,3840]{0,1:T(8,128)(2,1)S(1)} %bitcast.325, ...), kind=kOutput, calls=%fused_computation.62 | convolution fusion | flops 5039715328 | bytes 17718272 | tf_op jit(solution)/shard_map/tj,ij->ti/dot_general | solution.py:103
  552.6 32.9 %fusion.28 = bf16[512,1280]{1,0:T(8,128)(2,1)} fusion(f32[512,1280]{1,0:T(8,128)S(1)} %get-tuple-element.145, bf16[512,5120]{1,0:T(8,128)(2,1)} %get-tuple-element.146, f32[1280]{0:T(1024)S(1)} %copy-done.44, bf16[2560,256]{1,0:T(8,128)(2,1)} %maximum_select_fusion.24, bf16[2560,512]{1,0:T(8,128)(2,1)} %maximum_select_fusion.5, ...), kind=kOutput, calls=%fused_computation.55 | convolution fusion | flops 6824263680 | bytes 22287360 | tf_op jit(solution)/shard_map/dot_general | solution.py:334
  605.6 11.4 collective-permute-done.94
  638.7 14.9 %collective-permute-done.85 = bf16[2,80,1920]{2,1,0:T(8,128)(2,1)S(1)} collective-permute-done((bf16[2,80,1920]{2,1,0:T(8,128)(2,1)S(1)}, bf16[2,80,1920]{2,1,0:T(8,128)(2,1)S(1)}, u32[]{:S(2)}, u32[]{:S(2)}) %collective-permute-start.85) | collective-permute-done | bytes 614432 | tf_op jit(solution)/shard_map/ppermute | solution.py:124
  654.2 14.5 %collective-permute-done.78 = bf16[2,80,1920]{2,1,0:T(8,128)(2,1)S(1)} collective-permute-done((bf16[2,80,1920]{2,1,0:T(8,128)(2,1)S(1)}, bf16[2,80,1920]{2,1,0:T(8,128)(2,1)S(1)}, u32[]{:S(2)}, u32[]{:S(2)}) %collective-permute-start.78) | collective-permute-done | bytes 614432 | tf_op jit(solution)/shard_map/ppermute | solution.py:124
  669.3 13.6 %collective-permute-done.71 = bf16[2,80,1920]{2,1,0:T(8,128)(2,1)S(1)} collective-permute-done((bf16[2,80,1920]{2,1,0:T(8,128)(2,1)S(1)}, bf16[2,80,1920]{2,1,0:T(8,128)(2,1)S(1)}, u32[]{:S(2)}, u32[]{:S(2)}) %collective-permute-start.71) | collective-permute-done | bytes 614432 | tf_op jit(solution)/shard_map/ppermute | solution.py:124
  683.6 12.8 %collective-permute-done.64 = bf16[2,80,1920]{2,1,0:T(8,128)(2,1)S(1)} collective-permute-done((bf16[2,80,1920]{2,1,0:T(8,128)(2,1)S(1)}, bf16[2,80,1920]{2,1,0:T(8,128)(2,1)S(1)}, u32[]{:S(2)}, u32[]{:S(2)}) %collective-permute-start.64) | collective-permute-done | bytes 614432 | tf_op jit(solution)/shard_map/ppermute | solution.py:124
  765.3 16.8 %collective-permute-done.115 = bf16[2,80,2560]{2,1,0:T(8,128)(2,1)S(1)} collective-permute-done((bf16[2,80,2560]{2,1,0:T(8,128)(2,1)S(1)}, bf16[2,80,2560]{2,1,0:T(8,128)(2,1)S(1)}, u32[]{:S(2)}, u32[]{:S(2)}) %collective-permute-start.115) | collective-permute-done | bytes 819232 | tf_op jit(solution)/shard_map/ppermute | solution.py:124
  798.3 25.1 %collective-permute-done.89 = bf16[80,1920]{1,0:T(8,128)(2,1)S(1)} collective-permute-done((bf16[80,1920]{1,0:T(8,128)(2,1)S(1)}, bf16[80,1920]{1,0:T(8,128)(2,1)S(1)}, u32[]{:S(2)}, u32[]{:S(2)}) %collective-permute-start.89) | collective-permute-done | bytes 307232 | tf_op jit(solution)/shard_map/ppermute | solution.py:127
  824.7 9.8 collective-permute-done.82
  937.3 11.2 fusion.11
  949.9 28.0 %collective-permute-done.133 = bf16[80,2560]{1,0:T(8,128)(2,1)S(1)} collective-permute-done((bf16[80,2560]{1,0:T(8,128)(2,1)S(1)}, bf16[80,2560]{1,0:T(8,128)(2,1)S(1)}, u32[]{:S(2)}, u32[]{:S(2)}) %collective-permute-start.133) | collective-permute-done | bytes 409632 | tf_op jit(solution)/shard_map/ppermute | solution.py:127
  1005.4 9.0 collective-permute-done.134
  1046.5 9.7 collective-permute-done.160
  1082.0 11.3 collective-permute-start.161
  1133.3 9.7 collective-permute-done.163
  1173.3 11.3 copy.84
  1196.2 10.7 copy.89
  (719 shorter events, 659.8 us)
Async XLA Ops:
  23.9 43.4 %collective-permute-start.1 = (bf16[40,1024]{1,0:T(8,128)(2,1)}, bf16[40,1024]{1,0:T(8,128)(2,1)S(1)}, u32[]{:S(2)}, u32[]{:S(2)}) collective-permute-start(bf16[40,1024]{1,0:T(8,128)(2,1)} %constant_dynamic-slice_fusion.19), channel_id=1, source_target_pairs={{0,1},{1,0},{2,3},{3,2},{4,5},{5,4},{6,7},{7,6},{8,9},{9,8},{10,11... | collective-permute-start | bytes 245768 | tf_op jit(solution)/shard_map/ppermute | solution.py:124
  23.9 63.8 %collective-permute-start.27 = (bf16[320,256]{1,0:T(8,128)(2,1)S(1)}, bf16[320,256]{1,0:T(8,128)(2,1)S(1)}, u32[]{:S(2)}, u32[]{:S(2)}) collective-permute-start(bf16[320,256]{1,0:T(8,128)(2,1)S(1)} %constant_dynamic-slice_fusion.14), channel_id=1, source_target_pairs={{0,1},{1,0},{2,3},{3,2},{4,5},{5,4},{6,7},{7,6},{8,9},{9,8},{10,11... | collective-permute-start | bytes 491528 | tf_op jit(solution)/shard_map/ppermute | solution.py:124
  87.8 76.8 %collective-permute-start.19 = (bf16[320,1024]{1,0:T(8,128)(2,1)}, bf16[320,1024]{1,0:T(8,128)(2,1)S(1)}, u32[]{:S(2)}, u32[]{:S(2)}) collective-permute-start(bf16[320,1024]{1,0:T(8,128)(2,1)} %constant_dynamic-slice_fusion.16), channel_id=1, source_target_pairs={{0,1},{1,0},{2,3},{3,2},{4,5},{5,4},{6,7},{7,6},{8,9},{9,8},{10,11... | collective-permute-start | bytes 1966088 | tf_op jit(solution)/shard_map/ppermute | solution.py:124
  181.3 187.4 %collective-permute-start.42 = (bf16[320,1280]{1,0:T(8,128)(2,1)}, bf16[320,1280]{1,0:T(8,128)(2,1)}, u32[]{:S(2)}, u32[]{:S(2)}) collective-permute-start(bf16[320,1280]{1,0:T(8,128)(2,1)} %collective-permute-done.41), channel_id=1, source_target_pairs={{0,2},{2,0},{4,6},{6,4},{8,10},{10,8},{12,14},{14,12},{16,18},{18,... | collective-permute-start | bytes 2457608 | tf_op jit(solution)/shard_map/ppermute | solution.py:118
  205.5 150.2 %collective-permute-start.26 = (bf16[320,1024]{1,0:T(8,128)(2,1)S(1)}, bf16[320,1024]{1,0:T(8,128)(2,1)}, u32[]{:S(2)}, u32[]{:S(2)}) collective-permute-start(bf16[320,1024]{1,0:T(8,128)(2,1)S(1)} %maximum_select_fusion.43), channel_id=1, source_target_pairs={{0,2},{2,0},{4,6},{6,4},{8,10},{10,8},{12,14},{14,12},{16,18},{18,... | collective-permute-start | bytes 1966088 | tf_op jit(solution)/shard_map/ppermute | solution.py:118
  206.6 157.5 %collective-permute-start.39 = (bf16[160,1920]{1,0:T(8,128)(2,1)}, bf16[160,1920]{1,0:T(8,128)(2,1)}, u32[]{:S(2)}, u32[]{:S(2)}) collective-permute-start(bf16[160,1920]{1,0:T(8,128)(2,1)} %broadcast_select_fusion.2), channel_id=1, source_target_pairs={{0,4},{2,6},{4,0},{6,2},{8,12},{10,14},{12,8},{14,10},{16,20},{18,... | collective-permute-start | bytes 1843208 | tf_op jit(solution)/shard_map/ppermute | solution.py:121
  209.6 156.5 %collective-permute-start.33 = (bf16[160,1920]{1,0:T(8,128)(2,1)}, bf16[160,1920]{1,0:T(8,128)(2,1)}, u32[]{:S(2)}, u32[]{:S(2)}) collective-permute-start(bf16[160,1920]{1,0:T(8,128)(2,1)} %broadcast_select_fusion.3), channel_id=1, source_target_pairs={{0,4},{2,6},{4,0},{6,2},{8,12},{10,14},{12,8},{14,10},{16,20},{18,... | collective-permute-start | bytes 1843208 | tf_op jit(solution)/shard_map/ppermute | solution.py:121
  210.8 161.4 %collective-permute-start.53 = (bf16[640,512]{1,0:T(8,128)(2,1)S(1)}, bf16[640,512]{1,0:T(8,128)(2,1)}, u32[]{:S(2)}, u32[]{:S(2)}) collective-permute-start(bf16[640,512]{1,0:T(8,128)(2,1)S(1)} %broadcast_select_fusion), channel_id=1, source_target_pairs={{0,4},{2,6},{4,0},{6,2},{8,12},{10,14},{12,8},{14,10},{16,20},{18,... | collective-permute-start | bytes 1966088 | tf_op jit(solution)/shard_map/ppermute | solution.py:121
  368.7 256.9 %collective-permute-start.62 = (bf16[512,1280]{1,0:T(8,128)(2,1)}, bf16[512,1280]{1,0:T(8,128)(2,1)}, u32[]{:S(2)}, u32[]{:S(2)}) collective-permute-start(bf16[512,1280]{1,0:T(8,128)(2,1)} %fusion.30), channel_id=1, source_target_pairs={{0,2},{2,0},{4,6},{6,4},{8,10},{10,8},{12,14},{14,12},{16,18},{18,... | collective-permute-start | bytes 3932168 | tf_op jit(solution)/shard_map/ppermute | solution.py:118
  372.2 221.5 %collective-permute-start.92 = (bf16[512,1280]{0,1:T(8,128)(2,1)}, bf16[512,1280]{0,1:T(8,128)(2,1)}, u32[]{:S(2)}, u32[]{:S(2)}) collective-permute-start(bf16[512,1280]{0,1:T(8,128)(2,1)} %bitcast.8), channel_id=1, source_target_pairs={{0,2},{2,0},{4,6},{6,4},{8,10},{10,8},{12,14},{14,12},{16,18},{18,... | collective-permute-start | bytes 3932168 | tf_op jit(solution)/shard_map/ppermute | solution.py:118
  375.5 45.1 %collective-permute-start.54 = (bf16[1280,512]{1,0:T(8,128)(2,1)}, bf16[1280,512]{1,0:T(8,128)(2,1)}, u32[]{:S(2)}, u32[]{:S(2)}) collective-permute-start(bf16[1280,512]{1,0:T(8,128)(2,1)} %maximum_select_fusion.23), channel_id=1, source_target_pairs={{0,2},{2,0},{4,6},{6,4},{8,10},{10,8},{12,14},{14,12},{16,18},{18,... | collective-permute-start | bytes 3932168 | tf_op jit(solution)/shard_map/ppermute | solution.py:118
  377.1 47.5 %collective-permute-start.48 = (bf16[1280,512]{1,0:T(8,128)(2,1)}, bf16[1280,512]{1,0:T(8,128)(2,1)}, u32[]{:S(2)}, u32[]{:S(2)}) collective-permute-start(bf16[1280,512]{1,0:T(8,128)(2,1)} %maximum_select_fusion.22), channel_id=1, source_target_pairs={{0,2},{2,0},{4,6},{6,4},{8,10},{10,8},{12,14},{14,12},{16,18},{18,... | collective-permute-start | bytes 3932168 | tf_op jit(solution)/shard_map/ppermute | solution.py:118
  552.1 42.3 %collective-permute-start.93 = (bf16[512,640]{1,0:T(8,128)(2,1)}, bf16[512,640]{1,0:T(8,128)(2,1)S(1)}, u32[]{:S(2)}, u32[]{:S(2)}) collective-permute-start(bf16[512,640]{1,0:T(8,128)(2,1)} %get-tuple-element.117), channel_id=1, source_target_pairs={{0,2},{2,0},{4,6},{6,4},{8,10},{10,8},{12,14},{14,12},{16,18},{18,... | collective-permute-start | bytes 1966088 | tf_op jit(solution)/shard_map/ppermute | solution.py:118
  619.4 316.2 %collective-permute-start.137 = (bf16[512,640]{1,0:T(8,128)(2,1)S(1)}, bf16[512,640]{1,0:T(8,128)(2,1)S(1)}, u32[]{:S(2)}, u32[]{:S(2)}) collective-permute-start(bf16[512,640]{1,0:T(8,128)(2,1)S(1)} %copy-done.28), channel_id=1, source_target_pairs={{0,2},{2,0},{4,6},{6,4},{8,10},{10,8},{12,14},{14,12},{16,18},{18,... | collective-permute-start | bytes 1966088 | tf_op jit(solution)/shard_map/ppermute | solution.py:118
  623.6 73.7 %collective-permute-start.106 = (bf16[512,1280]{1,0:T(8,128)(2,1)S(1)}, bf16[512,1280]{1,0:T(8,128)(2,1)S(1)}, u32[]{:S(2)}, u32[]{:S(2)}) collective-permute-start(bf16[512,1280]{1,0:T(8,128)(2,1)S(1)} %copy-done.20), channel_id=1, source_target_pairs={{0,2},{2,0},{4,6},{6,4},{8,10},{10,8},{12,14},{14,12},{16,18},{18,... | collective-permute-start | bytes 3932168 | tf_op jit(solution)/shard_map/ppermute | solution.py:118
  625.5 311.8 %collective-permute-start.136 = (bf16[512,5120]{1,0:T(8,128)(2,1)}, bf16[512,5120]{1,0:T(8,128)(2,1)}, u32[]{:S(2)}, u32[]{:S(2)}) collective-permute-start(bf16[512,5120]{1,0:T(8,128)(2,1)} %get-tuple-element.146), channel_id=1, source_target_pairs={{0,2},{2,0},{4,6},{6,4},{8,10},{10,8},{12,14},{14,12},{16,18},{18,... | collective-permute-start | bytes 15728648 | tf_op jit(solution)/shard_map/ppermute | solution.py:118
  638.6 59.9 %collective-permute-start.107 = (bf16[512,2560]{1,0:T(8,128)(2,1)S(1)}, bf16[512,2560]{1,0:T(8,128)(2,1)S(1)}, u32[]{:S(2)}, u32[]{:S(2)}) collective-permute-start(bf16[512,2560]{1,0:T(8,128)(2,1)S(1)} %get-tuple-element.95), channel_id=1, source_target_pairs={{0,2},{2,0},{4,6},{6,4},{8,10},{10,8},{12,14},{14,12},{16,18},{18,... | collective-permute-start | bytes 7864328 | tf_op jit(solution)/shard_map/ppermute | solution.py:118
  713.3 48.3 %collective-permute-start.129 = (bf16[2,80,2560]{2,1,0:T(8,128)(2,1)S(1)}, bf16[2,80,2560]{2,1,0:T(8,128)(2,1)S(1)}, u32[]{:S(2)}, u32[]{:S(2)}) collective-permute-start(bf16[2,80,2560]{2,1,0:T(8,128)(2,1)S(1)} %dynamic-slice_bitcast_fusion.4), channel_id=1, source_target_pairs={{0,1},{1,0},{2,3},{3,2},{4,5},{5,4},{6,7},{7,6},{8,9},{9,8},{10,11... | collective-permute-start | bytes 2457608 | tf_op jit(solution)/shard_map/ppermute | solution.py:124
  794.5 60.8 %collective-permute-start.130 = (bf16[80,2560]{1,0:T(8,128)(2,1)S(1)}, bf16[80,2560]{1,0:T(8,128)(2,1)S(1)}, u32[]{:S(2)}, u32[]{:S(2)}) collective-permute-start(bf16[80,2560]{1,0:T(8,128)(2,1)S(1)} %dynamic-slice_bitcast_fusion.17), channel_id=1, source_target_pairs={{0,4},{2,6},{4,0},{6,2},{8,12},{10,14},{12,8},{14,10},{16,20},{18,... | collective-permute-start | bytes 1228808 | tf_op jit(solution)/shard_map/ppermute | solution.py:121
  797.7 58.1 %collective-permute-start.123 = (bf16[80,2560]{1,0:T(8,128)(2,1)S(1)}, bf16[80,2560]{1,0:T(8,128)(2,1)S(1)}, u32[]{:S(2)}, u32[]{:S(2)}) collective-permute-start(bf16[80,2560]{1,0:T(8,128)(2,1)S(1)} %dynamic-slice_bitcast_fusion.18), channel_id=1, source_target_pairs={{0,4},{2,6},{4,0},{6,2},{8,12},{10,14},{12,8},{14,10},{16,20},{18,... | collective-permute-start | bytes 1228808 | tf_op jit(solution)/shard_map/ppermute | solution.py:121
  855.9 63.8 %collective-permute-start.100 = (bf16[2,320,640]{2,1,0:T(8,128)(2,1)S(1)}, bf16[2,320,640]{2,1,0:T(8,128)(2,1)S(1)}, u32[]{:S(2)}, u32[]{:S(2)}) collective-permute-start(bf16[2,320,640]{2,1,0:T(8,128)(2,1)S(1)} %maximum_select_fusion.32), channel_id=1, source_target_pairs={{0,2},{2,0},{4,6},{6,4},{8,10},{10,8},{12,14},{14,12},{16,18},{18,... | collective-permute-start | bytes 2457608 | tf_op jit(solution)/shard_map/ppermute | solution.py:118
  925.2 52.7 %collective-permute-start.133 = (bf16[80,2560]{1,0:T(8,128)(2,1)S(1)}, bf16[80,2560]{1,0:T(8,128)(2,1)S(1)}, u32[]{:S(2)}, u32[]{:S(2)}) collective-permute-start(bf16[80,2560]{1,0:T(8,128)(2,1)S(1)} %add_convert_fusion.9), channel_id=1, source_target_pairs={{8,0},{10,2},{12,4},{14,6},{16,24},{18,26},{20,28},{22,30},{9,1},{... | collective-permute-start | bytes 1228808 | tf_op jit(solution)/shard_map/ppermute | solution.py:127
  926.8 59.8 %collective-permute-start.126 = (bf16[80,2560]{1,0:T(8,128)(2,1)S(1)}, bf16[80,2560]{1,0:T(8,128)(2,1)S(1)}, u32[]{:S(2)}, u32[]{:S(2)}) collective-permute-start(bf16[80,2560]{1,0:T(8,128)(2,1)S(1)} %add_convert_fusion.11), channel_id=1, source_target_pairs={{8,0},{10,2},{12,4},{14,6},{16,24},{18,26},{20,28},{22,30},{9,1},{... | collective-permute-start | bytes 1228808 | tf_op jit(solution)/shard_map/ppermute | solution.py:127
  928.4 67.0 %collective-permute-start.119 = (bf16[80,2560]{1,0:T(8,128)(2,1)S(1)}, bf16[80,2560]{1,0:T(8,128)(2,1)S(1)}, u32[]{:S(2)}, u32[]{:S(2)}) collective-permute-start(bf16[80,2560]{1,0:T(8,128)(2,1)S(1)} %add_convert_fusion.13), channel_id=1, source_target_pairs={{8,0},{10,2},{12,4},{14,6},{16,24},{18,26},{20,28},{22,30},{9,1},{... | collective-permute-start | bytes 1228808 | tf_op jit(solution)/shard_map/ppermute | solution.py:127
  935.6 68.0 %collective-permute-start.112 = (bf16[80,2560]{1,0:T(8,128)(2,1)S(1)}, bf16[80,2560]{1,0:T(8,128)(2,1)S(1)}, u32[]{:S(2)}, u32[]{:S(2)}) collective-permute-start(bf16[80,2560]{1,0:T(8,128)(2,1)S(1)} %add_convert_fusion.15), channel_id=1, source_target_pairs={{8,0},{10,2},{12,4},{14,6},{16,24},{18,26},{20,28},{22,30},{9,1},{... | collective-permute-start | bytes 1228808 | tf_op jit(solution)/shard_map/ppermute | solution.py:127
  949.2 93.4 %collective-permute-start.159 = (bf16[2,320,640]{2,1,0:T(8,128)(2,1)S(1)}, bf16[2,320,640]{2,1,0:T(8,128)(2,1)S(1)}, u32[]{:S(2)}, u32[]{:S(2)}) collective-permute-start(bf16[2,320,640]{2,1,0:T(8,128)(2,1)S(1)} %dynamic-slice_bitcast_fusion), channel_id=1, source_target_pairs={{0,1},{1,0},{2,3},{3,2},{4,5},{5,4},{6,7},{7,6},{8,9},{9,8},{10,11... | collective-permute-start | bytes 2457608 | tf_op jit(solution)/shard_map/ppermute | solution.py:124
  977.9 65.5 %collective-permute-start.152 = (bf16[2,320,640]{2,1,0:T(8,128)(2,1)S(1)}, bf16[2,320,640]{2,1,0:T(8,128)(2,1)S(1)}, u32[]{:S(2)}, u32[]{:S(2)}) collective-permute-start(bf16[2,320,640]{2,1,0:T(8,128)(2,1)S(1)} %dynamic-slice_bitcast_fusion.1), channel_id=1, source_target_pairs={{0,1},{1,0},{2,3},{3,2},{4,5},{5,4},{6,7},{7,6},{8,9},{9,8},{10,11... | collective-permute-start | bytes 2457608 | tf_op jit(solution)/shard_map/ppermute | solution.py:124
  986.7 57.1 %collective-permute-start.145 = (bf16[2,320,640]{2,1,0:T(8,128)(2,1)S(1)}, bf16[2,320,640]{2,1,0:T(8,128)(2,1)S(1)}, u32[]{:S(2)}, u32[]{:S(2)}) collective-permute-start(bf16[2,320,640]{2,1,0:T(8,128)(2,1)S(1)} %dynamic-slice_bitcast_fusion.2), channel_id=1, source_target_pairs={{0,1},{1,0},{2,3},{3,2},{4,5},{5,4},{6,7},{7,6},{8,9},{9,8},{10,11... | collective-permute-start | bytes 2457608 | tf_op jit(solution)/shard_map/ppermute | solution.py:124
  995.5 50.4 %collective-permute-start.138 = (bf16[2,320,640]{2,1,0:T(8,128)(2,1)S(1)}, bf16[2,320,640]{2,1,0:T(8,128)(2,1)S(1)}, u32[]{:S(2)}, u32[]{:S(2)}) collective-permute-start(bf16[2,320,640]{2,1,0:T(8,128)(2,1)S(1)} %dynamic-slice_bitcast_fusion.3), channel_id=1, source_target_pairs={{0,1},{1,0},{2,3},{3,2},{4,5},{5,4},{6,7},{7,6},{8,9},{9,8},{10,11... | collective-permute-start | bytes 2457608 | tf_op jit(solution)/shard_map/ppermute | solution.py:124
  1042.5 50.9 %collective-permute-start.135 = (bf16[2,80,2560]{2,1,0:T(8,128)(2,1)S(1)}, bf16[2,80,2560]{2,1,0:T(8,128)(2,1)S(1)}, u32[]{:S(2)}, u32[]{:S(2)}) collective-permute-start(bf16[2,80,2560]{2,1,0:T(8,128)(2,1)S(1)} %maximum_select_fusion.36), channel_id=1, source_target_pairs={{0,2},{2,0},{4,6},{6,4},{8,10},{10,8},{12,14},{14,12},{16,18},{18,... | collective-permute-start | bytes 2457608 | tf_op jit(solution)/shard_map/ppermute | solution.py:118
  1042.6 52.5 %collective-permute-start.128 = (bf16[2,80,2560]{2,1,0:T(8,128)(2,1)S(1)}, bf16[2,80,2560]{2,1,0:T(8,128)(2,1)S(1)}, u32[]{:S(2)}, u32[]{:S(2)}) collective-permute-start(bf16[2,80,2560]{2,1,0:T(8,128)(2,1)S(1)} %maximum_select_fusion.35), channel_id=1, source_target_pairs={{0,2},{2,0},{4,6},{6,4},{8,10},{10,8},{12,14},{14,12},{16,18},{18,... | collective-permute-start | bytes 2457608 | tf_op jit(solution)/shard_map/ppermute | solution.py:118
  1043.4 53.5 %collective-permute-start.121 = (bf16[2,80,2560]{2,1,0:T(8,128)(2,1)S(1)}, bf16[2,80,2560]{2,1,0:T(8,128)(2,1)S(1)}, u32[]{:S(2)}, u32[]{:S(2)}) collective-permute-start(bf16[2,80,2560]{2,1,0:T(8,128)(2,1)S(1)} %maximum_select_fusion.34), channel_id=1, source_target_pairs={{0,2},{2,0},{4,6},{6,4},{8,10},{10,8},{12,14},{14,12},{16,18},{18,... | collective-permute-start | bytes 2457608 | tf_op jit(solution)/shard_map/ppermute | solution.py:118
  (193 other events, 2764.4 us)

commit v2 on v1

--- a/solution.py
+++ b/solution.py
@@ -3,6 +3,8 @@
 import jax
 import jax.numpy as jnp
 from jax import lax
+from jax.experimental import pallas as pl
+from jax.experimental.pallas import tpu as pltpu
 from jax.sharding import PartitionSpec as P
 
 HEADS = 16
@@ -103,145 +105,515 @@
     return jnp.einsum("tj,ij->ti", grad_rows, weight_full, preferred_element_type=jnp.float32)
 
 
-def add_low(left, right):
-    return (left.astype(jnp.float32) + right.astype(jnp.float32)).astype(jnp.bfloat16)
+MESH = pl.DeviceIdType.MESH
+
+
+class Place:
+    def __init__(self, n_rep):
+        rep = lax.axis_index("rep")
+        self.nz = n_rep // 4
+        self.half = self.nz // 2
+        self.y = lax.axis_index("shard")
+        self.z, self.x, self.c = rep // 4, (rep // 2) % 2, rep % 2
+        self.low = self.z < self.half
+        self.depth = jnp.where(self.low, self.z, self.nz - 1 - self.z)
+        side = jnp.where(self.low, 1, -1)
+        self.to_core = {"rep": self.z * 4 + self.x * 2 + (1 - self.c)}
+        self.to_x = {"rep": self.z * 4 + (1 - self.x) * 2 + self.c}
+        self.to_y = {"shard": 1 - self.y}
+        self.to_in = {"rep": (self.z + side) * 4 + self.x * 2 + self.c}
+        self.to_out = {"rep": (self.z - side) * 4 + self.x * 2 + self.c}
+
+    def at_depth(self, depth):
+        return pl.when(self.depth == depth)
+
+    def meet(self, with_y):
+        barrier = pltpu.get_barrier_semaphore()
+        near = [self.to_core, self.to_x, self.to_in] + ([self.to_y] if with_y else [])
+        for device in near:
+            pl.semaphore_signal(barrier, inc=1, device_id=device, device_id_type=MESH)
+
+        @pl.when(self.depth > 0)
+        def _():
+            pl.semaphore_signal(barrier, inc=1, device_id=self.to_out, device_id_type=MESH)
+
+        pl.semaphore_wait(barrier, jnp.where(self.depth > 0, len(near) + 1, len(near)))
+
+
+def remote(src, dst, sems, k, device):
+    return pltpu.make_async_remote_copy(
+        src_ref=src,
+        dst_ref=dst,
+        send_sem=sems.at[0, k],
+        recv_sem=sems.at[1, k],
+        device_id=device,
+        device_id_type=MESH,
+    )
+
+
+def add_into(dst, one, two):
+    rows = dst.shape[0]
+    step = 32 if rows % 32 == 0 else rows
+
+    @pl.loop(0, rows // step)
+    def _(i):
+        spot = pl.ds(pl.multiple_of(i * step, step), step)
+        total = one[spot, :].astype(jnp.float32) + two[spot, :].astype(jnp.float32)
+        dst[spot, :] = total.astype(dst.dtype)
+
+
+def skewed(count, stages):
+    last = max(offset for offset, _ in stages)
+    for tick in range(count + last):
+        for offset, stage in sorted(stages, key=lambda item: -item[0]):
+            if 0 <= tick - offset < count:
+                stage(tick - offset)
+
+
+def gather_kernel(n_rep, chunks, shard_rows, rows, wide, *refs):
+    count, n_w = len(chunks), len(shard_rows)
+    shards, fulls = refs[:n_w], refs[n_w : 2 * n_w]
+    hold, own_in, own_out, y_sem, d_sem, in_sem, mid_sem, back_sem, x_sem, c_sem, cd_sem = refs[
+        2 * n_w :
+    ]
+    at = Place(n_rep)
+    nz, half = at.nz, at.half
+    plane = rows * 4 // 5
+    unit = plane // n_rep
+    straight = (rows - plane) // 2
+    mine, yours = at.y, 1 - at.y
+
+    def shard(k, first, size):
+        w, row0, col0 = chunks[k]
+        return shards[w].at[pl.ds(pl.multiple_of(row0 + first, 8), size), pl.ds(col0, wide)]
+
+    def full(k, owner, first, size):
+        w, row0, col0 = chunks[k]
+        start = pl.multiple_of(owner * shard_rows[w] + row0 + first, 8)
+        return fulls[w].at[pl.ds(start, size), pl.ds(col0, wide)]
+
+    def place(c, x, z):
+        return ((c * 2 + x) * nz + z) * unit
+
+    def y_copy(k, owner):
+        first = place(at.c, at.x, at.z)
+        return remote(shard(k, first, unit), full(k, owner, first, unit), y_sem, k, at.to_y)
+
+    def d_copy(k, owner):
+        first = plane + at.c * straight
+        return remote(
+            shard(k, first, straight), full(k, owner, first, straight), d_sem, k, at.to_y
+        )
+
+    def along(k, begin, size, sems, device):
+        view = full(k, yours, place(at.c, at.x, begin), size * unit)
+        return remote(view, view, sems, k, device)
+
+    def in_send(k, depth):
+        return along(k, jnp.where(at.low, 0, nz - 1 - depth), depth + 1, in_sem, at.to_in)
+
+    def in_take(k, depth):
+        return along(k, jnp.where(at.low, 0, nz - depth), depth, in_sem, at.to_in)
+
+    def mid_send(k):
+        return along(k, jnp.where(at.low, 0, half), half, mid_sem, at.to_in)
+
+    def mid_take(k):
+        return along(k, jnp.where(at.low, half, 0), half, mid_sem, at.to_in)
+
+    def back_send(k, depth):
+        return along(k, jnp.where(at.low, depth, 0), nz - depth, back_sem, at.to_out)
+
+    def back_take(k, depth):
+        return along(k, jnp.where(at.low, depth + 1, 0), nz - depth - 1, back_sem, at.to_out)
+
+    def x_copy(k, x):
+        view = full(k, yours, place(at.c, x, 0), nz * unit)
+        return remote(view, view, x_sem, k, at.to_x)
+
+    def c_copy(k, c):
+        view = full(k, yours, place(c, 0, 0), 2 * nz * unit)
+        return remote(view, view, c_sem, k, at.to_core)
+
+    def cd_copy(k, c):
+        view = full(k, yours, plane + c * straight, straight)
+        return remote(view, view, cd_sem, k, at.to_core)
+
+    def own_load(k):
+        return pltpu.make_async_copy(shard(k, 0, rows), hold.at[k % 3], own_in.at[k])
+
+    def own_store(k):
+        return pltpu.make_async_copy(hold.at[k % 3], full(k, mine, 0, rows), own_out.at[k])
+
+    def inner_send(k, depth):
+        (mid_send(k) if depth == half - 1 else in_send(k, depth)).start()
+
+    def take_own(k):
+        if k >= 3:
+            own_store(k - 3).wait()
+        own_load(k).start()
+
+    def crossed(k):
+        own_load(k).wait()
+        own_store(k).start()
+        y_copy(k, yours).wait_recv()
+
+        @at.at_depth(0)
+        def _():
+            inner_send(k, 0)
+
+        d_copy(k, yours).wait_recv()
+        cd_copy(k, at.c).start()
+
+    def pass_in(depth):
+        def stage(k):
+            @at.at_depth(depth)
+            def _():
+                in_take(k, depth).wait_recv()
+                inner_send(k, depth)
+
+        return stage
+
+    def middle(k):
+        @at.at_depth(half - 1)
+        def _():
+            mid_take(k).wait_recv()
+            if half > 1:
+                back_send(k, half - 1).start()
+            x_copy(k, at.x).start()
+
+    def pass_out(depth):
+        def stage(k):
+            @at.at_depth(depth)
+            def _():
+                back_take(k, depth).wait_recv()
+                if depth > 0:
+                    back_send(k, depth).start()
+                x_copy(k, at.x).start()
+
+        return stage
+
+    def crossed_x(k):
+        x_copy(k, 1 - at.x).wait_recv()
+        c_copy(k, at.c).start()
+
+    at.meet(True)
+    for k in range(count):
+        y_copy(k, mine).start()
+        d_copy(k, mine).start()
+    stages = [(0, take_own), (1, crossed)]
+    stages += [(1 + depth, pass_in(depth)) for depth in range(1, half)]
+    stages += [(1 + half, middle)]
+    stages += [(1 + half + (half - 1 - depth), pass_out(depth)) for depth in range(half - 1)]
+    stages += [(2 * half + 1, crossed_x)]
+    skewed(count, stages)
+    for k in range(count):
+        if k >= count - 3:
+            own_store(k).wait()
+        y_copy(k, mine).wait_send()
+        d_copy(k, mine).wait_send()
+        x_copy(k, at.x).wait_send()
+        c_copy(k, at.c).wait_send()
+        cd_copy(k, at.c).wait_send()
+        for depth in range(half):
+
+            @at.at_depth(depth)
+            def _():
+                (mid_send(k) if depth == half - 1 else in_send(k, depth)).wait_send()
+                if depth > 0:
+                    back_send(k, depth).wait_send()
+
+        c_copy(k, 1 - at.c).wait_recv()
+        cd_copy(k, 1 - at.c).wait_recv()
+
+
+def gather_weights(shards, n_rep, n_shard):
+    if n_shard != 2:
+        return [lax.all_gather(shard, "shard", axis=0, tiled=True) for shard in shards]
+    rows, wide, chunks = cut_chunks(shards)
+    count = len(chunks)
+    shapes = [(shard.shape[0] * n_shard, shard.shape[1]) for shard in shards]
+    kernel = partial(
+        gather_kernel, n_rep, chunks, [shard.shape[0] for shard in shards], rows, wide
+    )
+    pair = pltpu.SemaphoreType.DMA((2, count))
+    return pl.pallas_call(
+        kernel,
+        out_shape=[jax.ShapeDtypeStruct(shape, jnp.bfloat16) for shape in shapes],
+        in_specs=[pl.BlockSpec(memory_space=pl.ANY)] * len(shards),
+        out_specs=[pl.BlockSpec(memory_space=pl.ANY)] * len(shards),
+        scratch_shapes=[pltpu.VMEM((3, rows, wide), jnp.bfloat16)]
+        + [pltpu.SemaphoreType.DMA((count,))] * 2
+        + [pair] * 8,
+        compiler_params=pltpu.CompilerParams(
+            collective_id=0, has_side_effects=True, vmem_limit_bytes=60 << 20
+        ),
+        name="gather_weights",
+    )(*shards)
+
+
+def cut_chunks(shards):
+    rows = min(shard.shape[0] for shard in shards)
+    wide = min(shard.shape[1] for shard in shards)
+    chunks = []
+    for w, shard in enumerate(shards):
+        for row0 in range(0, shard.shape[0], rows):
+            for col0 in range(0, shard.shape[1], wide):
+                chunks.append((w, row0, col0))
+    return rows, wide, chunks
+
+
+def reduce_kernel(n_rep, parts, chunks, shard_rows, rows, wide, *refs):
+    count, n_w = len(chunks), len(shard_rows)
+    sources, outs, arrived = refs[:n_w], refs[n_w : 2 * n_w], refs[2 * n_w]
+    (
+        held, lent, got_y, got_x, got_in, got_mid, total,
+        own_in, lent_in, put, c0_sem, c1_sem, y_sem, x_sem, in_sem, mid_sem, back_sem,
+        ax_sem, ac_sem, af_sem,
+    ) = refs[2 * n_w + 1 :]
+    c_sems = [c0_sem, c1_sem]
+    at = Place(n_rep)
+    half = at.half
+    block = rows // 4
+    with_y = parts == 2
+    mine = at.y if with_y else 0
+
+    def source(k, owner, c):
+        w, row0, col0 = chunks[k]
+        start = pl.multiple_of(owner * shard_rows[w] + row0 + c * 2 * block, 8)
+        return sources[w].at[pl.ds(start, 2 * block), pl.ds(col0, wide)]
+
+    def out(k, c, x):
+        w, row0, col0 = chunks[k]
+        start = pl.multiple_of(row0 + (c * 2 + x) * block, 8)
+        return outs[w].at[pl.ds(start, block), pl.ds(col0, wide)]
+
+    def rows_of(x):
+        return pl.ds(pl.multiple_of(x * block, 8), block)
+
+    def c_send(k, owner):
+        return remote(
+            source(k, owner, 1 - at.c), arrived.at[k, owner], c_sems[owner], k, at.to_core
+        )
+
+    def own_load(k, owner):
+        return pltpu.make_async_copy(
+            source(k, owner, at.c), held.at[k, owner], own_in.at[owner, k]
+        )
+
+    def lent_load(k, owner):
+        return pltpu.make_async_copy(
+            arrived.at[k, owner], lent.at[k % 2, owner], lent_in.at[owner, k]
+        )
+
+    def y_send(k):
+        return remote(held.at[k, 1 - mine], got_y.at[k], y_sem, k, at.to_y)
+
+    def x_send(k):
+        return remote(
+            held.at[k, mine, rows_of(1 - at.x)], got_x.at[k], x_sem, k, at.to_x
+        )
+
+    def part(k):
+        return held.at[k, mine, rows_of(at.x)]
+
+    def in_send(k):
+        return remote(part(k), got_in.at[k], in_sem, k, at.to_in)
+
+    def mid_send(k):
+        return remote(part(k), got_mid.at[k], mid_sem, k, at.to_in)
+
+    def back_send(k):
+        return remote(total.at[k], total.at[k], back_sem, k, at.to_out)
+
+    def ax_send(k, x):
+        return remote(total.at[k], out(k, at.c, x), ax_sem, k, at.to_x)
+
+    def ac_send(k, c):
+        return remote(total.at[k], out(k, c, at.x), ac_sem, k, at.to_core)
+
+    def af_send(k, c):
+        view = out(k, c, 1 - at.x)
+        return remote(view, view, af_sem, k, at.to_core)
+
+    def own_put(k):
+        return pltpu.make_async_copy(total.at[k], out(k, at.c, at.x), put.at[k])
+
+    def start_core(k):
+        for owner in range(parts):
+            c_send(k, owner).start()
+            own_load(k, owner).start()
+
+    def load_core(k):
+        for owner in range(parts):
+            c_send(k, owner).wait_recv()
+            lent_load(k, owner).start()
+
+    def start_y(k):
+        for owner in range(parts):
+            own_load(k, owner).wait()
+            lent_load(k, owner).wait()
+        if with_y:
+            other = 1 - mine
+            add_into(held.at[k, other], held.at[k, other], lent.at[k % 2, other])
+            y_send(k).start()
+        add_into(held.at[k, mine], held.at[k, mine], lent.at[k % 2, mine])
+
+    def start_x(k):
+        if with_y:
+            y_send(k).wait_recv()
+            spot = rows_of(1 - at.x)
+            add_into(held.at[k, mine, spot], held.at[k, mine, spot], got_y.at[k, spot])
+        x_send(k).start()
+        if with_y:
+            add_into(part(k), part(k), got_y.at[k, rows_of(at.x)])
+
+    def inner_send(k, depth):
+        (mid_send(k) if depth == half - 1 else in_send(k)).start()
+
+    def start_z(k):
+        x_send(k).wait_recv()
+        add_into(part(k), part(k), got_x.at[k])
+
+        @at.at_depth(0)
+        def _():
+            inner_send(k, 0)
+
+    def pass_in(depth):
+        def stage(k):
+            @at.at_depth(depth)
+            def _():
+                in_send(k).wait_recv()
+                add_into(part(k), part(k), got_in.at[k])
+                inner_send(k, depth)
+
+        return stage
+
+    def spread(k, depth):
+        if depth > 0:
+            back_send(k).start()
+        ax_send(k, at.x).start()
+        ac_send(k, at.c).start()
+        own_put(k).start()
+
+    def middle(k):
+        @at.at_depth(half - 1)
+        def _():
+            mid_send(k).wait_recv()
+            add_into(total.at[k], part(k), got_mid.at[k])
+            spread(k, half - 1)
+
+    def pass_out(depth):
+        def stage(k):
+            @at.at_depth(depth)
+            def _():
+                back_send(k).wait_recv()
+                spread(k, depth)
+
+        return stage
+
+    def forward(k):
+        ax_send(k, 1 - at.x).wait_recv()
+        af_send(k, at.c).start()
+
+    at.meet(with_y)
+    stages = [(0, start_core), (1, load_core), (2, start_y), (4, start_x), (5, start_z)]
+    stages += [(6 + depth - 1, pass_in(depth)) for depth in range(1, half)]
+    stages += [(6 + half - 1, middle)]
+    stages += [(6 + half + (half - 2 - depth), pass_out(depth)) for depth in range(half - 1)]
+    stages += [(5 + 2 * half, forward)]
+    skewed(count, stages)
+    for k in range(count):
+        for owner in range(parts):
+            c_send(k, owner).wait_send()
+        if with_y:
+            y_send(k).wait_send()
+        x_send(k).wait_send()
+        for depth in range(half):
+
+            @at.at_depth(depth)
+            def _():
+                (mid_send(k) if depth == half - 1 else in_send(k)).wait_send()
+                if depth > 0:
+                    back_send(k).wait_send()
+
+        ax_send(k, at.x).wait_send()
+        ac_send(k, at.c).wait_send()
+        af_send(k, at.c).wait_send()
+        own_put(k).wait()
+        ac_send(k, 1 - at.c).wait_recv()
+        af_send(k, 1 - at.c).wait_recv()
+
+
+def reduce_products(products, n_rep, n_shard):
+    parts = n_shard
+    if n_shard != 2:
+        products = [
+            lax.psum_scatter(item, "shard", scatter_dimension=0, tiled=True) for item in products
+        ]
+        parts = 1
+    owned = [
+        jax.ShapeDtypeStruct((item.shape[0] // parts, item.shape[1]), jnp.bfloat16)
+        for item in products
+    ]
+    rows, wide, chunks = cut_chunks(owned)
+    count, block = len(chunks), rows // 4
+    kernel = partial(
+        reduce_kernel, n_rep, parts, chunks, [item.shape[0] for item in owned], rows, wide
+    )
+    pair = pltpu.SemaphoreType.DMA((2, count))
+    low = jnp.bfloat16
+    anywhere = pl.BlockSpec(memory_space=pl.ANY)
+    results = pl.pallas_call(
+        kernel,
+        out_shape=owned + [jax.ShapeDtypeStruct((count, parts, 2 * block, wide), low)],
+        in_specs=[anywhere] * len(products),
+        out_specs=[anywhere] * (len(products) + 1),
+        scratch_shapes=[
+            pltpu.VMEM((count, parts, 2 * block, wide), low),
+            pltpu.VMEM((2, parts, 2 * block, wide), low),
+            pltpu.VMEM((count, 2 * block, wide), low),
+            pltpu.VMEM((count, block, wide), low),
+            pltpu.VMEM((count, block, wide), low),
+            pltpu.VMEM((count, block, wide), low),
+            pltpu.VMEM((count, block, wide), low),
+            pltpu.SemaphoreType.DMA((parts, count)),
+            pltpu.SemaphoreType.DMA((parts, count)),
+            pltpu.SemaphoreType.DMA((count,)),
+        ]
+        + [pair] * 10,
+        compiler_params=pltpu.CompilerParams(
+            collective_id=1, has_side_effects=True, vmem_limit_bytes=62 << 20
+        ),
+        name="reduce_products",
+    )(*products)
+    return results[:-1]
 
 
 class Links:
     def __init__(self, n_rep, n_shard):
         self.nz, self.ny, self.n_rep = n_rep // 4, n_shard, n_rep
-        rep = lax.axis_index("rep")
         self.y = lax.axis_index("shard")
-        self.z, self.x, self.c = rep // 4, (rep // 2) % 2, rep % 2
-
-    def swap_core(self, item):
-        return lax.ppermute(item, "rep", [(i, i ^ 1) for i in range(self.n_rep)])
-
-    def swap_x(self, item):
-        return lax.ppermute(item, "rep", [(i, i ^ 2) for i in range(self.n_rep)])
-
-    def swap_y(self, item):
-        return lax.ppermute(item, "shard", [(0, 1), (1, 0)])
-
-    def send_z(self, item, pairs):
-        return lax.ppermute(
-            item, "rep", [(a * 4 + k, b * 4 + k) for a, b in pairs for k in range(4)]
-        )
-
-    def inward(self, step):
-        last = self.nz - 1
-        return [(step, step + 1), (last - step, last - step - 1)]
-
-    def outward(self, step):
-        return [(b, a) for a, b in self.inward(step)]
-
-    def middle(self):
-        half = self.nz // 2
-        return [(half - 1, half), (half, half - 1)]
-
-    def in_order(self, index, mine, theirs, axis=0):
-        first = jnp.concatenate([mine, theirs], axis=axis)
-        second = jnp.concatenate([theirs, mine], axis=axis)
-        return jnp.where(index == 0, first, second)
-
-    def reduce_z(self, part):
-        for step in range(self.nz // 2 - 1):
-            part = add_low(part, self.send_z(part, self.inward(step)))
-        part = add_low(part, self.send_z(part, self.middle()))
-        for step in reversed(range(self.nz // 2 - 1)):
-            moved = self.send_z(part, self.outward(step))
-            outer = (self.z == step) | (self.z == self.nz - 1 - step)
-            part = jnp.where(outer, moved, part)
-        return part
-
-    def gather_z(self, part):
-        low = self.z < self.nz // 2
-        own = part
-        for step in range(self.nz // 2 - 1):
-            moved = self.send_z(part, self.inward(step))
-            part = jnp.where(
-                low, jnp.concatenate([moved, own], 0), jnp.concatenate([own, moved], 0)
+
+    def gather_vector(self, vector):
+        return lax.all_gather(vector, "shard", axis=0, tiled=False)
+
+    def sum_all(self, vector):
+        for flip in (1, 2):
+            vector = vector + lax.ppermute(
+                vector, "rep", [(i, i ^ flip) for i in range(self.n_rep)]
             )
-        part = self.in_order(jnp.where(low, 0, 1), part, self.send_z(part, self.middle()))
-        for step in reversed(range(self.nz // 2 - 1)):
-            moved = self.send_z(part, self.outward(step))
-            outer = (self.z == step) | (self.z == self.nz - 1 - step)
-            part = jnp.where(outer, moved, part)
-        return part
-
-    def gather_plane(self, weight):
-        rows = weight.shape[0] // self.n_rep
-        place = ((self.c * 2 + self.x) * self.nz + self.z) * rows
-        part = self.swap_y(lax.dynamic_slice_in_dim(weight, place, rows, 0))
-        part = self.gather_z(part)
-        part = self.in_order(self.x, part, self.swap_x(part))
-        return self.in_order(self.c, part, self.swap_core(part))
-
-    def gather_straight(self, weight):
-        rows = weight.shape[0] // 2
-        part = self.swap_y(lax.dynamic_slice_in_dim(weight, self.c * rows, rows, 0))
-        return self.in_order(self.c, part, self.swap_core(part))
-
-    def gather_weight(self, weight, cuts):
-        if self.ny != 2:
-            return lax.all_gather(weight, "shard", axis=0, tiled=True)
-        pieces = []
-        for start, stop, plane in cuts:
-            block = weight[:, start:stop]
-            pieces.append(self.gather_plane(block) if plane else self.gather_straight(block))
-        other = jnp.concatenate(pieces, axis=1)
-        return self.in_order(self.y, weight, other)
-
-    def gather_vector(self, vector):
-        if self.ny != 2:
-            return lax.all_gather(vector, "shard", axis=0, tiled=False)
-        return self.in_order(self.y, vector[None], self.swap_y(vector)[None])
-
-    def sum_all(self, vector):
-        vector = vector + self.swap_core(vector)
-        vector = vector + self.swap_x(vector)
         step = 1
         while step < self.nz:
-            vector = vector + self.send_z(vector, [(i, i ^ step) for i in range(self.nz)])
+            pairs = [(i, i ^ (4 * step)) for i in range(self.n_rep)]
+            vector = vector + lax.ppermute(vector, "rep", pairs)
             step *= 2
         step = 1
         while step < self.ny:
-            vector = vector + lax.ppermute(
-                vector, "shard", [(i, i ^ step) for i in range(self.ny)]
-            )
+            pairs = [(i, i ^ step) for i in range(self.ny)]
+            vector = vector + lax.ppermute(vector, "shard", pairs)
             step *= 2
         return vector
-
-    def pick(self, stacked, index):
-        return lax.dynamic_index_in_dim(stacked, index, 0, keepdims=False)
-
-    def reduce_part(self, part):
-        if self.ny == 2:
-            got = self.swap_y(self.pick(part, 1 - self.y))
-            part = add_low(self.pick(part, self.y), got)
-        else:
-            part = lax.psum_scatter(part, "shard", scatter_dimension=0, tiled=False)
-        got = self.swap_x(self.pick(part, 1 - self.x))
-        part = add_low(self.pick(part, self.x), got)
-        part = self.reduce_z(part)
-        part = self.in_order(self.x, part[None], self.swap_x(part)[None])
-        return part
-
-    def weight_gradient(self, left, right, chunks):
-        half = right.shape[1] // 2
-        kept = lax.dynamic_slice_in_dim(right, self.c * half, half, 1)
-        sent = lax.dynamic_slice_in_dim(right, (1 - self.c) * half, half, 1)
-        both_left = jnp.concatenate([left, self.swap_core(left)], axis=0)
-        both_right = jnp.concatenate([kept, self.swap_core(sent)], axis=0)
-        product = row_product(both_left, both_right).astype(jnp.bfloat16)
-        rows = product.shape[0] // (self.ny * 2 * chunks)
-        product = product.reshape(self.ny, 2, chunks, rows, half)
-        parts = [self.reduce_part(product[:, :, i]) for i in range(chunks)]
-        full = []
-        for part in parts:
-            full.append(self.in_order(self.c, part, self.swap_core(part), axis=2))
-        total = jnp.stack(full, axis=1)
-        return total.reshape(2 * chunks * rows, 2 * half).astype(jnp.float32)
 
 
 def per_device(
@@ -290,18 +662,8 @@
         for i in range(len(sizes))
     ]
 
-    width = model_width
-    w_qkv = links.gather_weight(
-        qkv_weight,
-        [(0, 1024, True), (1024, 2048, True), (2048, 2816, True), (2816, 3840, False)],
-    )
-    w_proj = links.gather_weight(proj_weight, [(0, 1024, True), (1024, width, False)])
-    ff = fc1_weight.shape[1]
-    w_up = links.gather_weight(
-        fc1_weight, [(0, 1920, True), (1920, 3840, True), (3840, ff, False)]
-    )
-    w_down = links.gather_weight(
-        fc2_weight, [(0, 512, True), (512, 1024, True), (1024, width, False)]
+    w_qkv, w_proj, w_up, w_down = gather_weights(
+        [qkv_weight, proj_weight, fc1_weight, fc2_weight], n_rep, n_shard
     )
 
     input_rows = patches.astype(jnp.float32)
@@ -329,7 +691,7 @@
     sigmoid_up = 1.0 / (1.0 + jnp.exp(-quick_slope * up_pre))
     activation = (up_pre * sigmoid_up).astype(jnp.bfloat16)
 
-    d_w_down = links.weight_gradient(activation, cotangent, 4)
+    d_w_down = row_product(activation, cotangent).astype(jnp.bfloat16)
     out_full = (
         hidden_rows + jnp.dot(activation, w_down, preferred_element_type=jnp.float32) + b_down
     )
@@ -339,7 +701,7 @@
     grad_act = back_product(cotangent, w_down)
     slope_up = sigmoid_up + quick_slope * up_pre * sigmoid_up * (1.0 - sigmoid_up)
     grad_pre = (grad_act * slope_up).astype(jnp.bfloat16)
-    d_w_up = links.weight_gradient(second_normalized, grad_pre, 4)
+    d_w_up = row_product(second_normalized, grad_pre).astype(jnp.bfloat16)
     d_b_up = jnp.sum(grad_pre.astype(jnp.float32), axis=0)
     second_normalized_gradient = back_product(grad_pre, w_up)
     second_gain_gradient = jnp.sum(second_normalized_gradient * second_centered_standard, axis=0)
@@ -351,7 +713,7 @@
         second_norm_gain,
     )
     grad_branch = grad_hidden.astype(jnp.bfloat16)
-    d_w_proj = links.weight_gradient(heads_out, grad_branch, 1)
+    d_w_proj = row_product(heads_out, grad_branch).astype(jnp.bfloat16)
     d_b_proj = jnp.sum(grad_branch.astype(jnp.float32), axis=0)
     grad_heads = back_product(grad_branch, w_proj).astype(jnp.bfloat16).reshape(pack_shape)
     grad_query, grad_key, grad_value = lax.map(
@@ -366,7 +728,7 @@
         .reshape(row_count, 3 * model_width)
         .astype(jnp.bfloat16)
     )
-    d_w_qkv = links.weight_gradient(first_normalized, grad_qkv, 4)
+    d_w_qkv = row_product(first_normalized, grad_qkv).astype(jnp.bfloat16)
     d_b_qkv = jnp.sum(grad_qkv.astype(jnp.float32), axis=0)
     first_normalized_gradient = back_product(grad_qkv, w_qkv)
     first_gain_gradient = jnp.sum(first_normalized_gradient * first_centered_standard, axis=0)
@@ -377,6 +739,11 @@
         first_inverse_spread,
         first_norm_gain,
     )
+
+    d_w_down, d_w_up, d_w_proj, d_w_qkv = [
+        item.astype(jnp.float32)
+        for item in reduce_products([d_w_down, d_w_up, d_w_proj, d_w_qkv], n_rep, n_shard)
+    ]
 
     def own_parts(vectors):
         lens = [item.shape[0] for item in vectors]

time: 1220 us -> 702 us (0.58)
  waiting for transfers between devices: 475 us -> 6.76 us
  Pallas kernels: 0 us -> 406 us
  starting transfers between devices: 204 us -> 7.59 us
  other arithmetic: 216 us -> 66 us
  local copies, waits for them, and re-layouts: 99.4 us -> 28 us
  matrix products: 209 us -> 171 us
    ppermute x166 -> x10, waiting for transfers between devices: 475 us -> 6.76 us  [the longest x2 2.56 us: sum_all(): vector = vector + lax.ppermute(vector, 'shard', pairs)]
    pallas_call x0 -> x2, Pallas kernels: none -> 406 us  [the longest x1 275 us: reduce_products(): pl.pallas_call(kernel, out_shape=owned + [jax.ShapeDtypeStruct((count, pa...]
    ppermute x166 -> x10, starting transfers between devices: 204 us -> 7.59 us  [the longest x4 4.67 us: sum_all(): vector = vector + lax.ppermute(vector, 'rep', pairs)]
    select_n x85 -> x0, other arithmetic: 153 us -> none  [the longest x56 147 us: in_order(): return jnp.where(index == 0, first, second)]
    convert_element_type x3 -> x0, local copies, waits for them, and re-layouts: 26.5 us -> none  [weight_gradient(): return total.reshape(2 * chunks * rows, 2 * half).astype(jnp.float32)]
    dot_general x4, matrix products: 73.3 us -> 47.7 us  [back_product(): jnp.einsum('tj,ij->ti', grad_rows, weight_full, preferred_element_type=jn...]
    dot_general x1, matrix products: 32.9 us -> 16.1 us  [per_device(): jnp.dot(activation, w_down, preferred_element_type=jnp.float32)]
    dynamic_slice x16 -> x0, local copies, waits for them, and re-layouts: 16 us -> none  [the longest x8 7.04 us: gather_plane(): part = self.swap_y(lax.dynamic_slice_in_dim(weight, place, rows, 0))]
  transfers between devices with their start and end apart: 166 -> 10, of which waited for: 72 -> 4; matrix products, arithmetic and copies ran while one was open for 41% -> 12% of each run, Pallas kernels for 0% -> 40%
where the time goes in v2:
time: 702 us; the launch traced here: 692 us
  Pallas kernels  406 us (58%)
  matrix products  171 us (24%)
  other arithmetic  66 us (9%)
  local copies, waits for them, and re-layouts  28 us (4%)
  starting transfers between devices  7.59 us (1%)
    pallas_call x1, Pallas kernels, reduce_products(): pl.pallas_call(kernel, out_shape=owned + [jax.ShapeDtypeStruct((count, pa...  275 us
    pallas_call x1, Pallas kernels, gather_weights(): pl.pallas_call(kernel, out_shape=[jax.ShapeDtypeStruct(shape, jnp.bfloat1...  130 us
    dot_general x4, matrix products, back_product(): jnp.einsum('tj,ij->ti', grad_rows, weight_full, preferred_element_type=jn...  47.7 us
    dot_general x4, matrix products, row_product(): jnp.einsum('ti,tj->ij', left, right, preferred_element_type=jnp.float32)  35.9 us
    convert_element_type x4, other arithmetic, per_device(): item.astype(jnp.float32)  27.5 us
    dot_general x1, matrix products, per_device(): jnp.dot(activation, w_down, preferred_element_type=jnp.float32)  16.1 us
  transfers between devices with their start and end apart: 10, of which 4 were waited for; matrix products, arithmetic and copies ran while one was open for 12% of the time, Pallas kernels for 40%

profile of v2, /device:TPU:0, one launch (start us, length us, event | category | flops | bytes accessed | tf_op | source)
XLA Modules:
  0.0 692.4 jit_solution(12751022115014557300)
XLA Ops:
  7.6 5.5 all-gather.1
  16.0 130.1 %gather_weights.1 = (bf16[1280,3840]{1,0:T(8,128)(2,1)}, bf16[1280,1280]{1,0:T(8,128)(2,1)}, bf16[1280,5120]{1,0:T(8,128)(2,1)}, bf16[5120,1280]{1,0:T(8,128)(2,1)}) custom-call(bf16[640,3840]{1,0:T(8,128)(2,1)} %refs_0_.1, bf16[640,1280]{1,0:T(8,128)(2,1)} %refs_1_.1, bf16[640,5120]{1,0:T(8,128)(2,1)} %refs_2_.1, bf16[2560,1280]{1,0:T(8,128)(2,1)} %refs_3_.1), custom_call_target="tpu_custom_call" | custom-call | tf_op jit(solution)/shard_map/gather_weights/pallas_call | solution.py:340
  146.2 11.6 %convolution_add_fusion = f32[512,3840]{1,0:T(8,128)} fusion(bf16[1280,3840]{1,0:T(8,128)(2,1)} %get-tuple-element.73, f32[3840]{0:T(1024)S(1)} %reshape.368, bf16[512,1280]{1,0:T(8,128)(2,1)S(1)} %copy-done, f32[1280]{0:T(1024)S(1)} %reshape.367, f32[1280]{0:T(1024)S(1)} %reshape.366, f32[512]{0:T(512)S(1)} %add_rsqrt_fusion.1, ...), kind=kOutput, calls=%fused_computation.22 | convolution fusion | flops 5039063040 | bytes 19035136 | tf_op jit(solution)/shard_map/dot_general | solution.py:674
  157.8 9.1 %copy.51 = f32[512,3840]{0,1:T(8,128)} copy(f32[512,3840]{1,0:T(8,128)} %convolution_add_fusion) | data formatting | bytes 15728640 | tf_op jit(solution)/shard_map/add | solution.py:674
  166.9 4.9 slice_bitcast_fusion
  172.3 2.4 slice_negate_fusion.2
  175.4 3.1 fusion.27
  178.5 7.6 %fusion.50 = (f32[16,512]{1,0:T(8,128)S(1)}, f32[16,512,512]{1,2,0:T(8,128)}) fusion(bf16[512,16,80]{0,2,1:T(8,128)(2,1)S(1)} %get-tuple-element.94, bf16[512,16,80]{0,2,1:T(8,128)(2,1)S(1)} %get-tuple-element.93, pred[512,512]{0,1:T(8,128)(4,1)S(1)} %broadcast_compare_fusion), kind=kOutput, calls=%fused_computation.120 | convolution fusion | flops 683663360 | bytes 19693568 | tf_op jit(solution)/shard_map/while/body/eval_jaxpr/qhd,khd->hqk/dot_general | solution.py:59
  186.2 8.3 %fusion = f32[16,512]{1,0:T(8,128)S(1)} fusion(f32[16,512,512]{1,2,0:T(8,128)} %get-tuple-element.131, f32[16,512]{1,0:T(8,128)S(1)} %get-tuple-element.130), kind=kLoop, calls=%fused_computation.9 | loop fusion | flops 8380416 | bytes 16842752 | tf_op jit(solution)/shard_map/while/body/eval_jaxpr/reduce_sum | solution.py:71
  194.5 10.5 %fusion.33 = bf16[16,80,512]{2,1,0:T(8,128)(2,1)} fusion(f32[16,512,512]{1,2,0:T(8,128)} %get-tuple-element.131, f32[16,512]{1,0:T(8,128)S(1)} %fusion, f32[16,512]{1,0:T(8,128)S(1)} %get-tuple-element.130, f32[512,3,16,80]{0,3,2,1:T(8,128)} %bitcast.75), kind=kOutput, calls=%fused_computation.73 | convolution fusion | flops 684326912 | bytes 19464192 | tf_op jit(solution)/shard_map/while/body/eval_jaxpr/hqk,khd->qhd/dot_general | solution.py:73
  205.1 4.8 fusion.51
  210.3 10.4 %fusion.45 = f32[512,5120]{1,0:T(8,128)S(1)} fusion(bf16[1280,5120]{1,0:T(8,128)(2,1)} %get-tuple-element.75, f32[512,1280]{1,0:T(8,128)S(1)} %get-tuple-element.133, f32[1280]{0:T(1024)S(1)} %reshape.371, f32[1280]{0:T(1024)S(1)} %reshape.370, f32[512]{0:T(512)S(1)} %add_rsqrt_fusion, f32[512]{0:T(512)S(1)} %broadcast_multiply_fusion.8), kind=kOutput, calls=%fused_computation.115 | convolution fusion | flops 6714163200 | bytes 26228736 | tf_op jit(solution)/shard_map/dot_general | solution.py:690
  220.7 17.9 %convert_reduce_fusion = (f32[5120]{0:T(1024)S(1)}, bf16[512,5120]{1,0:T(8,128)(2,1)}) fusion(f32[512,5120]{1,0:T(8,128)S(1)} %fusion.45, f32[5120]{0:T(1024)S(1)} %reshape.372, bf16[5120,1280]{1,0:T(8,128)(2,1)} %get-tuple-element.76, bf16[512,1280]{1,0:T(8,128)(2,1)S(1)} %copy-done.18), kind=kOutput, calls=%fused_computation.13 | convolution fusion | flops 6744960000 | bytes 30187520 | tf_op jit(solution)/shard_map/tj,ij->ti/dot_general | solution.py:105
  238.6 14.3 %multiply_reduce_fusion.1 = (f32[1280]{0:T(1024)S(1)}, f32[512]{0:T(512)S(1)}, f32[512]{0:T(512)S(1)}, f32[1280]{0:T(1024)S(1)}, f32[512,1280]{1,0:T(8,128)}) fusion(f32[512,1280]{1,0:T(8,128)S(1)} %get-tuple-element.133, f32[512]{0:T(512)S(1)} %add_rsqrt_fusion, f32[512]{0:T(512)S(1)} %broadcast_multiply_fusion.8, f32[1280]{0:T(1024)S(1)} %reshape.370, ...), kind=kOutput, calls=%fused_computation.64 | convolution fusion | flops 6716781568 | bytes 23616512 | tf_op jit(solution)/shard_map/tj,ij->ti/dot_general | solution.py:105
  252.9 2.8 convert_reduce_fusion.4
  257.2 2.9 convolution_convert_fusion.4
  262.6 10.0 %fusion.30 = bf16[512,1,16,80]{0,3,2,1:T(8,128)(2,1)} fusion(bf16[512,16,80]{0,2,1:T(8,128)(2,1)} %bitcast.77, f32[16,512,512]{1,2,0:T(8,128)} %get-tuple-element.131, f32[16,512]{1,0:T(8,128)S(1)} %log_add_fusion), kind=kOutput, calls=%fused_computation.72 | convolution fusion | flops 679477248 | bytes 19431424 | tf_op jit(solution)/shard_map/while/body/eval_jaxpr/hqk,qhd->khd/dot_general | solution.py:94
  272.6 12.2 %multiply_reduce_fusion = (f32[16,512]{1,0:T(8,128)S(1)}, f32[16,512,512]{1,2,0:T(8,128)}) fusion(f32[16,512,512]{1,2,0:T(8,128)} %get-tuple-element.131, f32[16,512]{1,0:T(8,128)S(1)} %log_add_fusion, bf16[512,16,80]{0,2,1:T(8,128)(2,1)S(1)} %bitcast.78, f32[512,3,16,80]{0,3,2,1:T(8,128)} %bitcast.76), kind=kOutput, calls=%fused_computation.3 | convolution fusion | flops 683663360 | bytes 36241408 | tf_op jit(solution)/shard_map/while/body/eval_jaxpr/qhd,khd->hqk/dot_general | solution.py:81
  284.8 11.8 %multiply_convert_fusion = bf16[16,512,512]{1,2,0:T(8,128)(2,1)S(1)} fusion(f32[16,512,512]{1,2,0:T(8,128)} %get-tuple-element.136, f32[16,512,512]{1,2,0:T(8,128)} %get-tuple-element.131, f32[16,512]{1,0:T(8,128)S(1)} %get-tuple-element.135, f32[16,512]{1,0:T(8,128)S(1)} %log_add_fusion), kind=kLoop, calls=%fused_computation.2 | loop fusion | flops 16777216 | bytes 42008576 | tf_op jit(solution)/shard_map/while/body/eval_jaxpr/convert_element_type | solution.py:85
  296.6 2.6 fusion.52
  304.5 12.6 %fusion.22 = (f32[1280]{0:T(1024)S(1)}, f32[512]{0:T(512)S(1)}, f32[512]{0:T(512)S(1)}, f32[1280]{0:T(1024)S(1)}, f32[512,1280]{1,0:T(8,128)}) fusion(bf16[512,1280]{1,0:T(8,128)(2,1)S(1)} %copy-done.1, f32[512]{0:T(512)S(1)} %copy-done.25, f32[512]{0:T(512)S(1)} %copy-done.23, f32[1280]{0:T(1024)S(1)} %copy-done.20, bf16[512,3840]{0,1:T(8,128)(2,1)S(1)} %bitcast.81, ...), kind=kOutput, calls=%fused_computation.45 | convolution fusion | flops 5039715328 | bytes 17718272 | tf_op jit(solution)/shard_map/tj,ij->ti/dot_general | solution.py:105
  317.9 13.3 %convolution_convert_fusion.1.refs_0_ = bf16[5120,1280]{1,0:T(8,128)(2,1)} fusion(bf16[512,1280]{1,0:T(8,128)(2,1)} %param.31, f32[512,5120]{1,0:T(8,128)} %copy-done.30, f32[5120]{0:T(1024)S(1)} %reshape.372), kind=kOutput, calls=%fused_computation.1 | convolution fusion | flops 6733168640 | bytes 24924160 | tf_op jit(solution)/shard_map/ti,tj->ij/dot_general | solution.py:101
  331.3 10.6 %convolution_convert_fusion.refs_1_ = bf16[1280,5120]{1,0:T(8,128)(2,1)} fusion(bf16[512,5120]{1,0:T(8,128)(2,1)S(1)} %bitcast.91, f32[512,1280]{1,0:T(8,128)S(1)} %get-tuple-element.133, f32[1280]{0:T(1024)S(1)} %reshape.371, f32[1280]{0:T(1024)S(1)} %reshape.370, f32[512]{0:T(512)S(1)} %add_rsqrt_fusion, f32[512]{0:T(512)S(1)} %broadcast_multiply_fusion.8), kind=kOutput, calls=%fused_computation | convolution fusion | flops 6720716800 | bytes 20985856 | tf_op jit(solution)/shard_map/ti,tj->ij/dot_general | solution.py:101
  342.0 8.3 %convolution_convert_fusion.2.refs_3_ = bf16[1280,3840]{1,0:T(8,128)(2,1)} fusion(bf16[512,3840]{0,1:T(8,128)(2,1)S(1)} %bitcast.82, bf16[512,1280]{1,0:T(8,128)(2,1)S(1)} %copy-done.2, f32[1280]{0:T(1024)S(1)} %copy-done.27, f32[1280]{0:T(1024)S(1)} %copy-done.20, f32[512]{0:T(512)S(1)} %copy-done.25, f32[512]{0:T(512)S(1)} %copy-done.23), kind=kOutput, calls=%fused_computation.8 | convolution fusion | flops 5042012160 | bytes 15087616 | tf_op jit(solution)/shard_map/ti,tj->ij/dot_general | solution.py:101
  350.3 16.1 %fusion.15 = bf16[512,1280]{1,0:T(8,128)(2,1)} fusion(f32[512,1280]{1,0:T(8,128)S(1)} %get-tuple-element.133, bf16[5120,1280]{1,0:T(8,128)(2,1)} %get-tuple-element.76, f32[1280]{0:T(1024)S(1)} %reshape.373, f32[512,5120]{1,0:T(8,128)} %copy-done.30, f32[5120]{0:T(1024)S(1)} %reshape.372), kind=kOutput, calls=%fused_computation.38 | convolution fusion | flops 6728581120 | bytes 27550720 | tf_op jit(solution)/shard_map/dot_general | solution.py:696
  377.0 3.0 collective-permute-start.8
  380.1 3.6 convolution_convert_fusion.3.refs_2_
  383.7 275.4 %reduce_products.1 = (bf16[2560,1280]{1,0:T(8,128)(2,1)}, bf16[640,5120]{1,0:T(8,128)(2,1)}, bf16[640,1280]{1,0:T(8,128)(2,1)}, bf16[640,3840]{1,0:T(8,128)(2,1)}, bf16[12,2,320,1280]{3,2,1,0:T(8,128)(2,1)}) custom-call(bf16[5120,1280]{1,0:T(8,128)(2,1)} %convolution_convert_fusion.1.refs_0_, bf16[1280,5120]{1,0:T(8,128)(2,1)} %convolution_convert_fusion.refs_1_, ...), custom_call_target="tpu_custom_call" | custom-call | tf_op jit(solution)/shard_map/reduce_products/pallas_call | solution.py:567
  659.1 7.1 %convert_element_type.257 = f32[640,3840]{1,0:T(8,128)} convert(bf16[640,3840]{1,0:T(8,128)(2,1)} %get-tuple-element.77) | non-fusion elementwise | flops 2457600 | bytes 14745600 | tf_op jit(solution)/shard_map/convert_element_type | solution.py:744
  668.2 9.6 %convert_element_type.260 = f32[640,5120]{1,0:T(8,128)} convert(bf16[640,5120]{1,0:T(8,128)(2,1)} %get-tuple-element.79) | non-fusion elementwise | flops 3276800 | bytes 19660800 | tf_op jit(solution)/shard_map/convert_element_type | solution.py:744
  677.8 8.8 %convert_element_type.261 = f32[2560,1280]{1,0:T(8,128)} convert(bf16[2560,1280]{1,0:T(8,128)(2,1)} %get-tuple-element.80) | non-fusion elementwise | flops 3276800 | bytes 19660800 | tf_op jit(solution)/shard_map/convert_element_type | solution.py:744
  688.1 2.6 collective-permute-done.9
  (151 shorter events, 36.7 us)
Async XLA Ops:
  0.6 14.9 %copy-start = (bf16[512,1280]{1,0:T(8,128)(2,1)S(1)}, bf16[512,1280]{1,0:T(8,128)(2,1)}, u32[]{:S(2)}) copy-start(bf16[512,1280]{1,0:T(8,128)(2,1)} %param.16) | copy-start | bytes 3932164
  13.9 132.3 %copy-start.26 = (f32[1280]{0:T(1024)}, f32[1280]{0:T(1024)S(1)}, u32[]{:S(2)}) copy-start(f32[1280]{0:T(1024)S(1)} %reshape.367) | copy-start | bytes 15364
  13.9 132.3 %copy-start.19 = (f32[1280]{0:T(1024)}, f32[1280]{0:T(1024)S(1)}, u32[]{:S(2)}) copy-start(f32[1280]{0:T(1024)S(1)} %reshape.366) | copy-start | bytes 15364
  15.5 130.7 %copy-start.22 = (f32[512]{0:T(512)}, f32[512]{0:T(512)S(1)}, u32[]{:S(2)}) copy-start(f32[512]{0:T(512)S(1)} %broadcast_multiply_fusion.9) | copy-start | bytes 6148
  16.0 130.2 %copy-start.24 = (f32[512]{0:T(512)}, f32[512]{0:T(512)S(1)}, u32[]{:S(2)}) copy-start(f32[512]{0:T(512)S(1)} %add_rsqrt_fusion.1) | copy-start | bytes 6148
  178.5 7.7 %copy-start.4 = (bf16[512,16,80]{0,2,1:T(8,128)(2,1)}, bf16[512,16,80]{0,2,1:T(8,128)(2,1)S(1)}, u32[]{:S(2)}) copy-start(bf16[512,16,80]{0,2,1:T(8,128)(2,1)S(1)} %get-tuple-element.93) | copy-start | bytes 3932164
  178.5 7.7 %copy-start.7 = (bf16[512,16,80]{0,2,1:T(8,128)(2,1)}, bf16[512,16,80]{0,2,1:T(8,128)(2,1)S(1)}, u32[]{:S(2)}) copy-start(bf16[512,16,80]{0,2,1:T(8,128)(2,1)S(1)} %get-tuple-element.94) | copy-start | bytes 3932164
  210.3 10.4 %copy-start.18 = (bf16[512,1280]{1,0:T(8,128)(2,1)S(1)}, bf16[512,1280]{1,0:T(8,128)(2,1)}, u32[]{:S(2)}) copy-start(bf16[512,1280]{1,0:T(8,128)(2,1)} %param.31) | copy-start | bytes 3932164
  220.7 17.9 %copy-start.30 = (f32[512,5120]{1,0:T(8,128)}, f32[512,5120]{1,0:T(8,128)S(1)}, u32[]{:S(2)}) copy-start(f32[512,5120]{1,0:T(8,128)S(1)} %fusion.45) | copy-start | bytes 31457284
  262.6 10.0 %copy-start.6 = (bf16[512,1280]{0,1:T(8,128)(2,1)S(1)}, bf16[512,1280]{0,1:T(8,128)(2,1)}, u32[]{:S(2)}) copy-start(bf16[512,1280]{0,1:T(8,128)(2,1)} %copy.53) | copy-start | bytes 3932164
  284.8 11.8 %copy-start.8 = (bf16[512,16,80]{0,2,1:T(8,128)(2,1)S(1)}, bf16[512,16,80]{0,2,1:T(8,128)(2,1)}, u32[]{:S(2)}) copy-start(bf16[512,16,80]{0,2,1:T(8,128)(2,1)} %copy-done.7) | copy-start | bytes 3932164
  304.5 12.7 %copy-start.14 = (bf16[512,3,16,80]{0,3,2,1:T(8,128)(2,1)}, bf16[512,3,16,80]{0,3,2,1:T(8,128)(2,1)S(1)}, u32[]{:S(2)}) copy-start(bf16[512,3,16,80]{0,3,2,1:T(8,128)(2,1)S(1)} %get-tuple-element.90) | copy-start | bytes 11796484
  317.3 49.2 %collective-permute-start = (f32[7680]{0:T(1024)S(1)}, f32[7680]{0:T(1024)S(1)}, u32[]{:S(2)}, u32[]{:S(2)}) collective-permute-start(f32[7680]{0:T(1024)S(1)} %pad_maximum_fusion.2), channel_id=1, source_target_pairs={{0,2},{2,0},{4,6},{6,4},{8,10},{10,8},{12,14},{14,12},{16,18},{18,... | collective-permute-start | bytes 92168 | tf_op jit(solution)/shard_map/ppermute | solution.py:603
  317.7 13.6 %slice-start = ((s8[5242880]{0:T(1024)(128)(4,1)}), s8[4194304]{0:T(1024)(128)(4,1)S(1)}, s32[]{:S(2)}) async-start(s8[5242880]{0:T(1024)(128)(4,1)} %bitcast.90), calls=%async_computation | async-start | bytes 8388608
  317.7 13.6 %slice-start.1 = ((s8[5242880]{0:T(1024)(128)(4,1)}), s8[1048576]{0:T(1024)(128)(4,1)S(1)}, s32[]{:S(2)}) async-start(s8[5242880]{0:T(1024)(128)(4,1)} %bitcast.90), calls=%async_computation.1 | async-start | bytes 2097152
  317.7 48.9 %collective-permute-start.5 = (f32[8960]{0:T(1024)S(1)}, f32[8960]{0:T(1024)S(1)}, u32[]{:S(2)}, u32[]{:S(2)}) collective-permute-start(f32[8960]{0:T(1024)S(1)} %pad_maximum_fusion.1), channel_id=1, source_target_pairs={{0,2},{2,0},{4,6},{6,4},{8,10},{10,8},{12,14},{14,12},{16,18},{18,... | collective-permute-start | bytes 107528 | tf_op jit(solution)/shard_map/ppermute | solution.py:603
  331.3 10.7 %copy-start.2 = (bf16[512,1280]{1,0:T(8,128)(2,1)S(1)}, bf16[512,1280]{1,0:T(8,128)(2,1)}, u32[]{:S(2)}) copy-start(bf16[512,1280]{1,0:T(8,128)(2,1)} %param.16) | copy-start | bytes 3932164
  331.3 10.7 %copy-start.15 = (bf16[512,3,16,80]{0,3,2,1:T(8,128)(2,1)S(1)}, bf16[512,3,16,80]{0,3,2,1:T(8,128)(2,1)}, u32[]{:S(2)}) copy-start(bf16[512,3,16,80]{0,3,2,1:T(8,128)(2,1)} %copy-done.14) | copy-start | bytes 11796484
  331.3 10.6 %copy-start.27 = (f32[1280]{0:T(1024)S(1)}, f32[1280]{0:T(1024)}, u32[]{:S(2)}) copy-start(f32[1280]{0:T(1024)} %copy-done.26) | copy-start | bytes 15364
  341.9 8.4 %copy-start.21 = (f32[2,640]{1,0:T(2,128)S(1)}, f32[2,640]{1,0:T(2,128)}, u32[]{:S(2)}) copy-start(f32[2,640]{1,0:T(2,128)} %get-tuple-element.118) | copy-start | bytes 15364
  350.3 24.3 %copy-start.3 = (bf16[512,1280]{1,0:T(8,128)(2,1)S(1)}, bf16[512,1280]{1,0:T(8,128)(2,1)}, u32[]{:S(2)}) copy-start(bf16[512,1280]{1,0:T(8,128)(2,1)} %param.16) | copy-start | bytes 3932164
  350.3 24.3 %copy-start.11 = (f32[512,1280]{1,0:T(8,128)S(1)}, f32[512,1280]{1,0:T(8,128)}, u32[]{:S(2)}) copy-start(f32[512,1280]{1,0:T(8,128)} %copy-done.10) | copy-start | bytes 7864324
  350.3 24.3 %copy-start.16 = (f32[512,1280]{1,0:T(8,128)S(1)}, f32[512,1280]{1,0:T(8,128)}, u32[]{:S(2)}) copy-start(f32[512,1280]{1,0:T(8,128)} %get-tuple-element.138) | copy-start | bytes 7864324
  366.5 4.2 collective-permute-start.1
  366.6 4.5 collective-permute-start.6
  370.7 3.9 collective-permute-start.2
  371.1 5.9 collective-permute-start.7
  374.6 5.4 collective-permute-start.3
  377.0 309.6 %collective-permute-start.8 = (f32[8960]{0:T(1024)S(1)}, f32[8960]{0:T(1024)S(1)}, u32[]{:S(2)}, u32[]{:S(2)}) collective-permute-start(f32[8960]{0:T(1024)S(1)} %add.221), channel_id=1, source_target_pairs={{0,16},{2,18},{4,20},{6,22},{8,24},{10,26},{12,28},{14,30},{16,0},... | collective-permute-start | bytes 107528 | tf_op jit(solution)/shard_map/ppermute | solution.py:609
  380.0 306.7 %collective-permute-start.4 = (f32[7680]{0:T(1024)S(1)}, f32[7680]{0:T(1024)S(1)}, u32[]{:S(2)}, u32[]{:S(2)}) collective-permute-start(f32[7680]{0:T(1024)S(1)} %add.211), channel_id=1, source_target_pairs={{0,1},{1,0},{2,3},{3,2},{4,5},{5,4},{6,7},{7,6},{8,9},{9,8},{10,11... | collective-permute-start | bytes 92168 | tf_op jit(solution)/shard_map/ppermute | solution.py:614
  659.1 7.1 %copy-start.17 = (bf16[640,1280]{1,0:T(8,128)(2,1)S(1)}, bf16[640,1280]{1,0:T(8,128)(2,1)}, u32[]{:S(2)}) copy-start(bf16[640,1280]{1,0:T(8,128)(2,1)} %get-tuple-element.78) | copy-start | bytes 4915204
  686.6 4.0 collective-permute-start.9
  (11 other events, 30.4 us)

commit v3 on v2

--- a/solution.py
+++ b/solution.py
@@ -34,75 +34,61 @@
     quarter = head_size // 4
     counter = jnp.arange(quarter, dtype=jnp.float32)
     inverse = jnp.power(jnp.float32(10000.0), -2.0 * counter / (head_size // 2))
-    row_angle = positions[0].astype(jnp.float32)[:, None] * inverse[None, :]
-    col_angle = positions[1].astype(jnp.float32)[:, None] * inverse[None, :]
-    angle = jnp.concatenate([row_angle, col_angle], axis=1)
-    angle = jnp.concatenate([angle, angle], axis=1)
+    row_angle = inverse[:, None] * positions[0].astype(jnp.float32)[None, :]
+    col_angle = inverse[:, None] * positions[1].astype(jnp.float32)[None, :]
+    angle = jnp.concatenate([row_angle, col_angle], axis=0)
+    angle = jnp.concatenate([angle, angle], axis=0)
     return (jnp.cos(angle), jnp.sin(angle))
 
 
 def apply_rotary(matrix, cosine, sine):
-    half_size = matrix.shape[-1] // 2
-    turned = jnp.concatenate([-matrix[..., half_size:], matrix[..., :half_size]], axis=-1)
-    return matrix * cosine[:, None, :] + turned * sine[:, None, :]
-
-
-def rotary_back(grad_rows, cosine, sine):
-    half_size = grad_rows.shape[-1] // 2
-    sined = grad_rows * sine[:, None, :]
-    turned = jnp.concatenate([sined[..., half_size:], -sined[..., :half_size]], axis=-1)
-    return grad_rows * cosine[:, None, :] + turned
+    half_size = matrix.shape[-2] // 2
+    turned = jnp.concatenate([-matrix[..., half_size:, :], matrix[..., :half_size, :]], axis=-2)
+    return matrix * cosine + turned * sine
+
+
+def rotary_back(grad, cosine, sine):
+    half_size = grad.shape[-2] // 2
+    sined = grad * sine
+    turned = jnp.concatenate([sined[..., half_size:, :], -sined[..., :half_size, :]], axis=-2)
+    return grad * cosine + turned
+
+
+def contract(left, right, left_dim, right_dim):
+    return lax.dot_general(
+        left, right, (((left_dim,), (right_dim,)), ((), ())), preferred_element_type=jnp.float32
+    )
 
 
 def masked_scores(queries, keys_rot, ident, score_scale):
     scores = (
-        jnp.einsum("qhd,khd->hqk", queries, keys_rot, preferred_element_type=jnp.float32)
+        jnp.einsum("hdk,hdq->hkq", keys_rot, queries, preferred_element_type=jnp.float32)
         * score_scale
     )
     same_pic = ident[:, None] == ident[None, :]
     return jnp.where(same_pic[None], scores, -1000000000.0)
 
 
-def attend(pieces, score_scale):
-    queries, keys_rot, values_all, ident = pieces
+def attend(queries, keys_rot, values_all, ident, score_scale):
     scores = masked_scores(queries, keys_rot, ident, score_scale)
-    top_score = jnp.max(scores, axis=2, keepdims=True)
+    top_score = jnp.max(scores, axis=1, keepdims=True)
     exp_scores = jnp.exp(scores - top_score)
-    total = jnp.sum(exp_scores, axis=2, keepdims=True)
+    total = jnp.sum(exp_scores, axis=1, keepdims=True)
     probs = (exp_scores / total).astype(jnp.bfloat16)
-    attended = jnp.einsum("hqk,khd->qhd", probs, values_all, preferred_element_type=jnp.float32)
-    return (attended, (top_score + jnp.log(total))[:, :, 0])
-
-
-def attend_back(pieces, score_scale):
-    queries, keys_rot, values_all, ident, grad_heads, log_total = pieces
-    scores = masked_scores(queries, keys_rot, ident, score_scale)
-    probs = jnp.exp(scores - log_total[:, :, None])
-    grad_probs = jnp.einsum(
-        "qhd,khd->hqk", grad_heads, values_all, preferred_element_type=jnp.float32
-    )
-    inner = jnp.sum(probs * grad_probs, axis=2, keepdims=True)
+    attended = jnp.einsum("hdk,hkq->hdq", values_all, probs, preferred_element_type=jnp.float32)
+    return (attended, (top_score + jnp.log(total))[:, 0, :])
+
+
+def head_back(query, key, value, grad_head, same_pic, log_total, score_scale):
+    scores = jnp.where(same_pic, contract(key, query, 0, 0) * score_scale, -1000000000.0)
+    probs = jnp.exp(scores - log_total)
+    grad_probs = contract(value, grad_head, 0, 0)
+    inner = jnp.sum(probs * grad_probs, axis=0, keepdims=True)
     grad_scores = (probs * (grad_probs - inner)).astype(jnp.bfloat16)
-    grad_query = (
-        jnp.einsum("hqk,khd->qhd", grad_scores, keys_rot, preferred_element_type=jnp.float32)
-        * score_scale
-    )
-    grad_key = (
-        jnp.einsum("hqk,qhd->khd", grad_scores, queries, preferred_element_type=jnp.float32)
-        * score_scale
-    )
-    grad_value = jnp.einsum(
-        "hqk,qhd->khd", probs.astype(jnp.bfloat16), grad_heads, preferred_element_type=jnp.float32
-    )
+    grad_query = contract(key, grad_scores, 1, 0) * score_scale
+    grad_key = contract(query, grad_scores, 1, 1) * score_scale
+    grad_value = contract(grad_head, probs.astype(jnp.bfloat16), 1, 1)
     return (grad_query, grad_key, grad_value)
-
-
-def row_product(left, right):
-    return jnp.einsum("ti,tj->ij", left, right, preferred_element_type=jnp.float32)
-
-
-def back_product(grad_rows, weight_full):
-    return jnp.einsum("tj,ij->ti", grad_rows, weight_full, preferred_element_type=jnp.float32)
 
 
 MESH = pl.DeviceIdType.MESH
@@ -588,6 +574,372 @@
         name="reduce_products",
     )(*products)
     return results[:-1]
+
+
+class Cuts:
+    def __init__(self, sizes, n_shard):
+        self.shard_rows = [left // n_shard for left, _ in sizes]
+        self.rows = min(self.shard_rows) // 2
+        self.wide = min(right for _, right in sizes)
+        self.down = [rows // self.rows for rows in self.shard_rows]
+        self.across = [right // self.wide for _, right in sizes]
+        self.first = [0]
+        for down, across in zip(self.down, self.across):
+            self.first.append(self.first[-1] + down * across)
+        self.count = self.first[-1]
+
+    def weight_of(self, k, act):
+        for w, down in enumerate(self.down):
+
+            @pl.when((k >= self.first[w]) & (k < self.first[w + 1]))
+            def _():
+                inside = k - self.first[w]
+                act(w, inside % down, inside // down)
+
+    def whole(self, chunks, w):
+        first, down, rows, wide = self.first[w], self.down[w], self.rows, self.wide
+
+        def widen(part, dst):
+            dst[...] = part[0].astype(jnp.float32)
+
+        return pl.pallas_call(
+            widen,
+            grid=(down, self.across[w]),
+            in_specs=[pl.BlockSpec((1, rows, wide), lambda i, j: (first + j * down + i, 0, 0))],
+            out_specs=pl.BlockSpec((rows, wide), lambda i, j: (i, j)),
+            out_shape=jax.ShapeDtypeStruct(
+                (self.shard_rows[w], self.across[w] * wide), jnp.float32
+            ),
+            compiler_params=pltpu.CompilerParams(vmem_limit_bytes=24 << 20),
+            name="widen",
+        )(chunks)
+
+
+def backward_kernel(n_rep, cuts, n_heads, slots, score_scale, *refs):
+    (
+        left_0, left_1, left_2, left_3, right_0, right_1, right_2, qkv, w_qkv,
+        grad_heads, log_total, pic_key, pic_query, cosine, sine,
+        out, grad_qkv, grad_first, lent_left, lent_right,
+        op_left, op_right, held, got_y, got_x, got_in, got_mid, total, swap, w_block,
+        load_l, load_r, put, qkv_sem, block_sem,
+        l0_sem, l1_sem, r_sem, y_sem, x_sem, in_sem, mid_sem, back_sem, ax_sem, ac_sem, af_sem,
+    ) = refs
+    lefts = [left_0, left_1, left_2, left_3]
+    rights = [right_0, right_1, right_2, grad_qkv]
+    l_sems = [l0_sem, l1_sem]
+    at = Place(n_rep)
+    half = at.half
+    count, rows, wide = cuts.count, cuts.rows, cuts.wide
+    block, width = rows // 2, wide // 2
+    mine = at.y
+    head = qkv.shape[0] // (3 * n_heads)
+    model = n_heads * head
+
+    def left_rows(w, row, owner):
+        start = owner * cuts.shard_rows[w] + row * rows
+        return lefts[w].at[pl.ds(pl.multiple_of(start, 16), rows), :]
+
+    def right_rows(w, col, c):
+        start = col * wide + c * width
+        return rights[w].at[pl.ds(pl.multiple_of(start, 16), width), :]
+
+    def left_push(k, owner, src):
+        return remote(src, lent_left.at[k, owner], l_sems[owner], k, at.to_core)
+
+    def right_push(k, src):
+        return remote(src, lent_right.at[k], r_sem, k, at.to_core)
+
+    def left_load(k, whose, owner, src):
+        slot = k % 2
+        return pltpu.make_async_copy(
+            src, op_left.at[slot, whose, owner], load_l.at[whose, owner, k]
+        )
+
+    def right_load(k, whose, src):
+        return pltpu.make_async_copy(src, op_right.at[k % 2, whose], load_r.at[whose, k])
+
+    def rows_of(x):
+        return pl.ds(pl.multiple_of(x * block, 16), block)
+
+    def mine_of(k, x):
+        return held.at[k % slots, mine, rows_of(x)]
+
+    def y_send(k):
+        return remote(held.at[k % slots, 1 - mine], got_y.at[k], y_sem, k, at.to_y)
+
+    def x_send(k):
+        return remote(mine_of(k, 1 - at.x), got_x.at[k], x_sem, k, at.to_x)
+
+    def in_send(k):
+        return remote(mine_of(k, at.x), got_in.at[k], in_sem, k, at.to_in)
+
+    def mid_send(k):
+        return remote(mine_of(k, at.x), got_mid.at[k], mid_sem, k, at.to_in)
+
+    def back_send(k):
+        return remote(total.at[k], total.at[k], back_sem, k, at.to_out)
+
+    def out_of(k, c, x):
+        cols = pl.ds(pl.multiple_of(c * width, 128), width)
+        return out.at[k, rows_of(x), cols]
+
+    def ax_send(k, x):
+        return remote(total.at[k], out_of(k, at.c, x), ax_sem, k, at.to_x)
+
+    def ac_send(k, c):
+        return remote(total.at[k], out_of(k, c, at.x), ac_sem, k, at.to_core)
+
+    def af_send(k, c):
+        view = out_of(k, c, 1 - at.x)
+        return remote(view, view, af_sem, k, at.to_core)
+
+    def own_put(k):
+        return pltpu.make_async_copy(total.at[k], out_of(k, at.c, at.x), put.at[k])
+
+    def push(k):
+        def act(w, row, col):
+            for owner in range(2):
+                left_push(k, owner, left_rows(w, row, owner)).start()
+            right_push(k, right_rows(w, col, 1 - at.c)).start()
+
+        cuts.weight_of(k, act)
+
+    def load(k):
+        def act(w, row, col):
+            for owner in range(2):
+                left_load(k, 0, owner, left_rows(w, row, owner)).start()
+            right_load(k, 0, right_rows(w, col, at.c)).start()
+
+        cuts.weight_of(k, act)
+        for owner in range(2):
+            left_push(k, owner, lent_left.at[k, owner]).wait_recv()
+            left_load(k, 1, owner, lent_left.at[k, owner]).start()
+        right_push(k, lent_right.at[k]).wait_recv()
+        right_load(k, 1, lent_right.at[k]).start()
+
+    def product(k):
+        slot = k % 2
+        for whose in range(2):
+            for owner in range(2):
+                left_load(k, whose, owner, lent_left.at[k, owner]).wait()
+            right_load(k, whose, lent_right.at[k]).wait()
+        for owner in range(2):
+            left_push(k, owner, lent_left.at[k, owner]).wait_send()
+        right_push(k, lent_right.at[k]).wait_send()
+        for owner in (1 - mine, mine):
+            result = contract(op_left[slot, 0, owner], op_right[slot, 0], 1, 1)
+            result += contract(op_left[slot, 1, owner], op_right[slot, 1], 1, 1)
+            held[k % slots, owner] = result.astype(jnp.bfloat16)
+            if owner is not mine:
+                y_send(k).start()
+
+    def start_x(k):
+        y_send(k).wait_recv()
+        other = mine_of(k, 1 - at.x)
+        add_into(other, other, got_y.at[k, rows_of(1 - at.x)])
+        x_send(k).start()
+        own = mine_of(k, at.x)
+        add_into(own, own, got_y.at[k, rows_of(at.x)])
+        y_send(k).wait_send()
+
+    def inner_send(k, depth):
+        return mid_send(k) if depth == half - 1 else in_send(k)
+
+    def start_z(k):
+        x_send(k).wait_recv()
+        own = mine_of(k, at.x)
+        add_into(own, own, got_x.at[k])
+
+        @at.at_depth(0)
+        def _():
+            inner_send(k, 0).start()
+
+        x_send(k).wait_send()
+
+    def pass_in(depth):
+        def stage(k):
+            @at.at_depth(depth)
+            def _():
+                in_send(k).wait_recv()
+                own = mine_of(k, at.x)
+                add_into(own, own, got_in.at[k])
+                inner_send(k, depth).start()
+
+        return stage
+
+    def spread(k, depth):
+        if depth > 0:
+            back_send(k).start()
+        ax_send(k, at.x).start()
+        ac_send(k, at.c).start()
+        own_put(k).start()
+
+    def middle(k):
+        @at.at_depth(half - 1)
+        def _():
+            mid_send(k).wait_recv()
+            add_into(total.at[k], mine_of(k, at.x), got_mid.at[k])
+            spread(k, half - 1)
+
+    def pass_out(depth):
+        def stage(k):
+            @at.at_depth(depth)
+            def _():
+                back_send(k).wait_recv()
+                spread(k, depth)
+
+        return stage
+
+    def sent(k):
+        for depth in range(half):
+
+            @at.at_depth(depth)
+            def _():
+                inner_send(k, depth).wait_send()
+
+    def forward(k):
+        ax_send(k, 1 - at.x).wait_recv()
+        af_send(k, at.c).start()
+
+    def finish(k):
+        @pl.when(at.depth > 0)
+        def _():
+            back_send(k).wait_send()
+
+        ax_send(k, at.x).wait_send()
+        ac_send(k, at.c).wait_send()
+        af_send(k, at.c).wait_send()
+        own_put(k).wait()
+        ac_send(k, 1 - at.c).wait_recv()
+        af_send(k, 1 - at.c).wait_recv()
+
+    def head_step(h):
+        def part(i):
+            return pl.ds(pl.multiple_of(i * model + h * head, 16), head)
+
+        query, key, value = swap[part(0), :], swap[part(1), :], swap[part(2), :]
+        grads = head_back(
+            query,
+            key,
+            value,
+            grad_heads[part(0), :],
+            pic_key[...] == pic_query[...],
+            log_total[pl.ds(h, 1), :],
+            score_scale,
+        )
+        grad_query, grad_key, grad_value = grads
+        turn_c, turn_s = cosine[...], sine[...]
+        swap[part(0), :] = rotary_back(grad_query, turn_c, turn_s).astype(jnp.bfloat16)
+        swap[part(1), :] = rotary_back(grad_key, turn_c, turn_s).astype(jnp.bfloat16)
+        swap[part(2), :] = grad_value.astype(jnp.bfloat16)
+
+    def block_load(j):
+        cols = pl.ds(pl.multiple_of(j * width, 128), width)
+        return pltpu.make_async_copy(w_qkv.at[:, cols], w_block.at[j % 2], block_sem.at[j])
+
+    def first_step(j):
+        block_load(j).wait()
+        inside = pl.ds(pl.multiple_of(j * width, 16), width)
+        step = 256
+
+        @pl.loop(0, model // step)
+        def _(i):
+            spot = pl.ds(pl.multiple_of(i * step, 16), step)
+            grad_first[spot, :] += contract(w_block[j % 2, spot, :], swap[inside, :], 1, 0)
+
+    n_blocks = qkv.shape[0] // width
+    take_qkv = pltpu.make_async_copy(qkv, swap, qkv_sem.at[0])
+    give_qkv = pltpu.make_async_copy(swap, grad_qkv, qkv_sem.at[1])
+    take_qkv.start()
+    at.meet(True)
+    grad_first[...] = jnp.zeros_like(grad_first)
+    take_qkv.wait()
+    stages = [(0, push), (1, load), (2, product), (4, start_x), (6, start_z)]
+    stages += [(6 + depth, pass_in(depth)) for depth in range(1, half)]
+    stages += [(6 + half, middle)]
+    stages += [(6 + half + (half - 1 - depth), pass_out(depth)) for depth in range(half - 1)]
+    stages += [(slots + 2, sent), (7 + 2 * half, forward), (9 + 2 * half, finish)]
+    stages.sort(key=lambda item: -item[0])
+    per_tick = -(-n_heads // (cuts.first[3] - 2))
+    done = -(-n_heads // per_tick)
+
+    def tick_body(tick, carry):
+        for offset, stage in stages:
+
+            @pl.when((tick >= offset) & (tick < count + offset))
+            def _():
+                stage(tick - offset)
+
+        @pl.when(tick < done)
+        def _():
+            @pl.loop(0, per_tick)
+            def _(i):
+                head_step(tick * per_tick + i)
+
+        @pl.when(tick == done)
+        def _():
+            give_qkv.start()
+            give_qkv.wait()
+
+        @pl.when((tick > done) & (tick <= done + n_blocks))
+        def _():
+            first_step(tick - done - 1)
+
+        @pl.when((tick >= done) & (tick < done + n_blocks))
+        def _():
+            block_load(tick - done).start()
+
+        return carry
+
+    lax.fori_loop(0, count + 9 + 2 * half, tick_body, 0)
+
+
+def reduce_backward(lefts, rights, qkv, w_qkv, small, n_rep, n_heads, score_scale):
+    tokens = qkv.shape[1]
+    sizes = [(left.shape[0], right.shape[0]) for left, right in zip(lefts, rights + [qkv])]
+    cuts = Cuts(sizes, 2)
+    half = n_rep // 8
+    slots = 3 + 2 * half
+    count, rows, wide = cuts.count, cuts.rows, cuts.wide
+    block, width = rows // 2, wide // 2
+    low, dma = jnp.bfloat16, pltpu.SemaphoreType.DMA
+    anywhere, local = pl.BlockSpec(memory_space=pl.ANY), pl.BlockSpec(memory_space=pltpu.VMEM)
+    model = w_qkv.shape[0]
+    chunks, grad_qkv, grad_first, _, _ = pl.pallas_call(
+        partial(backward_kernel, n_rep, cuts, n_heads, slots, score_scale),
+        out_shape=[
+            jax.ShapeDtypeStruct((count, rows, wide), low),
+            jax.ShapeDtypeStruct(qkv.shape, low),
+            jax.ShapeDtypeStruct((model, tokens), jnp.float32),
+            jax.ShapeDtypeStruct((count, 2, rows, tokens), low),
+            jax.ShapeDtypeStruct((count, width, tokens), low),
+        ],
+        in_specs=[anywhere] * 9 + [local] * len(small),
+        out_specs=[anywhere, anywhere, local, anywhere, anywhere],
+        scratch_shapes=[
+            pltpu.VMEM((2, 2, 2, rows, tokens), low),
+            pltpu.VMEM((2, 2, width, tokens), low),
+            pltpu.VMEM((slots, 2, rows, width), low),
+            pltpu.VMEM((count, rows, width), low),
+            pltpu.VMEM((count, block, width), low),
+            pltpu.VMEM((count, block, width), low),
+            pltpu.VMEM((count, block, width), low),
+            pltpu.VMEM((count, block, width), low),
+            pltpu.VMEM(qkv.shape, low),
+            pltpu.VMEM((2, model, width), low),
+            dma((2, 2, count)),
+            dma((2, count)),
+            dma((count,)),
+            dma((2,)),
+            dma((qkv.shape[0] // width,)),
+        ]
+        + [dma((2, count))] * 11,
+        compiler_params=pltpu.CompilerParams(
+            collective_id=1, has_side_effects=True, vmem_limit_bytes=63 << 20
+        ),
+        name="reduce_backward",
+    )(*lefts, *rights, qkv, w_qkv, *small)
+    return [cuts.whole(chunks, w) for w in range(len(sizes))], grad_qkv, grad_first
 
 
 class Links:
@@ -647,8 +999,9 @@
     pic_ends = jnp.cumsum(lengths[:, :-1], axis=1)
     slot_index = jnp.arange(length, dtype=jnp.int32)
     idents = jnp.sum((slot_index[None, :, None] >= pic_ends[:, None, :]).astype(jnp.int32), axis=2)
+    pack_index = jnp.arange(pack_count, dtype=jnp.int32)
+    idents = (idents + pack_index[:, None] * lengths.shape[1]).reshape(-1)
     cosine, sine = rotary_tables(positions, head_size)
-    pack_shape = (pack_count, length, head_count, head_size)
 
     small = [ln1_gain, ln1_bias, qkv_bias, proj_bias, ln2_gain, ln2_bias, fc1_bias, fc2_bias]
     sizes = [item.shape[0] for item in small]
@@ -671,39 +1024,31 @@
     first_normalized = (first_centered_standard * first_norm_gain + first_norm_bias).astype(
         jnp.bfloat16
     )
-    qkv_rows = jnp.dot(first_normalized, w_qkv, preferred_element_type=jnp.float32) + b_qkv
-    qkv_rows = qkv_rows.reshape(row_count, 3, head_count, head_size)
-    queries = apply_rotary(qkv_rows[:, 0], cosine, sine).astype(jnp.bfloat16).reshape(pack_shape)
-    keys_rot = apply_rotary(qkv_rows[:, 1], cosine, sine).astype(jnp.bfloat16).reshape(pack_shape)
-    values_all = qkv_rows[:, 2].astype(jnp.bfloat16).reshape(pack_shape)
-    attended, log_total = lax.map(
-        partial(attend, score_scale=score_scale), (queries, keys_rot, values_all, idents)
-    )
-    heads_out = attended.reshape(row_count, model_width).astype(jnp.bfloat16)
-    hidden_rows = (
-        input_rows + jnp.dot(heads_out, w_proj, preferred_element_type=jnp.float32) + b_proj
-    )
+    qkv_rows = contract(w_qkv, first_normalized, 0, 1) + b_qkv[:, None]
+    qkv_rows = qkv_rows.reshape(3, head_count, head_size, row_count)
+    queries = apply_rotary(qkv_rows[0], cosine, sine).astype(jnp.bfloat16)
+    keys_rot = apply_rotary(qkv_rows[1], cosine, sine).astype(jnp.bfloat16)
+    values_all = qkv_rows[2].astype(jnp.bfloat16)
+    attended, log_total = attend(queries, keys_rot, values_all, idents, score_scale)
+    heads_out = attended.reshape(model_width, row_count).astype(jnp.bfloat16)
+    hidden_rows = input_rows + contract(heads_out, w_proj, 0, 0) + b_proj
     second_centered_standard, second_inverse_spread = apply_layer_norm(hidden_rows)
     second_normalized = (second_centered_standard * second_norm_gain + second_norm_bias).astype(
         jnp.bfloat16
     )
-    up_pre = jnp.dot(second_normalized, w_up, preferred_element_type=jnp.float32) + b_up
+    up_pre = contract(w_up, second_normalized, 0, 1) + b_up[:, None]
     sigmoid_up = 1.0 / (1.0 + jnp.exp(-quick_slope * up_pre))
     activation = (up_pre * sigmoid_up).astype(jnp.bfloat16)
 
-    d_w_down = row_product(activation, cotangent).astype(jnp.bfloat16)
-    out_full = (
-        hidden_rows + jnp.dot(activation, w_down, preferred_element_type=jnp.float32) + b_down
-    )
+    out_full = hidden_rows + contract(activation, w_down, 0, 0) + b_down
     layer_out = out_full.astype(jnp.bfloat16)
     grad_out = cotangent.astype(jnp.float32)
     d_b_down = jnp.sum(grad_out, axis=0)
-    grad_act = back_product(cotangent, w_down)
+    grad_act = contract(w_down, cotangent, 1, 1)
     slope_up = sigmoid_up + quick_slope * up_pre * sigmoid_up * (1.0 - sigmoid_up)
     grad_pre = (grad_act * slope_up).astype(jnp.bfloat16)
-    d_w_up = row_product(second_normalized, grad_pre).astype(jnp.bfloat16)
-    d_b_up = jnp.sum(grad_pre.astype(jnp.float32), axis=0)
-    second_normalized_gradient = back_product(grad_pre, w_up)
+    d_b_up = jnp.sum(grad_pre.astype(jnp.float32), axis=1)
+    second_normalized_gradient = contract(grad_pre, w_up, 0, 1)
     second_gain_gradient = jnp.sum(second_normalized_gradient * second_centered_standard, axis=0)
     d_bias_two = jnp.sum(second_normalized_gradient, axis=0)
     grad_hidden = grad_out + norm_gradient_step(
@@ -713,24 +1058,44 @@
         second_norm_gain,
     )
     grad_branch = grad_hidden.astype(jnp.bfloat16)
-    d_w_proj = row_product(heads_out, grad_branch).astype(jnp.bfloat16)
     d_b_proj = jnp.sum(grad_branch.astype(jnp.float32), axis=0)
-    grad_heads = back_product(grad_branch, w_proj).astype(jnp.bfloat16).reshape(pack_shape)
-    grad_query, grad_key, grad_value = lax.map(
-        partial(attend_back, score_scale=score_scale),
-        (queries, keys_rot, values_all, idents, grad_heads, log_total),
-    )
-    rows_shape = (row_count, head_count, head_size)
-    grad_query = rotary_back(grad_query.reshape(rows_shape), cosine, sine)
-    grad_key = rotary_back(grad_key.reshape(rows_shape), cosine, sine)
-    grad_qkv = (
-        jnp.stack([grad_query, grad_key, grad_value.reshape(rows_shape)], axis=1)
-        .reshape(row_count, 3 * model_width)
-        .astype(jnp.bfloat16)
-    )
-    d_w_qkv = row_product(first_normalized, grad_qkv).astype(jnp.bfloat16)
-    d_b_qkv = jnp.sum(grad_qkv.astype(jnp.float32), axis=0)
-    first_normalized_gradient = back_product(grad_qkv, w_qkv)
+    grad_heads = contract(w_proj, grad_branch, 1, 1).astype(jnp.bfloat16)
+    lefts = [activation, second_normalized.T, heads_out, first_normalized.T]
+    rights = [cotangent.T, grad_pre, grad_branch.T]
+    qkv_shape = (3 * model_width, row_count)
+    if n_shard == 2:
+        qkv = jnp.stack([queries, keys_rot, values_all]).reshape(qkv_shape)
+        small_args = [
+            grad_heads, log_total, idents[:, None], idents[None, :], cosine, sine,
+        ]
+        products, grad_qkv, first_gradient = reduce_backward(
+            lefts, rights, qkv, w_qkv, small_args, n_rep, head_count, score_scale
+        )
+    else:
+        back = partial(head_back, score_scale=score_scale)
+        grad_query, grad_key, grad_value = jax.vmap(back, in_axes=(0, 0, 0, 0, None, 0))(
+            queries,
+            keys_rot,
+            values_all,
+            grad_heads.reshape(head_count, head_size, row_count),
+            idents[:, None] == idents[None, :],
+            log_total[:, None, :],
+        )
+        grad_query = rotary_back(grad_query, cosine, sine)
+        grad_key = rotary_back(grad_key, cosine, sine)
+        grad_qkv = jnp.stack([grad_query, grad_key, grad_value]).reshape(qkv_shape)
+        grad_qkv = grad_qkv.astype(jnp.bfloat16)
+        first_gradient = contract(w_qkv, grad_qkv, 1, 0)
+        products = [
+            contract(left, right, 1, 1).astype(jnp.bfloat16)
+            for left, right in zip(lefts, rights + [grad_qkv])
+        ]
+        products = [
+            item.astype(jnp.float32) for item in reduce_products(products, n_rep, n_shard)
+        ]
+    d_w_down, d_w_up, d_w_proj, d_w_qkv = products
+    d_b_qkv = jnp.sum(grad_qkv.astype(jnp.float32), axis=1)
+    first_normalized_gradient = first_gradient.T
     first_gain_gradient = jnp.sum(first_normalized_gradient * first_centered_standard, axis=0)
     d_bias_one = jnp.sum(first_normalized_gradient, axis=0)
     d_patches = grad_hidden + norm_gradient_step(
@@ -739,11 +1104,6 @@
         first_inverse_spread,
         first_norm_gain,
     )
-
-    d_w_down, d_w_up, d_w_proj, d_w_qkv = [
-        item.astype(jnp.float32)
-        for item in reduce_products([d_w_down, d_w_up, d_w_proj, d_w_qkv], n_rep, n_shard)
-    ]
 
     def own_parts(vectors):
         lens = [item.shape[0] for item in vectors]

time: 702 us -> 603 us (0.86)
  matrix products: 171 us -> 92.6 us
  other arithmetic: 66 us -> 42.5 us
    dot_general x18 -> x9, matrix products: 171 us -> 92.6 us  [the longest x7 74.3 us: contract(): lax.dot_general(left, right, (((left_dim,), (right_dim,)), ((), ())), pre...]
    convert_element_type x7 -> x2, other arithmetic: 42.4 us -> 4.81 us  [the longest x1 4.81 us: per_device(): queries = apply_rotary(qkv_rows[0], cosine, sine).astype(jnp.bfloat16)]
    unnamed x75 -> x65, local copies, waits for them, and re-layouts: 7.87 us -> 21.1 us
    reduce_sum x2 -> x5, other arithmetic: 9.46 us -> 19.3 us  [the longest x1 9.2 us: attend(): total = jnp.sum(exp_scores, axis=1, keepdims=True)]
    add x1 -> x0, local copies, waits for them, and re-layouts: 9.06 us -> none  [per_device(): jnp.dot(first_normalized, w_qkv, preferred_element_type=jnp.float32) + b_qkv]
    pallas_call x1 -> x5, Pallas kernels: 275 us -> 276 us  [the longest x1 258 us: reduce_backward(): pl.pallas_call(partial(backward_kernel, n_rep, cuts, n_heads, slots, scor...]
  transfers between devices with their start and end apart: 10 -> 10, of which waited for: 4 -> 6; matrix products, arithmetic and copies ran while one was open for 12% -> 7% of each run, Pallas kernels for 40% -> 46%
where the time goes in v3:
time: 603 us; the launch traced here: 598 us
  Pallas kernels  406 us (67%)
  matrix products  92.6 us (15%)
  other arithmetic  42.5 us (7%)
  local copies, waits for them, and re-layouts  33.1 us (5%)
  waiting for transfers between devices  10.2 us (2%)
  starting transfers between devices  7.36 us (1%)
    pallas_call x1, Pallas kernels, reduce_backward(): pl.pallas_call(partial(backward_kernel, n_rep, cuts, n_heads, slots, scor...  258 us
    pallas_call x1, Pallas kernels, gather_weights(): pl.pallas_call(kernel, out_shape=[jax.ShapeDtypeStruct(shape, jnp.bfloat1...  130 us
    dot_general x7, matrix products, contract(): lax.dot_general(left, right, (((left_dim,), (right_dim,)), ((), ())), pre...  74.3 us
    unnamed x65, local copies, waits for them, and re-layouts  21.1 us
    pallas_call x4, Pallas kernels, whole(): pl.pallas_call(widen, grid=(down, self.across[w]), in_specs=[pl.BlockSpec...  17.4 us
  transfers between devices with their start and end apart: 10, of which 6 were waited for; matrix products, arithmetic and copies ran while one was open for 7% of the time, Pallas kernels for 46%

profile of v3, /device:TPU:0, one launch (start us, length us, event | category | flops | bytes accessed | tf_op | source)
XLA Modules:
  0.0 598.5 jit_solution(10224633137020771197)
XLA Ops:
  7.5 5.5 all-gather.1
  16.1 130.1 %gather_weights.1 = (bf16[1280,3840]{1,0:T(8,128)(2,1)}, bf16[1280,1280]{1,0:T(8,128)(2,1)}, bf16[1280,5120]{1,0:T(8,128)(2,1)}, bf16[5120,1280]{1,0:T(8,128)(2,1)}) custom-call(bf16[640,3840]{1,0:T(8,128)(2,1)} %refs_0_.1, bf16[640,1280]{1,0:T(8,128)(2,1)} %refs_1_.1, bf16[640,5120]{1,0:T(8,128)(2,1)} %refs_2_.1, bf16[2560,1280]{1,0:T(8,128)(2,1)} %refs_3_.1), custom_call_target="tpu_custom_call" | custom-call | tf_op jit(solution)/shard_map/gather_weights/pallas_call | solution.py:326
  146.3 8.9 %convolution_add_fusion = f32[3840,512]{1,0:T(8,128)S(1)} fusion(bf16[1280,3840]{1,0:T(8,128)(2,1)} %get-tuple-element.21.refs_8_, f32[3840]{0:T(1024)S(1)} %reshape.455, bf16[512,1280]{0,1:T(8,128)(2,1)S(1)} %copy.65, f32[1280]{0:T(1024)S(1)} %reshape.454, f32[1280]{0:T(1024)S(1)} %reshape.453, f32[512]{0:T(512)S(1)} %add_rsqrt_fusion.1, ...), kind=kOutput, calls=%fused_computation.11 | convolution fusion | flops 5039063040 | bytes 19035136 | tf_op jit(solution)/shard_map/dot_general | solution.py:58
  156.4 2.9 fusion.48
  162.3 6.1 %fusion.42 = (f32[1,16,40,512]{3,2,1,0:T(8,128)}, f32[1,16,40,512]{3,2,1,0:T(8,128)}, f32[16,40,512]{2,1,0:T(8,128)S(1)}, f32[16,40,512]{2,1,0:T(8,128)S(1)}, f3...) fusion(f32[16,80,512]{2,1,0:T(8,128)} %bitcast.53, ...), kind=kLoop, calls=%fused_computation.103 | loop fusion | flops 655360 | bytes 15728640 | tf_op jit(solution)/shard_map/concatenate | solution.py:46
  168.3 9.1 %fusion = (f32[16,512]{1,0:T(8,128)S(1)}, f32[16,512,512]{2,1,0:T(8,128)}) fusion(pred[512,512]{1,0:T(8,128)(4,1)S(1)} %broadcast_compare_fusion, f32[16,40,512]{2,1,0:T(8,128)} %get-tuple-element.135, f32[16,40,512]{2,1,0:T(8,128)S(1)} %get-tuple-element.134, f32[16,80,512]{2,1,0:T(8,128)S(1)} %bitcast.58, f32[80,512]{1,0:T(8,128)S(1)} %get-tuple-element.107.refs_14_, ...), kind=kOutput, calls=%fused_computation.3 | convolution fusion | flops 690216960 | bytes 27885568 | tf_op jit(solution)/shard_map/hdk,hdq->hkq/dot_general | solution.py:65
  177.4 9.2 %fusion.1 = f32[16,512]{1,0:T(8,128)S(1)} fusion(f32[16,512,512]{2,1,0:T(8,128)} %get-tuple-element.125, f32[16,512]{1,0:T(8,128)S(1)} %get-tuple-element.124, pred[512,512]{1,0:T(8,128)(4,1)S(1)} %broadcast_compare_fusion), kind=kLoop, calls=%fused_computation.4 | loop fusion | flops 16769024 | bytes 17104896 | tf_op jit(solution)/shard_map/reduce_sum | solution.py:76
  186.7 9.1 %fusion.29 = bf16[16,80,512]{2,1,0:T(8,128)(2,1)S(1)} fusion(bf16[16,80,512]{2,1,0:T(8,128)(2,1)} %bitcast.61, f32[16,512,512]{2,1,0:T(8,128)} %get-tuple-element.125, f32[16,512]{1,0:T(8,128)S(1)} %fusion.1, f32[16,512]{1,0:T(8,128)S(1)} %get-tuple-element.124, pred[512,512]{1,0:T(8,128)(4,1)S(1)} %broadcast_compare_fusion), kind=kOutput, calls=%fused_computation.59 | convolution fusion | flops 692715520 | bytes 19726336 | tf_op jit(solution)/shard_map/hdk,hkq->hdq/dot_general | solution.py:78
  195.8 2.1 fusion.51
  198.3 15.9 %multiply_convert_fusion.1 = (bf16[5120,512]{1,0:T(8,128)(2,1)}, f32[5120,512]{1,0:T(8,128)}) fusion(f32[5120]{0:T(1024)S(1)} %reshape.459, bf16[1280,5120]{1,0:T(8,128)(2,1)} %get-tuple-element.23, f32[512,1280]{0,1:T(8,128)S(1)} %get-tuple-element.127, f32[1280]{0:T(1024)S(1)} %reshape.458, f32[1280]{0:T(1024)S(1)} %reshape.457, ...), kind=kOutput, calls=%fused_computation.7 | convolution fusion | flops 6729891840 | bytes 31492096 | tf_op jit(solution)/shard_map/dot_general | solution.py:58
  214.1 17.6 %convert_reduce_fusion = (f32[5120]{0:T(1024)S(1)}, bf16[5120,512]{1,0:T(8,128)(2,1)}) fusion(f32[5120,512]{1,0:T(8,128)} %get-tuple-element.129, f32[5120]{0:T(1024)S(1)} %reshape.459, bf16[5120,1280]{1,0:T(8,128)(2,1)} %get-tuple-element.24, bf16[512,1280]{1,0:T(8,128)(2,1)S(1)} %copy-done.19), kind=kOutput, calls=%fused_computation.5 | convolution fusion | flops 6744960000 | bytes 30187520 | tf_op jit(solution)/shard_map/dot_general | solution.py:58
  231.8 13.8 %fusion.52 = (f32[1280]{0:T(1024)S(1)}, f32[512,1280]{1,0:T(8,128)}) fusion(bf16[5120,512]{1,0:T(8,128)(2,1)} %get-tuple-element.131.refs_5_, bf16[1280,5120]{1,0:T(8,128)(2,1)} %get-tuple-element.23), kind=kOutput, calls=%fused_computation.112 | convolution fusion | flops 6711540736 | bytes 20976640 | tf_op jit(solution)/shard_map/dot_general | solution.py:58
  245.6 3.3 copy.71
  248.9 4.3 multiply_reduce_fusion
  257.3 2.9 convolution_convert_fusion.refs_9_
  262.5 4.8 fusion.25
  267.3 2.2 pad_maximum_fusion
  269.5 258.5 %reduce_backward.1 = (bf16[24,320,1280]{2,1,0:T(8,128)(2,1)}, bf16[3840,512]{1,0:T(8,128)(2,1)}, f32[1280,512]{1,0:T(8,128)}, bf16[24,2,320,512]{3,2,1,0:T(8,128)(2,1)}, bf16[24,640,512]{2,1,0:T(8,128)(2,1)}) custom-call(bf16[5120,512]{1,0:T(8,128)(2,1)} %get-tuple-element.128.refs_0_, bf16[1280,512]{1,0:T(8,128)(2,1)} %get-tuple-element.94.refs_1_, ...), custom_call_target="tpu_custom_call" | custom-call | tf_op jit(solution)/shard_map/reduce_backward/pallas_call | solution.py:908
  528.0 2.9 convert_reduce_fusion.1
  532.2 2.0 reduce_sum.176
  534.7 13.1 %fusion.11 = bf16[512,1280]{0,1:T(8,128)(2,1)} fusion(f32[512,1280]{0,1:T(8,128)} %copy-done.6, bf16[5120,512]{1,0:T(8,128)(2,1)} %get-tuple-element.128.refs_0_, bf16[5120,1280]{1,0:T(8,128)(2,1)} %get-tuple-element.24, f32[1280]{0:T(1024)S(1)} %reshape.460), kind=kOutput, calls=%fused_computation.27 | convolution fusion | flops 6712852480 | bytes 22287360 | tf_op jit(solution)/shard_map/dot_general | solution.py:58
  550.0 1.9 collective-permute-done.1
  553.9 1.8 collective-permute-done.2
  561.9 2.3 fusion.17
  564.2 6.6 %copy-done = bf16[24,320,1280]{2,1,0:T(8,128)(2,1)S(1)} copy-done((bf16[24,320,1280]{2,1,0:T(8,128)(2,1)S(1)}, bf16[24,320,1280]{2,1,0:T(8,128)(2,1)}, u32[]{:S(2)}) %copy-start) | copy-done | bytes 19660824
  570.8 1.8 widen.5
  572.6 4.3 widen.4
  577.0 5.6 widen.7
  582.6 5.6 widen.6
  588.2 2.6 copy.75
  590.8 2.1 copy.76
  595.0 1.9 collective-permute-done.9
  (133 shorter events, 36.4 us)
Async XLA Ops:
  15.4 239.7 %copy-start.1 = (bf16[512,1280]{0,1:T(8,128)(2,1)}, bf16[512,1280]{0,1:T(8,128)(2,1)S(1)}, u32[]{:S(2)}) copy-start(bf16[512,1280]{0,1:T(8,128)(2,1)S(1)} %copy.65) | copy-start | bytes 3932164
  156.4 2.9 copy-start.25
  156.4 3.2 copy-start.22
  159.6 102.0 %copy-start.20 = (s32[512]{0:T(512)}, s32[512]{0:T(512)S(1)}, u32[]{:S(2)}) copy-start(s32[512]{0:T(512)S(1)} %fusion.37) | copy-start | bytes 6148
  161.5 91.7 %copy-start.13 = (bf16[512,1280]{0,1:T(8,128)(2,1)}, bf16[512,1280]{0,1:T(8,128)(2,1)S(1)}, u32[]{:S(2)}) copy-start(bf16[512,1280]{0,1:T(8,128)(2,1)S(1)} %copy.69) | copy-start | bytes 3932164
  162.2 100.2 %copy-start.16 = (f32[80,512]{1,0:T(8,128)}, f32[80,512]{1,0:T(8,128)S(1)}, u32[]{:S(2)}) copy-start(f32[80,512]{1,0:T(8,128)S(1)} %get-tuple-element.106.refs_13_) | copy-start | bytes 491524
  162.2 100.2 %copy-start.17 = (f32[80,512]{1,0:T(8,128)}, f32[80,512]{1,0:T(8,128)S(1)}, u32[]{:S(2)}) copy-start(f32[80,512]{1,0:T(8,128)S(1)} %get-tuple-element.107.refs_14_) | copy-start | bytes 491524
  162.2 6.1 %copy-start.3 = (f32[1280,512]{1,0:T(8,128)S(1)}, f32[1280,512]{1,0:T(8,128)}, u32[]{:S(2)}) copy-start(f32[1280,512]{1,0:T(8,128)} %get-tuple-element.92) | copy-start | bytes 7864324
  162.2 6.1 %copy-start.5 = (f32[1280,512]{1,0:T(8,128)S(1)}, f32[1280,512]{1,0:T(8,128)}, u32[]{:S(2)}) copy-start(f32[1280,512]{1,0:T(8,128)} %get-tuple-element.93) | copy-start | bytes 7864324
  186.6 9.1 %copy-start.23 = (bf16[1280,1280]{1,0:T(8,128)(2,1)S(1)}, bf16[1280,1280]{1,0:T(8,128)(2,1)}, u32[]{:S(2)}) copy-start(bf16[1280,1280]{1,0:T(8,128)(2,1)} %get-tuple-element.22) | copy-start | bytes 9830404
  197.9 16.2 %copy-start.6 = (f32[512,1280]{0,1:T(8,128)}, f32[512,1280]{0,1:T(8,128)S(1)}, u32[]{:S(2)}) copy-start(f32[512,1280]{0,1:T(8,128)S(1)} %get-tuple-element.127) | copy-start | bytes 7864324
  198.3 15.9 %copy-start.19 = (bf16[512,1280]{1,0:T(8,128)(2,1)S(1)}, bf16[512,1280]{1,0:T(8,128)(2,1)}, u32[]{:S(2)}) copy-start(bf16[512,1280]{1,0:T(8,128)(2,1)} %param.31) | copy-start | bytes 3932164
  248.9 4.3 copy-start.7
  248.9 4.3 copy-start.8
  253.2 4.1 copy-start.24
  254.7 5.6 copy-start.11
  254.7 294.5 %collective-permute-start.5 = (f32[8960]{0:T(1024)S(1)}, f32[8960]{0:T(1024)S(1)}, u32[]{:S(2)}, u32[]{:S(2)}) collective-permute-start(f32[8960]{0:T(1024)S(1)} %pad_maximum_fusion.2), channel_id=1, source_target_pairs={{0,2},{2,0},{4,6},{6,4},{8,10},{10,8},{12,14},{14,12},{16,18},{18,... | collective-permute-start | bytes 107528 | tf_op jit(solution)/shard_map/ppermute | solution.py:955
  262.5 4.8 copy-start.15
  527.9 3.3 copy-start.9
  531.3 3.4 copy-start.21
  534.2 13.5 %collective-permute-start = (f32[7680]{0:T(1024)S(1)}, f32[7680]{0:T(1024)S(1)}, u32[]{:S(2)}, u32[]{:S(2)}) collective-permute-start(f32[7680]{0:T(1024)S(1)} %pad_maximum_fusion.3), channel_id=1, source_target_pairs={{0,2},{2,0},{4,6},{6,4},{8,10},{10,8},{12,14},{14,12},{16,18},{18,... | collective-permute-start | bytes 92168 | tf_op jit(solution)/shard_map/ppermute | solution.py:955
  534.7 27.2 %copy-start.10 = (f32[1280,512]{1,0:T(8,128)S(1)}, f32[1280,512]{1,0:T(8,128)}, u32[]{:S(2)}) copy-start(f32[1280,512]{1,0:T(8,128)} %get-tuple-element.25) | copy-start | bytes 7864324
  534.7 27.2 %copy-start.12 = (f32[512,1280]{0,1:T(8,128)S(1)}, f32[512,1280]{0,1:T(8,128)}, u32[]{:S(2)}) copy-start(f32[512,1280]{0,1:T(8,128)} %copy-done.11) | copy-start | bytes 7864324
  547.8 4.0 collective-permute-start.1
  549.2 4.0 collective-permute-start.6
  551.8 3.9 collective-permute-start.2
  553.2 4.0 collective-permute-start.7
  555.7 4.8 collective-permute-start.3
  557.2 35.7 %collective-permute-start.8 = (f32[8960]{0:T(1024)S(1)}, f32[8960]{0:T(1024)S(1)}, u32[]{:S(2)}, u32[]{:S(2)}) collective-permute-start(f32[8960]{0:T(1024)S(1)} %add.225), channel_id=1, source_target_pairs={{0,16},{2,18},{4,20},{6,22},{8,24},{10,26},{12,28},{14,30},{16,0},... | collective-permute-start | bytes 107528 | tf_op jit(solution)/shard_map/ppermute | solution.py:961
  560.6 33.1 %collective-permute-start.4 = (f32[7680]{0:T(1024)S(1)}, f32[7680]{0:T(1024)S(1)}, u32[]{:S(2)}, u32[]{:S(2)}) collective-permute-start(f32[7680]{0:T(1024)S(1)} %add.215), channel_id=1, source_target_pairs={{0,1},{1,0},{2,3},{3,2},{4,5},{5,4},{6,7},{7,6},{8,9},{9,8},{10,11... | collective-permute-start | bytes 92168 | tf_op jit(solution)/shard_map/ppermute | solution.py:966
  564.2 6.6 %copy-start = (bf16[24,320,1280]{2,1,0:T(8,128)(2,1)S(1)}, bf16[24,320,1280]{2,1,0:T(8,128)(2,1)}, u32[]{:S(2)}) copy-start(bf16[24,320,1280]{2,1,0:T(8,128)(2,1)} %get-tuple-element.27.part) | copy-start | bytes 58982404
  592.9 4.0 collective-permute-start.9
  (4 other events, 9.8 us)

commit v4 on v3

--- a/solution.py
+++ b/solution.py
@@ -154,188 +154,6 @@
         for offset, stage in sorted(stages, key=lambda item: -item[0]):
             if 0 <= tick - offset < count:
                 stage(tick - offset)
-
-
-def gather_kernel(n_rep, chunks, shard_rows, rows, wide, *refs):
-    count, n_w = len(chunks), len(shard_rows)
-    shards, fulls = refs[:n_w], refs[n_w : 2 * n_w]
-    hold, own_in, own_out, y_sem, d_sem, in_sem, mid_sem, back_sem, x_sem, c_sem, cd_sem = refs[
-        2 * n_w :
-    ]
-    at = Place(n_rep)
-    nz, half = at.nz, at.half
-    plane = rows * 4 // 5
-    unit = plane // n_rep
-    straight = (rows - plane) // 2
-    mine, yours = at.y, 1 - at.y
-
-    def shard(k, first, size):
-        w, row0, col0 = chunks[k]
-        return shards[w].at[pl.ds(pl.multiple_of(row0 + first, 8), size), pl.ds(col0, wide)]
-
-    def full(k, owner, first, size):
-        w, row0, col0 = chunks[k]
-        start = pl.multiple_of(owner * shard_rows[w] + row0 + first, 8)
-        return fulls[w].at[pl.ds(start, size), pl.ds(col0, wide)]
-
-    def place(c, x, z):
-        return ((c * 2 + x) * nz + z) * unit
-
-    def y_copy(k, owner):
-        first = place(at.c, at.x, at.z)
-        return remote(shard(k, first, unit), full(k, owner, first, unit), y_sem, k, at.to_y)
-
-    def d_copy(k, owner):
-        first = plane + at.c * straight
-        return remote(
-            shard(k, first, straight), full(k, owner, first, straight), d_sem, k, at.to_y
-        )
-
-    def along(k, begin, size, sems, device):
-        view = full(k, yours, place(at.c, at.x, begin), size * unit)
-        return remote(view, view, sems, k, device)
-
-    def in_send(k, depth):
-        return along(k, jnp.where(at.low, 0, nz - 1 - depth), depth + 1, in_sem, at.to_in)
-
-    def in_take(k, depth):
-        return along(k, jnp.where(at.low, 0, nz - depth), depth, in_sem, at.to_in)
-
-    def mid_send(k):
-        return along(k, jnp.where(at.low, 0, half), half, mid_sem, at.to_in)
-
-    def mid_take(k):
-        return along(k, jnp.where(at.low, half, 0), half, mid_sem, at.to_in)
-
-    def back_send(k, depth):
-        return along(k, jnp.where(at.low, depth, 0), nz - depth, back_sem, at.to_out)
-
-    def back_take(k, depth):
-        return along(k, jnp.where(at.low, depth + 1, 0), nz - depth - 1, back_sem, at.to_out)
-
-    def x_copy(k, x):
-        view = full(k, yours, place(at.c, x, 0), nz * unit)
-        return remote(view, view, x_sem, k, at.to_x)
-
-    def c_copy(k, c):
-        view = full(k, yours, place(c, 0, 0), 2 * nz * unit)
-        return remote(view, view, c_sem, k, at.to_core)
-
-    def cd_copy(k, c):
-        view = full(k, yours, plane + c * straight, straight)
-        return remote(view, view, cd_sem, k, at.to_core)
-
-    def own_load(k):
-        return pltpu.make_async_copy(shard(k, 0, rows), hold.at[k % 3], own_in.at[k])
-
-    def own_store(k):
-        return pltpu.make_async_copy(hold.at[k % 3], full(k, mine, 0, rows), own_out.at[k])
-
-    def inner_send(k, depth):
-        (mid_send(k) if depth == half - 1 else in_send(k, depth)).start()
-
-    def take_own(k):
-        if k >= 3:
-            own_store(k - 3).wait()
-        own_load(k).start()
-
-    def crossed(k):
-        own_load(k).wait()
-        own_store(k).start()
-        y_copy(k, yours).wait_recv()
-
-        @at.at_depth(0)
-        def _():
-            inner_send(k, 0)
-
-        d_copy(k, yours).wait_recv()
-        cd_copy(k, at.c).start()
-
-    def pass_in(depth):
-        def stage(k):
-            @at.at_depth(depth)
-            def _():
-                in_take(k, depth).wait_recv()
-                inner_send(k, depth)
-
-        return stage
-
-    def middle(k):
-        @at.at_depth(half - 1)
-        def _():
-            mid_take(k).wait_recv()
-            if half > 1:
-                back_send(k, half - 1).start()
-            x_copy(k, at.x).start()
-
-    def pass_out(depth):
-        def stage(k):
-            @at.at_depth(depth)
-            def _():
-                back_take(k, depth).wait_recv()
-                if depth > 0:
-                    back_send(k, depth).start()
-                x_copy(k, at.x).start()
-
-        return stage
-
-    def crossed_x(k):
-        x_copy(k, 1 - at.x).wait_recv()
-        c_copy(k, at.c).start()
-
-    at.meet(True)
-    for k in range(count):
-        y_copy(k, mine).start()
-        d_copy(k, mine).start()
-    stages = [(0, take_own), (1, crossed)]
-    stages += [(1 + depth, pass_in(depth)) for depth in range(1, half)]
-    stages += [(1 + half, middle)]
-    stages += [(1 + half + (half - 1 - depth), pass_out(depth)) for depth in range(half - 1)]
-    stages += [(2 * half + 1, crossed_x)]
-    skewed(count, stages)
-    for k in range(count):
-        if k >= count - 3:
-            own_store(k).wait()
-        y_copy(k, mine).wait_send()
-        d_copy(k, mine).wait_send()
-        x_copy(k, at.x).wait_send()
-        c_copy(k, at.c).wait_send()
-        cd_copy(k, at.c).wait_send()
-        for depth in range(half):
-
-            @at.at_depth(depth)
-            def _():
-                (mid_send(k) if depth == half - 1 else in_send(k, depth)).wait_send()
-                if depth > 0:
-                    back_send(k, depth).wait_send()
-
-        c_copy(k, 1 - at.c).wait_recv()
-        cd_copy(k, 1 - at.c).wait_recv()
-
-
-def gather_weights(shards, n_rep, n_shard):
-    if n_shard != 2:
-        return [lax.all_gather(shard, "shard", axis=0, tiled=True) for shard in shards]
-    rows, wide, chunks = cut_chunks(shards)
-    count = len(chunks)
-    shapes = [(shard.shape[0] * n_shard, shard.shape[1]) for shard in shards]
-    kernel = partial(
-        gather_kernel, n_rep, chunks, [shard.shape[0] for shard in shards], rows, wide
-    )
-    pair = pltpu.SemaphoreType.DMA((2, count))
-    return pl.pallas_call(
-        kernel,
-        out_shape=[jax.ShapeDtypeStruct(shape, jnp.bfloat16) for shape in shapes],
-        in_specs=[pl.BlockSpec(memory_space=pl.ANY)] * len(shards),
-        out_specs=[pl.BlockSpec(memory_space=pl.ANY)] * len(shards),
-        scratch_shapes=[pltpu.VMEM((3, rows, wide), jnp.bfloat16)]
-        + [pltpu.SemaphoreType.DMA((count,))] * 2
-        + [pair] * 8,
-        compiler_params=pltpu.CompilerParams(
-            collective_id=0, has_side_effects=True, vmem_limit_bytes=60 << 20
-        ),
-        name="gather_weights",
-    )(*shards)
 
 
 def cut_chunks(shards):
@@ -611,6 +429,11 @@
                 (self.shard_rows[w], self.across[w] * wide), jnp.float32
             ),
             compiler_params=pltpu.CompilerParams(vmem_limit_bytes=24 << 20),
+            cost_estimate=pl.CostEstimate(
+                flops=0,
+                transcendentals=0,
+                bytes_accessed=6 * down * self.across[w] * rows * wide,
+            ),
             name="widen",
         )(chunks)
 
@@ -942,13 +765,413 @@
     return [cuts.whole(chunks, w) for w in range(len(sizes))], grad_qkv, grad_first
 
 
+def forward_kernel(n_rep, cuts, n_heads, score_scale, *refs):
+    n_w = len(cuts.down)
+    shards, refs = refs[:n_w], refs[n_w:]
+    (
+        normed, patches, cotangent, qkv_bias, proj_bias, gain, bias, up_bias, down_bias,
+        pic_key, pic_query, cosine, sine,
+    ) = refs[:13]
+    fulls, refs = refs[13 : 13 + n_w], refs[13 + n_w :]
+    (
+        swap, heads_out, log_total, hidden, normed_two, act_turned, pre_turned, layer_out,
+        hold, w_block, turned, up_pre, act, out_sum,
+        own_in, own_out, w_sem, y_sem, d_sem, in_sem, mid_sem, back_sem, x_sem, c_sem, cd_sem,
+    ) = refs
+    at = Place(n_rep)
+    nz, half = at.nz, at.half
+    count, rows, wide = cuts.count, cuts.rows, cuts.wide
+    plane = rows * 4 // 5
+    unit = plane // n_rep
+    straight = (rows - plane) // 2
+    mine, yours = at.y, 1 - at.y
+    model = normed.shape[1]
+    tokens = normed.shape[0]
+    head = model // n_heads
+
+    def shard(w, row, col, first, size):
+        start = pl.multiple_of(row * rows + first, 16)
+        cols = pl.ds(pl.multiple_of(col * wide, 128), wide)
+        return shards[w].at[pl.ds(start, size), cols]
+
+    def full(w, row, col, owner, first, size):
+        start = pl.multiple_of(owner * cuts.shard_rows[w] + row * rows + first, 16)
+        cols = pl.ds(pl.multiple_of(col * wide, 128), wide)
+        return fulls[w].at[pl.ds(start, size), cols]
+
+    def alike(size):
+        return fulls[0].at[pl.ds(0, size), pl.ds(0, wide)]
+
+    def place(c, x, z):
+        return ((c * 2 + x) * nz + z) * unit
+
+    def spread_copy(k, first, size, sems, device):
+        def act_on(w, row, col):
+            view = full(w, row, col, yours, first, size)
+            remote(view, view, sems, k, device).start()
+
+        cuts.weight_of(k, act_on)
+
+    def settle(k, size, sems, device, received):
+        view = alike(size)
+        copy = remote(view, view, sems, k, device)
+        if received:
+            copy.wait_recv()
+        else:
+            copy.wait_send()
+
+    def along(k, begin, size, sems, device):
+        spread_copy(k, place(at.c, at.x, begin), size * unit, sems, device)
+
+    def start_y(k):
+        def act_on(w, row, col):
+            first = place(at.c, at.x, at.z)
+            remote(
+                shard(w, row, col, first, unit),
+                full(w, row, col, mine, first, unit),
+                y_sem, k, at.to_y,
+            ).start()
+            first = plane + at.c * straight
+            remote(
+                shard(w, row, col, first, straight),
+                full(w, row, col, mine, first, straight),
+                d_sem, k, at.to_y,
+            ).start()
+
+        cuts.weight_of(k, act_on)
+
+    def inner_send(k, depth):
+        if depth == half - 1:
+            along(k, jnp.where(at.low, 0, half), half, mid_sem, at.to_in)
+        else:
+            along(k, jnp.where(at.low, 0, nz - 1 - depth), depth + 1, in_sem, at.to_in)
+
+    def back_start(k, depth):
+        along(k, jnp.where(at.low, depth, 0), nz - depth, back_sem, at.to_out)
+
+    def x_start(k):
+        along(k, 0, nz, x_sem, at.to_x)
+
+    def crossed(k):
+        settle(k, unit, y_sem, at.to_y, True)
+
+        @at.at_depth(0)
+        def _():
+            inner_send(k, 0)
+
+        settle(k, straight, d_sem, at.to_y, True)
+        spread_copy(k, plane + at.c * straight, straight, cd_sem, at.to_core)
+
+    def pass_in(depth):
+        def stage(k):
+            @at.at_depth(depth)
+            def _():
+                settle(k, depth * unit, in_sem, at.to_in, True)
+                inner_send(k, depth)
+
+        return stage
+
+    def middle(k):
+        @at.at_depth(half - 1)
+        def _():
+            settle(k, half * unit, mid_sem, at.to_in, True)
+            if half > 1:
+                back_start(k, half - 1)
+            x_start(k)
+
+    def pass_out(depth):
+        def stage(k):
+            @at.at_depth(depth)
+            def _():
+                settle(k, (nz - depth - 1) * unit, back_sem, at.to_out, True)
+                if depth > 0:
+                    back_start(k, depth)
+                x_start(k)
+
+        return stage
+
+    def crossed_x(k):
+        settle(k, nz * unit, x_sem, at.to_x, True)
+        spread_copy(k, place(at.c, 0, 0), 2 * nz * unit, c_sem, at.to_core)
+
+    def own_load(k, view):
+        return pltpu.make_async_copy(view, hold.at[k % 3], own_in.at[k])
+
+    def own_store(k, view):
+        return pltpu.make_async_copy(hold.at[k % 3], view, own_out.at[k])
+
+    def take_own(k):
+        cuts.weight_of(k, lambda w, row, col: own_load(k, shard(w, row, col, 0, rows)).start())
+
+    def give_own(k):
+        own_load(k, alike(rows)).wait()
+        cuts.weight_of(
+            k, lambda w, row, col: own_store(k, full(w, row, col, mine, 0, rows)).start()
+        )
+
+    def arrived(k):
+        own_store(k, alike(rows)).wait()
+        settle(k, 2 * nz * unit, c_sem, at.to_core, True)
+        settle(k, straight, cd_sem, at.to_core, True)
+        settle(k, unit, y_sem, at.to_y, False)
+        settle(k, straight, d_sem, at.to_y, False)
+        settle(k, nz * unit, x_sem, at.to_x, False)
+        settle(k, 2 * nz * unit, c_sem, at.to_core, False)
+        settle(k, straight, cd_sem, at.to_core, False)
+        for depth in range(half):
+
+            @at.at_depth(depth)
+            def _():
+                if depth == half - 1:
+                    settle(k, half * unit, mid_sem, at.to_in, False)
+                else:
+                    settle(k, (depth + 1) * unit, in_sem, at.to_in, False)
+                if depth > 0:
+                    settle(k, (nz - depth) * unit, back_sem, at.to_out, False)
+
+    def block_of(u, view):
+        return pltpu.make_async_copy(view, w_block.at[u % 2], w_sem.at[0, u])
+
+    def half_block(u, owner, view):
+        spot = pl.ds(owner * (wide // 2), wide // 2)
+        return pltpu.make_async_copy(view, w_block.at[u % 2, spot, :], w_sem.at[owner, u])
+
+    def columns(w, col):
+        return fulls[w].at[:, pl.ds(pl.multiple_of(col * wide, 128), wide)]
+
+    def down_rows(i, owner):
+        start = owner * cuts.shard_rows[3] + i * (wide // 2)
+        return fulls[3].at[pl.ds(pl.multiple_of(start, 16), wide // 2), :]
+
+    step = 256
+
+    def qkv_step(b, u):
+        block_of(u, columns(0, 0)).wait()
+
+        @pl.loop(0, wide // step)
+        def _(i):
+            spot = pl.ds(pl.multiple_of(i * step, 128), step)
+            col = pl.ds(pl.multiple_of(b * wide + i * step, 128), step)
+            part = contract(normed[...], w_block[u % 2, :, spot], 1, 0) + qkv_bias[:, col]
+            turned[pl.ds(pl.multiple_of(i * step, 16), step), :] = part.T
+
+        @pl.loop(0, n_heads)
+        def _(h):
+            part = turned[pl.ds(pl.multiple_of(h * head, 8), head), :]
+            spot = pl.ds(pl.multiple_of(b * model + h * head, 16), head)
+
+            @pl.when(b < 2)
+            def _():
+                swap[spot, :] = apply_rotary(part, cosine[...], sine[...]).astype(jnp.bfloat16)
+
+            @pl.when(b == 2)
+            def _():
+                swap[spot, :] = part.astype(jnp.bfloat16)
+
+    def head_step(h):
+        def part(i):
+            return swap[pl.ds(pl.multiple_of(i * model + h * head, 16), head), :]
+
+        scores = contract(part(1), part(0), 0, 0) * score_scale
+        scores = jnp.where(pic_key[...] == pic_query[...], scores, -1000000000.0)
+        top = jnp.max(scores, axis=0, keepdims=True)
+        exp_scores = jnp.exp(scores - top)
+        total = jnp.sum(exp_scores, axis=0, keepdims=True)
+        probs = (exp_scores / total).astype(jnp.bfloat16)
+        attended = contract(part(2), probs, 1, 0)
+        heads_out[pl.ds(pl.multiple_of(h * head, 16), head), :] = attended.astype(jnp.bfloat16)
+        log_total[pl.ds(h, 1), :] = top + jnp.log(total)
+
+    def proj_step(u):
+        block_of(u, columns(0, 0)).wait()
+
+        @pl.loop(0, tokens // step)
+        def _(i):
+            spot = pl.ds(pl.multiple_of(i * step, 16), step)
+            lanes = pl.ds(pl.multiple_of(i * step, 128), step)
+            branch = contract(heads_out[:, lanes], w_block[u % 2], 0, 0)
+            rows_in = patches[spot, :].astype(jnp.float32) + branch + proj_bias[...]
+            hidden[spot, :] = rows_in
+            out_sum[spot, :] = rows_in + down_bias[...]
+            standard, _ = apply_layer_norm(rows_in)
+            normed_two[spot, :] = (standard * gain[...] + bias[...]).astype(jnp.bfloat16)
+
+    def up_step(c, u):
+        block_of(u, columns(0, 0)).wait()
+
+        @pl.loop(0, wide // step)
+        def _(i):
+            spot = pl.ds(pl.multiple_of(i * step, 128), step)
+            col = pl.multiple_of(c * wide + i * step, 128)
+            cols = pl.ds(col, step)
+            pre = contract(normed_two[...], w_block[u % 2, :, spot], 1, 0) + up_bias[:, cols]
+            up_pre[:, cols] = pre
+            result = (pre / (1.0 + jnp.exp(-quick_slope * pre))).astype(jnp.bfloat16)
+            act[:, cols] = result
+            act_turned[pl.ds(col, step), :] = result.T
+
+    def down_step(i, u):
+        for owner in range(2):
+            half_block(u, owner, down_rows(0, 0)).wait()
+            size = wide // 2
+            col = pl.multiple_of(owner * cuts.shard_rows[3] + i * size, 128)
+
+            @pl.loop(0, tokens // step)
+            def _(j):
+                spot = pl.ds(pl.multiple_of(j * step, 16), step)
+                lanes = pl.ds(pl.multiple_of(j * step, 128), step)
+                weight = w_block[u % 2, pl.ds(owner * size, size), :]
+                pre = up_pre[spot, pl.ds(col, size)]
+                sigmoid = 1.0 / (1.0 + jnp.exp(-quick_slope * pre))
+                slope = sigmoid + quick_slope * pre * sigmoid * (1.0 - sigmoid)
+                grad = contract(cotangent[spot, :], weight, 1, 1) * slope
+                pre_turned[pl.ds(col, size), lanes] = grad.astype(jnp.bfloat16).T
+                out_sum[spot, :] += contract(act[spot, pl.ds(col, size)], weight, 1, 0)
+
+    offset = 2 * half + 2
+    stages = [(1, crossed)]
+    stages += [(1 + depth, pass_in(depth)) for depth in range(1, half)]
+    stages += [(1 + half, middle)]
+    stages += [(1 + half + (half - 1 - depth), pass_out(depth)) for depth in range(half - 1)]
+    stages += [(2 * half + 1, crossed_x)]
+    stages += [(offset - 2, take_own), (offset - 1, give_own), (offset, arrived)]
+    stages.sort(key=lambda item: -item[0])
+    n_up, n_down = cuts.across[2], cuts.down[3] // 2
+    per_tick = 3
+    first_head = cuts.first[1] + 1
+    at_proj = first_head + -(-n_heads // per_tick)
+    at_up = at_proj + 1
+    at_down = max(at_up + n_up, cuts.first[3] + 2)
+    n_steps = 4 + n_up + n_down
+
+    at.meet(True)
+
+    @pl.loop(0, count)
+    def _(k):
+        start_y(k)
+
+    def tick_body(tick, carry):
+        for lag, stage in stages:
+
+            @pl.when((tick >= lag) & (tick < count + lag))
+            def _():
+                stage(tick - lag)
+
+        now = tick - offset
+
+        @pl.when((now >= 2) & (now < first_head) & (now % 2 == 0))
+        def _():
+            qkv_step(now // 2 - 1, now // 2 - 1)
+
+        @pl.when((now >= first_head) & (now < at_proj))
+        def _():
+            @pl.loop(0, per_tick)
+            def _(i):
+                h = (now - first_head) * per_tick + i
+
+                @pl.when(h < n_heads)
+                def _():
+                    head_step(h)
+
+        @pl.when(now == at_proj)
+        def _():
+            proj_step(3)
+
+        @pl.when((now >= at_up) & (now < at_up + n_up))
+        def _():
+            up_step(now - at_up, now - at_up + 4)
+
+        down_i = (now - at_down) // 2
+
+        @pl.when((now >= at_down) & (down_i < n_down) & ((now - at_down) % 2 == 0))
+        def _():
+            down_step(down_i, down_i + 4 + n_up)
+
+        soon = now + 1
+
+        @pl.when((soon >= 2) & (soon < first_head) & (soon % 2 == 0))
+        def _():
+            block_of(soon // 2 - 1, columns(0, soon // 2 - 1)).start()
+
+        @pl.when(soon == at_proj)
+        def _():
+            block_of(3, columns(1, 0)).start()
+
+        @pl.when((soon >= at_up) & (soon < at_up + n_up))
+        def _():
+            block_of(soon - at_up + 4, columns(2, soon - at_up)).start()
+
+        next_i = (soon - at_down) // 2
+
+        @pl.when((soon >= at_down) & (next_i < n_down) & ((soon - at_down) % 2 == 0))
+        def _():
+            for owner in range(2):
+                half_block(next_i + 4 + n_up, owner, down_rows(next_i, owner)).start()
+
+        return carry
+
+    lax.fori_loop(0, offset + at_down + 2 * n_down - 1, tick_body, 0)
+    layer_out[...] = out_sum[...].astype(jnp.bfloat16)
+
+
+def gather_forward(shards, inputs, n_rep, n_heads, score_scale):
+    cuts = Cuts([(shard.shape[0] * 2, shard.shape[1]) for shard in shards], 2)
+    tokens, model = inputs[0].shape
+    wide_two = shards[2].shape[1]
+    count, rows, wide = cuts.count, cuts.rows, cuts.wide
+    low, dma = jnp.bfloat16, pltpu.SemaphoreType.DMA
+    anywhere, local = pl.BlockSpec(memory_space=pl.ANY), pl.BlockSpec(memory_space=pltpu.VMEM)
+    n_steps = 4 + cuts.across[2] + cuts.down[3] // 2
+
+    def shape(*sizes, kind=low):
+        return jax.ShapeDtypeStruct(sizes, kind)
+
+    results = pl.pallas_call(
+        partial(forward_kernel, n_rep, cuts, n_heads, score_scale),
+        out_shape=[shape(item.shape[0] * 2, item.shape[1]) for item in shards]
+        + [
+            shape(3 * model, tokens),
+            shape(model, tokens),
+            shape(n_heads, tokens, kind=jnp.float32),
+            shape(tokens, model, kind=jnp.float32),
+            shape(tokens, model),
+            shape(wide_two, tokens),
+            shape(wide_two, tokens),
+            shape(tokens, model),
+        ],
+        in_specs=[anywhere] * len(shards) + [local] * len(inputs),
+        out_specs=[anywhere] * len(shards) + [local] * 8,
+        scratch_shapes=[
+            pltpu.VMEM((3, rows, wide), low),
+            pltpu.VMEM((2, model, wide), low),
+            pltpu.VMEM((model, tokens), jnp.float32),
+            pltpu.VMEM((tokens, wide_two), jnp.float32),
+            pltpu.VMEM((tokens, wide_two), low),
+            pltpu.VMEM((tokens, model), jnp.float32),
+            dma((count,)),
+            dma((count,)),
+            dma((2, n_steps)),
+        ]
+        + [dma((2, count))] * 8,
+        compiler_params=pltpu.CompilerParams(
+            collective_id=0, has_side_effects=True, vmem_limit_bytes=63 << 20
+        ),
+        name="gather_forward",
+    )(*shards, *inputs)
+    return results[: len(shards)], results[len(shards) :]
+
+
 class Links:
     def __init__(self, n_rep, n_shard):
         self.nz, self.ny, self.n_rep = n_rep // 4, n_shard, n_rep
         self.y = lax.axis_index("shard")
 
     def gather_vector(self, vector):
-        return lax.all_gather(vector, "shard", axis=0, tiled=False)
+        if self.ny != 2:
+            return lax.all_gather(vector, "shard", axis=0, tiled=False)
+        other = lax.ppermute(vector, "shard", [(0, 1), (1, 0)])
+        low, high = jnp.where(self.y == 0, vector, other), jnp.where(self.y == 0, other, vector)
+        return jnp.stack([low, high])
 
     def sum_all(self, vector):
         for flip in (1, 2):
@@ -1005,8 +1228,11 @@
 
     small = [ln1_gain, ln1_bias, qkv_bias, proj_bias, ln2_gain, ln2_bias, fc1_bias, fc2_bias]
     sizes = [item.shape[0] for item in small]
-    gathered = links.gather_vector(jnp.concatenate(small))
     spots = [sum(sizes[:i]) for i in range(len(sizes) + 1)]
+    packed = sum(
+        jnp.pad(item, (spots[i], spots[-1] - spots[i + 1])) for i, item in enumerate(small)
+    )
+    gathered = links.gather_vector(packed)
     (
         first_norm_gain, first_norm_bias, b_qkv, b_proj,
         second_norm_gain, second_norm_bias, b_up, b_down,
@@ -1015,38 +1241,51 @@
         for i in range(len(sizes))
     ]
 
-    w_qkv, w_proj, w_up, w_down = gather_weights(
-        [qkv_weight, proj_weight, fc1_weight, fc2_weight], n_rep, n_shard
-    )
-
     input_rows = patches.astype(jnp.float32)
     first_centered_standard, first_inverse_spread = apply_layer_norm(input_rows)
     first_normalized = (first_centered_standard * first_norm_gain + first_norm_bias).astype(
         jnp.bfloat16
     )
-    qkv_rows = contract(w_qkv, first_normalized, 0, 1) + b_qkv[:, None]
-    qkv_rows = qkv_rows.reshape(3, head_count, head_size, row_count)
-    queries = apply_rotary(qkv_rows[0], cosine, sine).astype(jnp.bfloat16)
-    keys_rot = apply_rotary(qkv_rows[1], cosine, sine).astype(jnp.bfloat16)
-    values_all = qkv_rows[2].astype(jnp.bfloat16)
-    attended, log_total = attend(queries, keys_rot, values_all, idents, score_scale)
-    heads_out = attended.reshape(model_width, row_count).astype(jnp.bfloat16)
-    hidden_rows = input_rows + contract(heads_out, w_proj, 0, 0) + b_proj
-    second_centered_standard, second_inverse_spread = apply_layer_norm(hidden_rows)
-    second_normalized = (second_centered_standard * second_norm_gain + second_norm_bias).astype(
-        jnp.bfloat16
-    )
-    up_pre = contract(w_up, second_normalized, 0, 1) + b_up[:, None]
-    sigmoid_up = 1.0 / (1.0 + jnp.exp(-quick_slope * up_pre))
-    activation = (up_pre * sigmoid_up).astype(jnp.bfloat16)
-
-    out_full = hidden_rows + contract(activation, w_down, 0, 0) + b_down
-    layer_out = out_full.astype(jnp.bfloat16)
+    shards = [qkv_weight, proj_weight, fc1_weight, fc2_weight]
+    qkv_shape = (3 * model_width, row_count)
     grad_out = cotangent.astype(jnp.float32)
     d_b_down = jnp.sum(grad_out, axis=0)
-    grad_act = contract(w_down, cotangent, 1, 1)
-    slope_up = sigmoid_up + quick_slope * up_pre * sigmoid_up * (1.0 - sigmoid_up)
-    grad_pre = (grad_act * slope_up).astype(jnp.bfloat16)
+    if n_shard == 2:
+        rows_in = [
+            item[None, :]
+            for item in (b_qkv, b_proj, second_norm_gain, second_norm_bias, b_up, b_down)
+        ]
+        inputs = [first_normalized, patches, cotangent] + rows_in
+        inputs += [idents[:, None], idents[None, :], cosine, sine]
+        weights, results = gather_forward(shards, inputs, n_rep, head_count, score_scale)
+        w_qkv, w_proj, w_up, w_down = weights
+        qkv, heads_out, log_total, hidden_rows, second_normalized = results[:5]
+        activation, grad_pre, layer_out = results[5:]
+        second_centered_standard, second_inverse_spread = apply_layer_norm(hidden_rows)
+    else:
+        w_qkv, w_proj, w_up, w_down = [
+            lax.all_gather(shard, "shard", axis=0, tiled=True) for shard in shards
+        ]
+        qkv_rows = contract(w_qkv, first_normalized, 0, 1) + b_qkv[:, None]
+        qkv_rows = qkv_rows.reshape(3, head_count, head_size, row_count)
+        queries = apply_rotary(qkv_rows[0], cosine, sine).astype(jnp.bfloat16)
+        keys_rot = apply_rotary(qkv_rows[1], cosine, sine).astype(jnp.bfloat16)
+        values_all = qkv_rows[2].astype(jnp.bfloat16)
+        attended, log_total = attend(queries, keys_rot, values_all, idents, score_scale)
+        heads_out = attended.reshape(model_width, row_count).astype(jnp.bfloat16)
+        hidden_rows = input_rows + contract(heads_out, w_proj, 0, 0) + b_proj
+        second_centered_standard, second_inverse_spread = apply_layer_norm(hidden_rows)
+        second_normalized = (
+            second_centered_standard * second_norm_gain + second_norm_bias
+        ).astype(jnp.bfloat16)
+        up_pre = contract(w_up, second_normalized, 0, 1) + b_up[:, None]
+        sigmoid_up = 1.0 / (1.0 + jnp.exp(-quick_slope * up_pre))
+        activation = (up_pre * sigmoid_up).astype(jnp.bfloat16)
+        out_full = hidden_rows + contract(activation, w_down, 0, 0) + b_down
+        layer_out = out_full.astype(jnp.bfloat16)
+        grad_act = contract(w_down, cotangent, 1, 1)
+        slope_up = sigmoid_up + quick_slope * up_pre * sigmoid_up * (1.0 - sigmoid_up)
+        grad_pre = (grad_act * slope_up).astype(jnp.bfloat16)
     d_b_up = jnp.sum(grad_pre.astype(jnp.float32), axis=1)
     second_normalized_gradient = contract(grad_pre, w_up, 0, 1)
     second_gain_gradient = jnp.sum(second_normalized_gradient * second_centered_standard, axis=0)
@@ -1062,9 +1301,7 @@
     grad_heads = contract(w_proj, grad_branch, 1, 1).astype(jnp.bfloat16)
     lefts = [activation, second_normalized.T, heads_out, first_normalized.T]
     rights = [cotangent.T, grad_pre, grad_branch.T]
-    qkv_shape = (3 * model_width, row_count)
     if n_shard == 2:
-        qkv = jnp.stack([queries, keys_rot, values_all]).reshape(qkv_shape)
         small_args = [
             grad_heads, log_total, idents[:, None], idents[None, :], cosine, sine,
         ]

time: 603 us -> 535 us (0.89)
  matrix products: 92.6 us -> 14.6 us
  Pallas kernels: 406 us -> 444 us
  other arithmetic: 42.5 us -> 23 us
    dot_general x7 -> x2, matrix products: 74.3 us -> 14.6 us  [contract(): lax.dot_general(left, right, (((left_dim,), (right_dim,)), ((), ())), pre...]
    pallas_call x1, Pallas kernels: 130 us -> 164 us  [gather_forward(): pl.pallas_call(partial(forward_kernel, n_rep, cuts, n_heads, score_scale)...]
    dot_general x2 -> x0, matrix products: 18.2 us -> none  [the longest x1 9.1 us: masked_scores(): jnp.einsum('hdk,hdq->hkq', keys_rot, queries, preferred_element_type=jnp....]
    concatenate x1 -> x0, other arithmetic: 6.07 us -> none  [apply_rotary(): jnp.concatenate([-matrix[..., half_size:, :], matrix[..., :half_size, :]]...]
    unnamed x65 -> x56, local copies, waits for them, and re-layouts: 21.1 us -> 20.5 us
  transfers between devices with their start and end apart: 10 -> 11, of which waited for: 6 -> 7; matrix products, arithmetic and copies ran while one was open for 7% -> 2% of each run, Pallas kernels for 46% -> 3%
where the time goes in v4:
time: 535 us; the launch traced here: 534 us
  Pallas kernels  444 us (83%)
  local copies, waits for them, and re-layouts  32.2 us (6%)
  other arithmetic  23 us (4%)
  matrix products  14.6 us (3%)
  starting transfers between devices  11.2 us (2%)
  waiting for transfers between devices  8.85 us (2%)
    pallas_call x1, Pallas kernels, reduce_backward(): pl.pallas_call(partial(backward_kernel, n_rep, cuts, n_heads, slots, scor...  262 us
    pallas_call x1, Pallas kernels, gather_forward(): pl.pallas_call(partial(forward_kernel, n_rep, cuts, n_heads, score_scale)...  164 us
    unnamed x56, local copies, waits for them, and re-layouts  20.5 us
    pallas_call x4, Pallas kernels, whole(): pl.pallas_call(widen, grid=(down, self.across[w]), in_specs=[pl.BlockSpec...  17.4 us
    dot_general x2, matrix products, contract(): lax.dot_general(left, right, (((left_dim,), (right_dim,)), ((), ())), pre...  14.6 us
  transfers between devices with their start and end apart: 11, of which 7 were waited for; matrix products, arithmetic and copies ran while one was open for 2% of the time, Pallas kernels for 3%

profile of v4, /device:TPU:0, one launch (start us, length us, event | category | flops | bytes accessed | tf_op | source)
XLA Modules:
  0.0 534.5 jit_solution(8914573346077073150)
XLA Ops:
  1.5 3.1 collective-permute-start
  4.6 1.7 copy.50
  7.3 1.3 fusion.15
  9.6 1.5 copy.53
  11.9 1.6 fusion.28.refs_3_
  13.5 1.4 copy.51.refs_4_
  18.5 164.3 %gather_forward.1 = (bf16[1280,3840]{1,0:T(8,128)(2,1)}, bf16[1280,1280]{1,0:T(8,128)(2,1)}, bf16[1280,5120]{1,0:T(8,128)(2,1)}, bf16[5120,1280]{1,0:T(8,128)(2,...) custom-call(bf16[640,3840]{1,0:T(8,128)(2,1)} %refs_0_.1, ...), custom_call_target="tpu_custom_call" | custom-call | tf_op jit(solution)/shard_map/gather_forward/pallas_call | solution.py:1129
  182.9 11.5 %fusion.22 = (f32[1280]{0:T(1024)S(1)}, f32[512,1280]{1,0:T(8,128)S(1)}) fusion(bf16[5120,512]{1,0:T(8,128)(2,1)} %get-tuple-element.30.refs_5_, bf16[1280,5120]{1,0:T(8,128)(2,1)} %get-tuple-element.31), kind=kOutput, calls=%fused_computation.66 | convolution fusion | flops 6711540736 | bytes 20976640 | tf_op jit(solution)/shard_map/dot_general | solution.py:58
  194.4 2.1 copy.55
  196.5 2.1 copy.54
  198.7 1.9 reduce_sum.159
  201.0 2.4 copy.56
  203.4 2.8 multiply_reduce_fusion
  206.3 1.5 convert_reduce_fusion.4
  209.0 2.1 copy-done.21
  211.2 3.0 convolution_convert_fusion.refs_9_
  214.2 261.8 %reduce_backward.1 = (bf16[24,320,1280]{2,1,0:T(8,128)(2,1)}, bf16[3840,512]{1,0:T(8,128)(2,1)}, f32[1280,512]{1,0:T(8,128)}, bf16[24,2,320,512]{3,2,1,0:T(8,128)(2,1)}, bf16[24,640,512]{2,1,0:T(8,128)(2,1)}) custom-call(bf16[5120,512]{1,0:T(8,128)(2,1)} %get-tuple-element.32.refs_0_, bf16[1280,512]{1,0:T(8,128)(2,1)} %bitcast.49, ...), custom_call_target="tpu_custom_call" | custom-call | tf_op jit(solution)/shard_map/reduce_backward/pallas_call | solution.py:731
  476.0 3.2 fusion.12
  479.5 3.4 convert_reduce_fusion
  487.3 2.0 collective-permute-done.2
  491.4 1.8 collective-permute-done.3
  494.2 2.0 collective-permute-start.9
  496.2 1.9 collective-permute-done.4
  498.2 2.4 fusion.11
  500.6 6.6 %copy-done = bf16[24,320,1280]{2,1,0:T(8,128)(2,1)S(1)} copy-done((bf16[24,320,1280]{2,1,0:T(8,128)(2,1)S(1)}, bf16[24,320,1280]{2,1,0:T(8,128)(2,1)}, u32[]{:S(2)}) %copy-start) | copy-done | bytes 19660824
  507.2 4.3 widen.4
  511.5 1.8 widen.5
  513.3 5.6 %widen.6 = f32[640,5120]{1,0:T(8,128)} custom-call(bf16[24,320,1280]{2,1,0:T(8,128)(2,1)S(1)} %copy-done), custom_call_target="tpu_custom_call" | custom-call | bytes 19660800 | tf_op jit(solution)/shard_map/widen/pallas_call | solution.py:423
  518.9 5.6 %widen.7 = f32[2560,1280]{1,0:T(8,128)} custom-call(bf16[24,320,1280]{2,1,0:T(8,128)(2,1)S(1)} %copy-done), custom_call_target="tpu_custom_call" | custom-call | bytes 19660800 | tf_op jit(solution)/shard_map/widen/pallas_call | solution.py:423
  524.6 2.1 copy.60
  526.7 2.0 collective-permute-start.10
  532.0 2.5 copy.68
  (113 shorter events, 20.0 us)
Async XLA Ops:
  1.5 9.6 %collective-permute-start = (bf16[8320]{0:T(1024)(128)(2,1)S(1)}, bf16[8320]{0:T(1024)(128)(2,1)S(1)}, u32[]{:S(2)}, u32[]{:S(2)}) collective-permute-start(bf16[8320]{0:T(1024)(128)(2,1)S(1)} %pad_add_fusion), channel_id=1, source_target_pairs={{0,1},{1,0},{2,3},{3,2},{4,5},{5,4},{6,7},{7,6},{8,9},{9,8},{10,11... | collective-permute-start | bytes 49928 | tf_op jit(solution)/shard_map/ppermute | solution.py:1172
  4.5 5.1 copy-start.9
  6.3 5.6 %copy-start.1 = (bf16[512,1280]{0,1:T(8,128)(2,1)}, bf16[512,1280]{0,1:T(8,128)(2,1)S(1)}, u32[]{:S(2)}) copy-start(bf16[512,1280]{0,1:T(8,128)(2,1)S(1)} %copy.50) | copy-start | bytes 3932164
  6.5 4.6 copy-start.12
  6.5 4.6 copy-start.13
  6.5 4.5 copy-start.14
  6.6 4.5 copy-start.15
  6.6 4.5 copy-start.16
  6.6 4.5 copy-start.17
  6.6 4.5 copy-start.18
  6.6 4.5 copy-start.19
  8.7 3.2 copy-start.11
  203.4 2.8 copy-start.4
  203.4 2.9 copy-start.7
  207.8 6.4 %copy-start.5 = (f32[512,1280]{0,1:T(8,128)}, f32[512,1280]{0,1:T(8,128)S(1)}, u32[]{:S(2)}) copy-start(f32[512,1280]{0,1:T(8,128)S(1)} %get-tuple-element.91) | copy-start | bytes 7864324
  207.8 3.3 copy-start.21
  476.0 3.2 copy-start.3
  479.5 3.7 copy-start.10
  483.0 15.3 %copy-start.2 = (bf16[512,1280]{0,1:T(8,128)(2,1)S(1)}, bf16[512,1280]{0,1:T(8,128)(2,1)}, u32[]{:S(2)}) copy-start(bf16[512,1280]{0,1:T(8,128)(2,1)} %copy-done.1) | copy-start | bytes 3932164
  483.0 15.3 %copy-start.6 = (f32[512,1280]{0,1:T(8,128)S(1)}, f32[512,1280]{0,1:T(8,128)}, u32[]{:S(2)}) copy-start(f32[512,1280]{0,1:T(8,128)} %copy-done.5) | copy-start | bytes 7864324
  483.8 1.3 collective-permute-start.1
  484.3 1.9 collective-permute-start.6
  485.1 4.1 collective-permute-start.2
  486.2 4.0 collective-permute-start.7
  489.3 3.9 collective-permute-start.3
  490.2 4.0 collective-permute-start.8
  493.2 4.9 collective-permute-start.4
  494.2 32.4 %collective-permute-start.9 = (f32[8960]{0:T(1024)S(1)}, f32[8960]{0:T(1024)S(1)}, u32[]{:S(2)}, u32[]{:S(2)}) collective-permute-start(f32[8960]{0:T(1024)S(1)} %add.168), channel_id=1, source_target_pairs={{0,16},{2,18},{4,20},{6,22},{8,24},{10,26},{12,28},{14,30},{16,0},... | collective-permute-start | bytes 107528 | tf_op jit(solution)/shard_map/ppermute | solution.py:1184
  498.1 30.5 %collective-permute-start.5 = (f32[7680]{0:T(1024)S(1)}, f32[7680]{0:T(1024)S(1)}, u32[]{:S(2)}, u32[]{:S(2)}) collective-permute-start(f32[7680]{0:T(1024)S(1)} %add.158), channel_id=1, source_target_pairs={{0,1},{1,0},{2,3},{3,2},{4,5},{5,4},{6,7},{7,6},{8,9},{9,8},{10,11... | collective-permute-start | bytes 92168 | tf_op jit(solution)/shard_map/ppermute | solution.py:1189
  500.6 6.6 %copy-start = (bf16[24,320,1280]{2,1,0:T(8,128)(2,1)S(1)}, bf16[24,320,1280]{2,1,0:T(8,128)(2,1)}, u32[]{:S(2)}) copy-start(bf16[24,320,1280]{2,1,0:T(8,128)(2,1)} %get-tuple-element.41.part) | copy-start | bytes 58982404
  518.9 5.6 %copy-start.8 = (f32[512,1280]{0,1:T(8,128)S(1)}, f32[512,1280]{0,1:T(8,128)}, u32[]{:S(2)}) copy-start(f32[512,1280]{0,1:T(8,128)} %fusion.11) | copy-start | bytes 7864324
  526.7 4.0 collective-permute-start.10
  (2 other events, 5.1 us)

commit v5 on v4

--- a/solution.py
+++ b/solution.py
@@ -440,11 +440,13 @@
 
 def backward_kernel(n_rep, cuts, n_heads, slots, score_scale, *refs):
     (
-        left_0, left_1, left_2, left_3, right_0, right_1, right_2, qkv, w_qkv,
-        grad_heads, log_total, pic_key, pic_query, cosine, sine,
-        out, grad_qkv, grad_first, lent_left, lent_right,
+        left_0, left_1, left_2, left_3, right_0, right_1, qkv, w_qkv, w_up, w_proj,
+        hidden, cotangent, patches,
+        log_total, pic_key, pic_query, cosine, sine, gain_one, gain_two, down_sum,
+        out, right_2, grad_qkv, d_rows, sums, lent_left, lent_right,
         op_left, op_right, held, got_y, got_x, got_in, got_mid, total, swap, w_block,
-        load_l, load_r, put, qkv_sem, block_sem,
+        pre_block, turned, branch, grad_heads, rows_in, got_sums,
+        load_l, load_r, put, once_sem, block_sem, sum_sem,
         l0_sem, l1_sem, r_sem, y_sem, x_sem, in_sem, mid_sem, back_sem, ax_sem, ac_sem, af_sem,
     ) = refs
     lefts = [left_0, left_1, left_2, left_3]
@@ -656,26 +658,185 @@
         swap[part(1), :] = rotary_back(grad_key, turn_c, turn_s).astype(jnp.bfloat16)
         swap[part(2), :] = grad_value.astype(jnp.bfloat16)
 
-    def block_load(j):
+    tokens = qkv.shape[1]
+    wide_two = right_1.shape[0]
+    n_up, n_qkv = wide_two // width, qkv.shape[0] // width
+    ends = [0]
+    for size in (model, model, wide_two, model, model, model, qkv.shape[0], model):
+        ends.append(ends[-1] + size)
+
+    def sums_of(i, start=0, size=model):
+        return pl.ds(pl.multiple_of(ends[i] + start, 128), size)
+
+    def column_sums(block):
+        ones = jnp.ones((8, tokens), jnp.bfloat16)
+        return contract(ones, block, 1, 1)[0:1, :]
+
+    def w_load(src, j, slot):
         cols = pl.ds(pl.multiple_of(j * width, 128), width)
-        return pltpu.make_async_copy(w_qkv.at[:, cols], w_block.at[j % 2], block_sem.at[j])
-
-    def first_step(j):
-        block_load(j).wait()
-        inside = pl.ds(pl.multiple_of(j * width, 16), width)
+        return lambda k: pltpu.make_async_copy(src.at[:, cols], w_block.at[slot], block_sem.at[0, k])
+
+    def pre_load(j, slot):
+        spot = pl.ds(pl.multiple_of(j * width, 16), width)
+        return pltpu.make_async_copy(right_1.at[spot, :], pre_block.at[slot], block_sem.at[1, j])
+
+    def once(i, src, dst):
+        return pltpu.make_async_copy(src, dst, once_sem.at[i])
+
+    def add_turned(slot, right):
         step = 256
 
         @pl.loop(0, model // step)
         def _(i):
             spot = pl.ds(pl.multiple_of(i * step, 16), step)
-            grad_first[spot, :] += contract(w_block[j % 2, spot, :], swap[inside, :], 1, 0)
-
-    n_blocks = qkv.shape[0] // width
-    take_qkv = pltpu.make_async_copy(qkv, swap, qkv_sem.at[0])
-    give_qkv = pltpu.make_async_copy(swap, grad_qkv, qkv_sem.at[1])
+            turned[spot, :] += contract(w_block[slot, spot, :], right, 1, 0)
+
+    def clear_turned():
+        turned[...] = jnp.zeros_like(turned)
+
+    def load_up(pair):
+        for slot in range(2):
+            j = pair * 2 + slot
+            w_load(w_up, j, slot)(j).start()
+            pre_load(j, slot).start()
+
+    def up_step(pair):
+        for slot in range(2):
+            j = pair * 2 + slot
+            w_load(w_up, j, slot)(j).wait()
+            pre_load(j, slot).wait()
+            block = pre_block[slot]
+            add_turned(slot, block)
+            sums[:, sums_of(2, j * width, width)] = column_sums(block)
+
+    def load_proj():
+        for slot in range(2):
+            w_load(w_proj, slot, slot)(n_up + slot).start()
+
+    def load_qkv(pair):
+        for slot in range(2):
+            j = pair * 2 + slot
+            w_load(w_qkv, j, slot)(n_up + 2 + j).start()
+
+    def qkv_step(pair):
+        for slot in range(2):
+            j = pair * 2 + slot
+            w_load(w_qkv, j, slot)(n_up + 2 + j).wait()
+            block = swap[pl.ds(pl.multiple_of(j * width, 16), width), :]
+            add_turned(slot, block)
+            sums[:, sums_of(6, j * width, width)] = column_sums(block)
+
+    step = 128
+
+    def norm_two():
+        once(2, hidden, d_rows).wait()
+        once(3, cotangent, rows_in).wait()
+
+        @pl.loop(0, tokens // step)
+        def _(i):
+            spot = pl.ds(pl.multiple_of(i * step, 16), step)
+            lanes = pl.ds(pl.multiple_of(i * step, 128), step)
+            standard, inverse = apply_layer_norm(d_rows[spot, :])
+            grad = turned[:, lanes].T
+            sums[:, sums_of(0)] += jnp.sum(grad * standard, axis=0, keepdims=True)
+            sums[:, sums_of(1)] += jnp.sum(grad, axis=0, keepdims=True)
+            back = norm_gradient_step(grad, standard, inverse, gain_two[...])
+            back = back + rows_in[spot, :].astype(jnp.float32)
+            d_rows[spot, :] = back
+            low = back.astype(jnp.bfloat16)
+            branch[:, lanes] = low.T
+
+        sums[:, sums_of(7)] = column_sums(branch[...])
+        once(4, patches, rows_in).start()
+        once(5, branch, right_2).start()
+        for slot in range(2):
+            w_load(w_proj, slot, slot)(n_up + slot).wait()
+
+        @pl.loop(0, model // step)
+        def _(i):
+            spot = pl.ds(pl.multiple_of(i * step, 16), step)
+            result = contract(w_block[0, spot, :], branch[pl.ds(0, width), :], 1, 0)
+            result += contract(w_block[1, spot, :], branch[pl.ds(width, width), :], 1, 0)
+            grad_heads[spot, :] = result.astype(jnp.bfloat16)
+
+        once(5, branch, right_2).wait()
+        clear_turned()
+
+    def norm_one():
+        once(4, patches, rows_in).wait()
+
+        @pl.loop(0, tokens // step)
+        def _(i):
+            spot = pl.ds(pl.multiple_of(i * step, 16), step)
+            lanes = pl.ds(pl.multiple_of(i * step, 128), step)
+            standard, inverse = apply_layer_norm(rows_in[spot, :].astype(jnp.float32))
+            grad = turned[:, lanes].T
+            sums[:, sums_of(4)] += jnp.sum(grad * standard, axis=0, keepdims=True)
+            sums[:, sums_of(5)] += jnp.sum(grad, axis=0, keepdims=True)
+            d_rows[spot, :] += norm_gradient_step(grad, standard, inverse, gain_one[...])
+
+    def sums_to(i, device):
+        return remote(sums, got_sums.at[i], sum_sem, i, device)
+
+    def swap_sums(i, device):
+        def begin():
+            sums_to(i, device).start()
+
+        def end():
+            sums_to(i, device).wait()
+            sums[...] += got_sums[i]
+
+        return begin, end
+
+    def sums_in(depth):
+        def act():
+            @at.at_depth(depth)
+            def _():
+                if depth > 0:
+                    sums_to(3, at.to_in).wait_recv()
+                    sums[...] += got_sums[3]
+                sums_to(4 if depth == half - 1 else 3, at.to_in).start()
+
+            @at.at_depth(depth - 1)
+            def _():
+                if depth > 0:
+                    sums_to(3, at.to_in).wait_send()
+
+        return act
+
+    def sums_middle():
+        @at.at_depth(half - 1)
+        def _():
+            sums_to(4, at.to_in).wait()
+            sums[...] += got_sums[4]
+            if half > 1:
+                sums_to(5, at.to_out).start()
+
+    def sums_out(depth):
+        def act():
+            @at.at_depth(depth)
+            def _():
+                sums_to(5, at.to_out).wait_recv()
+                sums[...] = got_sums[5]
+                if depth > 0:
+                    sums_to(5, at.to_out).start()
+
+            @at.at_depth(depth + 1)
+            def _():
+                sums_to(5, at.to_out).wait_send()
+
+        return act
+
+    take_qkv = once(0, qkv, swap)
+    give_qkv = once(1, swap, grad_qkv)
     take_qkv.start()
+    once(2, hidden, d_rows).start()
+    once(3, cotangent, rows_in).start()
     at.meet(True)
-    grad_first[...] = jnp.zeros_like(grad_first)
+    load_up(0)
+    clear_turned()
+    sums[...] = jnp.zeros_like(sums)
+    sums[:, sums_of(3)] = down_sum[...]
     take_qkv.wait()
     stages = [(0, push), (1, load), (2, product), (4, start_x), (6, start_z)]
     stages += [(6 + depth, pass_in(depth)) for depth in range(1, half)]
@@ -683,8 +844,28 @@
     stages += [(6 + half + (half - 1 - depth), pass_out(depth)) for depth in range(half - 1)]
     stages += [(slots + 2, sent), (7 + 2 * half, forward), (9 + 2 * half, finish)]
     stages.sort(key=lambda item: -item[0])
-    per_tick = -(-n_heads // (cuts.first[3] - 2))
-    done = -(-n_heads // per_tick)
+    per_tick = 2
+    at_norm = n_up // 2
+    at_heads = at_norm + 1
+    at_qkv = at_heads + -(-n_heads // per_tick)
+    at_one = at_qkv + n_qkv // 2
+    begins, ends_of = zip(
+        swap_sums(0, at.to_core), swap_sums(1, at.to_x), swap_sums(2, at.to_y)
+    )
+    events = {at_norm: [norm_two], at_one: [norm_one, begins[0]]}
+    now = at_one
+    for i in range(3):
+        now += 1
+        events[now] = [ends_of[i]] + ([begins[i + 1]] if i < 2 else [sums_in(0)])
+    for act in (
+        [sums_in(depth) for depth in range(1, half)]
+        + [sums_middle]
+        + [sums_out(depth) for depth in reversed(range(half - 1))]
+    ):
+        now += 1
+        events[now] = [act]
+    last = count + 9 + 2 * half
+    assert now < last and at_norm < cuts.first[2] and at_qkv < cuts.first[3]
 
     def tick_body(tick, carry):
         for offset, stage in stages:
@@ -693,52 +874,80 @@
             def _():
                 stage(tick - offset)
 
-        @pl.when(tick < done)
+        @pl.when(tick < at_norm)
+        def _():
+            up_step(tick)
+
+        @pl.when(tick < at_norm - 1)
+        def _():
+            load_up(tick + 1)
+
+        @pl.when(tick == at_norm - 1)
+        def _():
+            load_proj()
+
+        for when, acts in events.items():
+
+            @pl.when(tick == when)
+            def _():
+                for act in acts:
+                    act()
+
+        @pl.when((tick >= at_heads) & (tick < at_qkv))
         def _():
             @pl.loop(0, per_tick)
             def _(i):
-                head_step(tick * per_tick + i)
-
-        @pl.when(tick == done)
+                h = (tick - at_heads) * per_tick + i
+
+                @pl.when(h < n_heads)
+                def _():
+                    head_step(h)
+
+        @pl.when(tick == at_qkv)
         def _():
             give_qkv.start()
             give_qkv.wait()
 
-        @pl.when((tick > done) & (tick <= done + n_blocks))
-        def _():
-            first_step(tick - done - 1)
-
-        @pl.when((tick >= done) & (tick < done + n_blocks))
-        def _():
-            block_load(tick - done).start()
+        @pl.when((tick >= at_qkv) & (tick < at_one))
+        def _():
+            qkv_step(tick - at_qkv)
+
+        @pl.when((tick >= at_qkv - 1) & (tick < at_one - 1))
+        def _():
+            load_qkv(tick - at_qkv + 1)
 
         return carry
 
-    lax.fori_loop(0, count + 9 + 2 * half, tick_body, 0)
-
-
-def reduce_backward(lefts, rights, qkv, w_qkv, small, n_rep, n_heads, score_scale):
-    tokens = qkv.shape[1]
-    sizes = [(left.shape[0], right.shape[0]) for left, right in zip(lefts, rights + [qkv])]
+    lax.fori_loop(0, last, tick_body, 0)
+
+
+def reduce_backward(lefts, rights, others, small, n_rep, n_heads, score_scale):
+    qkv, _, w_up, w_proj, hidden = others[:5]
+    tokens, model = hidden.shape
+    sizes = [(left.shape[0], right) for left, right in zip(lefts, (model, w_up.shape[1], model))]
+    sizes.append((model, qkv.shape[0]))
     cuts = Cuts(sizes, 2)
     half = n_rep // 8
     slots = 3 + 2 * half
     count, rows, wide = cuts.count, cuts.rows, cuts.wide
     block, width = rows // 2, wide // 2
-    low, dma = jnp.bfloat16, pltpu.SemaphoreType.DMA
+    n_sums = 6 * model + w_up.shape[1] + qkv.shape[0]
+    low, full, dma = jnp.bfloat16, jnp.float32, pltpu.SemaphoreType.DMA
     anywhere, local = pl.BlockSpec(memory_space=pl.ANY), pl.BlockSpec(memory_space=pltpu.VMEM)
-    model = w_qkv.shape[0]
-    chunks, grad_qkv, grad_first, _, _ = pl.pallas_call(
+    n_blocks = (w_up.shape[1] + qkv.shape[0]) // width + 2
+    chunks, _, _, d_rows, sums, _, _ = pl.pallas_call(
         partial(backward_kernel, n_rep, cuts, n_heads, slots, score_scale),
         out_shape=[
             jax.ShapeDtypeStruct((count, rows, wide), low),
+            jax.ShapeDtypeStruct((model, tokens), low),
             jax.ShapeDtypeStruct(qkv.shape, low),
-            jax.ShapeDtypeStruct((model, tokens), jnp.float32),
+            jax.ShapeDtypeStruct((tokens, model), full),
+            jax.ShapeDtypeStruct((1, n_sums), full),
             jax.ShapeDtypeStruct((count, 2, rows, tokens), low),
             jax.ShapeDtypeStruct((count, width, tokens), low),
         ],
-        in_specs=[anywhere] * 9 + [local] * len(small),
-        out_specs=[anywhere, anywhere, local, anywhere, anywhere],
+        in_specs=[anywhere] * (len(lefts) + len(rights) + len(others)) + [local] * len(small),
+        out_specs=[anywhere] * 3 + [local] * 2 + [anywhere] * 2,
         scratch_shapes=[
             pltpu.VMEM((2, 2, 2, rows, tokens), low),
             pltpu.VMEM((2, 2, width, tokens), low),
@@ -750,19 +959,26 @@
             pltpu.VMEM((count, block, width), low),
             pltpu.VMEM(qkv.shape, low),
             pltpu.VMEM((2, model, width), low),
+            pltpu.VMEM((2, width, tokens), low),
+            pltpu.VMEM((model, tokens), full),
+            pltpu.VMEM((model, tokens), low),
+            pltpu.VMEM((model, tokens), low),
+            pltpu.VMEM((tokens, model), low),
+            pltpu.VMEM((6, 1, n_sums), full),
             dma((2, 2, count)),
             dma((2, count)),
             dma((count,)),
-            dma((2,)),
-            dma((qkv.shape[0] // width,)),
+            dma((6,)),
+            dma((2, n_blocks)),
+            dma((2, 6)),
         ]
         + [dma((2, count))] * 11,
         compiler_params=pltpu.CompilerParams(
             collective_id=1, has_side_effects=True, vmem_limit_bytes=63 << 20
         ),
         name="reduce_backward",
-    )(*lefts, *rights, qkv, w_qkv, *small)
-    return [cuts.whole(chunks, w) for w in range(len(sizes))], grad_qkv, grad_first
+    )(*lefts, *rights, *others, *small)
+    return [cuts.whole(chunks, w) for w in range(len(sizes))], d_rows, sums[0]
 
 
 def forward_kernel(n_rep, cuts, n_heads, score_scale, *refs):
@@ -774,8 +990,8 @@
     ) = refs[:13]
     fulls, refs = refs[13 : 13 + n_w], refs[13 + n_w :]
     (
-        swap, heads_out, log_total, hidden, normed_two, act_turned, pre_turned, layer_out,
-        hold, w_block, turned, up_pre, act, out_sum,
+        swap, heads_out, log_total, hidden, two_turned, act_turned, pre_turned, layer_out,
+        hold, w_block, turned, up_pre, act, out_sum, normed_two,
         own_in, own_out, w_sem, y_sem, d_sem, in_sem, mid_sem, back_sem, x_sem, c_sem, cd_sem,
     ) = refs
     at = Place(n_rep)
@@ -994,7 +1210,9 @@
             hidden[spot, :] = rows_in
             out_sum[spot, :] = rows_in + down_bias[...]
             standard, _ = apply_layer_norm(rows_in)
-            normed_two[spot, :] = (standard * gain[...] + bias[...]).astype(jnp.bfloat16)
+            result = (standard * gain[...] + bias[...]).astype(jnp.bfloat16)
+            normed_two[spot, :] = result
+            two_turned[:, lanes] = result.T
 
     def up_step(c, u):
         block_of(u, columns(0, 0)).wait()
@@ -1134,7 +1352,7 @@
             shape(model, tokens),
             shape(n_heads, tokens, kind=jnp.float32),
             shape(tokens, model, kind=jnp.float32),
-            shape(tokens, model),
+            shape(model, tokens),
             shape(wide_two, tokens),
             shape(wide_two, tokens),
             shape(tokens, model),
@@ -1148,6 +1366,7 @@
             pltpu.VMEM((tokens, wide_two), jnp.float32),
             pltpu.VMEM((tokens, wide_two), low),
             pltpu.VMEM((tokens, model), jnp.float32),
+            pltpu.VMEM((tokens, model), low),
             dma((count,)),
             dma((count,)),
             dma((2, n_steps)),
@@ -1259,9 +1478,16 @@
         inputs += [idents[:, None], idents[None, :], cosine, sine]
         weights, results = gather_forward(shards, inputs, n_rep, head_count, score_scale)
         w_qkv, w_proj, w_up, w_down = weights
-        qkv, heads_out, log_total, hidden_rows, second_normalized = results[:5]
+        qkv, heads_out, log_total, hidden_rows, second_turned = results[:5]
         activation, grad_pre, layer_out = results[5:]
-        second_centered_standard, second_inverse_spread = apply_layer_norm(hidden_rows)
+        others = [qkv, w_qkv, w_up, w_proj, hidden_rows, cotangent, patches]
+        row_args = [first_norm_gain[None, :], second_norm_gain[None, :], d_b_down[None, :]]
+        small_args = [log_total, idents[:, None], idents[None, :], cosine, sine] + row_args
+        lefts = [activation, second_turned, heads_out, first_normalized.T]
+        rights = [cotangent.T, grad_pre]
+        products, d_patches, total = reduce_backward(
+            lefts, rights, others, small_args, n_rep, head_count, score_scale
+        )
     else:
         w_qkv, w_proj, w_up, w_down = [
             lax.all_gather(shard, "shard", axis=0, tiled=True) for shard in shards
@@ -1286,29 +1512,21 @@
         grad_act = contract(w_down, cotangent, 1, 1)
         slope_up = sigmoid_up + quick_slope * up_pre * sigmoid_up * (1.0 - sigmoid_up)
         grad_pre = (grad_act * slope_up).astype(jnp.bfloat16)
-    d_b_up = jnp.sum(grad_pre.astype(jnp.float32), axis=1)
-    second_normalized_gradient = contract(grad_pre, w_up, 0, 1)
-    second_gain_gradient = jnp.sum(second_normalized_gradient * second_centered_standard, axis=0)
-    d_bias_two = jnp.sum(second_normalized_gradient, axis=0)
-    grad_hidden = grad_out + norm_gradient_step(
-        second_normalized_gradient,
-        second_centered_standard,
-        second_inverse_spread,
-        second_norm_gain,
-    )
-    grad_branch = grad_hidden.astype(jnp.bfloat16)
-    d_b_proj = jnp.sum(grad_branch.astype(jnp.float32), axis=0)
-    grad_heads = contract(w_proj, grad_branch, 1, 1).astype(jnp.bfloat16)
-    lefts = [activation, second_normalized.T, heads_out, first_normalized.T]
-    rights = [cotangent.T, grad_pre, grad_branch.T]
-    if n_shard == 2:
-        small_args = [
-            grad_heads, log_total, idents[:, None], idents[None, :], cosine, sine,
-        ]
-        products, grad_qkv, first_gradient = reduce_backward(
-            lefts, rights, qkv, w_qkv, small_args, n_rep, head_count, score_scale
+        d_b_up = jnp.sum(grad_pre.astype(jnp.float32), axis=1)
+        second_normalized_gradient = contract(grad_pre, w_up, 0, 1)
+        second_gain_gradient = jnp.sum(
+            second_normalized_gradient * second_centered_standard, axis=0
         )
-    else:
+        d_bias_two = jnp.sum(second_normalized_gradient, axis=0)
+        grad_hidden = grad_out + norm_gradient_step(
+            second_normalized_gradient,
+            second_centered_standard,
+            second_inverse_spread,
+            second_norm_gain,
+        )
+        grad_branch = grad_hidden.astype(jnp.bfloat16)
+        d_b_proj = jnp.sum(grad_branch.astype(jnp.float32), axis=0)
+        grad_heads = contract(w_proj, grad_branch, 1, 1).astype(jnp.bfloat16)
         back = partial(head_back, score_scale=score_scale)
         grad_query, grad_key, grad_value = jax.vmap(back, in_axes=(0, 0, 0, 0, None, 0))(
             queries,
@@ -1322,42 +1540,43 @@
         grad_key = rotary_back(grad_key, cosine, sine)
         grad_qkv = jnp.stack([grad_query, grad_key, grad_value]).reshape(qkv_shape)
         grad_qkv = grad_qkv.astype(jnp.bfloat16)
-        first_gradient = contract(w_qkv, grad_qkv, 1, 0)
+        first_normalized_gradient = contract(grad_qkv, w_qkv, 0, 1)
+        lefts = [activation, second_normalized.T, heads_out, first_normalized.T]
+        rights = [cotangent.T, grad_pre, grad_branch.T, grad_qkv]
         products = [
-            contract(left, right, 1, 1).astype(jnp.bfloat16)
-            for left, right in zip(lefts, rights + [grad_qkv])
+            contract(left, right, 1, 1).astype(jnp.bfloat16) for left, right in zip(lefts, rights)
         ]
         products = [
             item.astype(jnp.float32) for item in reduce_products(products, n_rep, n_shard)
         ]
+        d_b_qkv = jnp.sum(grad_qkv.astype(jnp.float32), axis=1)
+        first_gain_gradient = jnp.sum(first_normalized_gradient * first_centered_standard, axis=0)
+        d_bias_one = jnp.sum(first_normalized_gradient, axis=0)
+        d_patches = grad_hidden + norm_gradient_step(
+            first_normalized_gradient,
+            first_centered_standard,
+            first_inverse_spread,
+            first_norm_gain,
+        )
+        total = jnp.concatenate(
+            [
+                second_gain_gradient, d_bias_two, d_b_up, d_b_down,
+                first_gain_gradient, d_bias_one, d_b_qkv, d_b_proj,
+            ]
+        )
+        total = links.sum_all(total)
     d_w_down, d_w_up, d_w_proj, d_w_qkv = products
-    d_b_qkv = jnp.sum(grad_qkv.astype(jnp.float32), axis=1)
-    first_normalized_gradient = first_gradient.T
-    first_gain_gradient = jnp.sum(first_normalized_gradient * first_centered_standard, axis=0)
-    d_bias_one = jnp.sum(first_normalized_gradient, axis=0)
-    d_patches = grad_hidden + norm_gradient_step(
-        first_normalized_gradient,
-        first_centered_standard,
-        first_inverse_spread,
-        first_norm_gain,
-    )
-
-    def own_parts(vectors):
-        lens = [item.shape[0] for item in vectors]
-        total = links.sum_all(jnp.concatenate(vectors))
-        result, start = [], 0
-        for size in lens:
-            own = size // n_shard
-            result.append(lax.dynamic_slice_in_dim(total, start + links.y * own, own, 0))
-            start += size
-        return result
-
-    m_gain, m_bias, m_upb, m_downb = own_parts(
-        [second_gain_gradient, d_bias_two, d_b_up, d_b_down]
-    )
-    a_gain, a_bias, a_qkvb, a_projb = own_parts(
-        [first_gain_gradient, d_bias_one, d_b_qkv, d_b_proj]
-    )
+
+    ff = fc1_weight.shape[1]
+    own_parts, start = [], 0
+    for size in (
+        model_width, model_width, ff, model_width,
+        model_width, model_width, 3 * model_width, model_width,
+    ):
+        own = size // n_shard
+        own_parts.append(lax.dynamic_slice_in_dim(total, start + links.y * own, own, 0))
+        start += size
+    m_gain, m_bias, m_upb, m_downb, a_gain, a_bias, a_qkvb, a_projb = own_parts
     return (
         layer_out,
         d_patches,

time: 535 us -> 485 us (0.907)
  other arithmetic: 23 us -> 5.54 us
  matrix products: 14.6 us -> 0 us
  local copies, waits for them, and re-layouts: 32.2 us -> 21.5 us
  Pallas kernels: 444 us -> 453 us
  waiting for transfers between devices: 8.85 us -> 0.01 us
  starting transfers between devices: 11.2 us -> 3.06 us
    dot_general x2 -> x0, matrix products: 14.6 us -> none  [contract(): lax.dot_general(left, right, (((left_dim,), (right_dim,)), ((), ())), pre...]
    reduce_sum x6 -> x1, other arithmetic: 11.7 us -> 0.22 us  [per_device(): d_b_down = jnp.sum(grad_out, axis=0)]
    pallas_call x1, Pallas kernels: 262 us -> 271 us  [reduce_backward(): pl.pallas_call(partial(backward_kernel, n_rep, cuts, n_heads, slots, scor...]
    ppermute x10 -> x0, waiting for transfers between devices: 8.84 us -> none  [the longest x4 4.6 us: sum_all(): vector = vector + lax.ppermute(vector, 'rep', pairs)]
    ppermute x10 -> x0, starting transfers between devices: 8.11 us -> none  [the longest x4 3.22 us: sum_all(): vector = vector + lax.ppermute(vector, 'rep', pairs)]
    unnamed x56 -> x43, local copies, waits for them, and re-layouts: 20.5 us -> 16.6 us
  transfers between devices with their start and end apart: 11 -> 1, of which waited for: 7 -> 0; matrix products, arithmetic and copies ran while one was open for 2% -> 1% of each run, Pallas kernels for 3% -> 0%
where the time goes in v5:
time: 485 us; the launch traced here: 484 us
  Pallas kernels  453 us (93%)
  local copies, waits for them, and re-layouts  21.5 us (4%)
  other arithmetic  5.54 us (1%)
    pallas_call x1, Pallas kernels, reduce_backward(): pl.pallas_call(partial(backward_kernel, n_rep, cuts, n_heads, slots, scor...  271 us
    pallas_call x1, Pallas kernels, gather_forward(): pl.pallas_call(partial(forward_kernel, n_rep, cuts, n_heads, score_scale)...  164 us
    pallas_call x4, Pallas kernels, whole(): pl.pallas_call(widen, grid=(down, self.across[w]), in_specs=[pl.BlockSpec...  17.4 us
    unnamed x43, local copies, waits for them, and re-layouts  16.6 us
  transfers between devices with their start and end apart: 1, of which 0 were waited for; matrix products, arithmetic and copies ran while one was open for 1% of the time, Pallas kernels for 0%

profile of v5, /device:TPU:0, one launch (start us, length us, event | category | flops | bytes accessed | tf_op | source)
XLA Modules:
  0.0 484.2 jit_solution(17687103201618093489)
XLA Ops:
  0.6 0.8 pad_add_fusion
  1.5 3.1 collective-permute-start
  4.5 1.7 copy.38
  6.3 0.2 convert_reduce_fusion
  6.5 0.4 fusion.2
  7.1 0.2 convert_reduce_fusion.1
  7.6 1.3 fusion.6
  9.0 1.5 copy.41
  10.4 0.9 copy.40.refs_13_.refs_14_
  11.3 0.6 broadcast_in_dim.2.refs_20_
  12.2 0.5 fusion.5
  12.7 1.6 fusion.9.refs_3_
  14.3 1.4 copy.39.refs_4_
  15.7 0.6 copy.43
  16.3 0.6 copy.44
  16.9 0.6 copy.45
  17.5 0.6 copy.46
  18.1 0.6 copy.47
  18.7 0.6 copy.48
  19.3 0.6 copy.49
  19.9 164.4 %gather_forward.1 = (bf16[1280,3840]{1,0:T(8,128)(2,1)}, bf16[1280,1280]{1,0:T(8,128)(2,1)}, bf16[1280,5120]{1,0:T(8,128)(2,1)}, bf16[5120,1280]{1,0:T(8,128)(2,...) custom-call(bf16[640,3840]{1,0:T(8,128)(2,1)} %refs_0_.1, ...), custom_call_target="tpu_custom_call" | custom-call | tf_op jit(solution)/shard_map/gather_forward/pallas_call | solution.py:1347
  184.4 271.4 %reduce_backward.1 = (bf16[24,320,1280]{2,1,0:T(8,128)(2,1)}, bf16[1280,512]{1,0:T(8,128)(2,1)}, bf16[3840,512]{1,0:T(8,128)(2,1)}, f32[512,1280]{1,0:T(8,128)},...) custom-call(bf16[5120,512]{1,0:T(8,128)(2,1)} %get-tuple-element.29.refs_0_, ...), custom_call_target="tpu_custom_call" | custom-call | tf_op jit(solution)/shard_map/reduce_backward/pallas_call | solution.py:938
  455.8 6.6 %copy-done = bf16[24,320,1280]{2,1,0:T(8,128)(2,1)S(1)} copy-done((bf16[24,320,1280]{2,1,0:T(8,128)(2,1)S(1)}, bf16[24,320,1280]{2,1,0:T(8,128)(2,1)}, u32[]{:S(2)}) %copy-start) | copy-done | bytes 19660824
  462.4 4.3 widen.4
  466.7 1.8 widen.5
  468.5 5.6 %widen.6 = f32[640,5120]{1,0:T(8,128)} custom-call(bf16[24,320,1280]{2,1,0:T(8,128)(2,1)S(1)} %copy-done), custom_call_target="tpu_custom_call" | custom-call | bytes 19660800 | tf_op jit(solution)/shard_map/widen/pallas_call | solution.py:423
  474.1 5.6 %widen.7 = f32[2560,1280]{1,0:T(8,128)} custom-call(bf16[24,320,1280]{2,1,0:T(8,128)(2,1)S(1)} %copy-done), custom_call_target="tpu_custom_call" | custom-call | bytes 19660800 | tf_op jit(solution)/shard_map/widen/pallas_call | solution.py:423
  479.8 0.6 dynamic-slice_reduce_fusion.1
  480.4 0.6 dynamic-slice_reduce_fusion
  481.0 0.6 dynamic-slice_reduce_fusion.2
  481.7 1.1 copy.52
  482.7 1.5 copy.53
  (48 shorter events, 0.6 us)
Async XLA Ops:
  1.5 10.4 %collective-permute-start = (bf16[8320]{0:T(1024)(128)(2,1)S(1)}, bf16[8320]{0:T(1024)(128)(2,1)S(1)}, u32[]{:S(2)}, u32[]{:S(2)}) collective-permute-start(bf16[8320]{0:T(1024)(128)(2,1)S(1)} %pad_add_fusion), channel_id=1, source_target_pairs={{0,1},{1,0},{2,3},{3,2},{4,5},{5,4},{6,7},{7,6},{8,9},{9,8},{10,11... | collective-permute-start | bytes 49928 | tf_op jit(solution)/shard_map/ppermute | solution.py:1391
  4.5 2.5 copy-start.14
  4.5 2.5 copy-start.1
  6.3 1.0 copy-start.15
  6.9 5.0 %copy-start.5 = (bf16[2560]{0:T(1024)(128)(2,1)S(1)}, bf16[2560]{0:T(1024)(128)(2,1)}, u32[]{:S(2)}) copy-start(bf16[2560]{0:T(1024)(128)(2,1)} %param.28) | copy-start | bytes 15364
  6.9 5.0 %copy-start.7 = (bf16[1920]{0:T(1024)(128)(2,1)S(1)}, bf16[1920]{0:T(1024)(128)(2,1)}, u32[]{:S(2)}) copy-start(bf16[1920]{0:T(1024)(128)(2,1)} %param.22) | copy-start | bytes 11524
  7.0 5.0 %copy-start.8 = (bf16[640]{0:T(1024)(128)(2,1)S(1)}, bf16[640]{0:T(1024)(128)(2,1)}, u32[]{:S(2)}) copy-start(bf16[640]{0:T(1024)(128)(2,1)} %param.30) | copy-start | bytes 3844
  7.0 5.0 %copy-start.9 = (bf16[640]{0:T(1024)(128)(2,1)S(1)}, bf16[640]{0:T(1024)(128)(2,1)}, u32[]{:S(2)}) copy-start(bf16[640]{0:T(1024)(128)(2,1)} %param.26) | copy-start | bytes 3844
  7.0 5.0 %copy-start.10 = (bf16[640]{0:T(1024)(128)(2,1)S(1)}, bf16[640]{0:T(1024)(128)(2,1)}, u32[]{:S(2)}) copy-start(bf16[640]{0:T(1024)(128)(2,1)} %param.25) | copy-start | bytes 3844
  7.0 5.0 %copy-start.11 = (bf16[640]{0:T(1024)(128)(2,1)S(1)}, bf16[640]{0:T(1024)(128)(2,1)}, u32[]{:S(2)}) copy-start(bf16[640]{0:T(1024)(128)(2,1)} %param.24) | copy-start | bytes 3844
  7.0 5.0 %copy-start.12 = (bf16[640]{0:T(1024)(128)(2,1)S(1)}, bf16[640]{0:T(1024)(128)(2,1)}, u32[]{:S(2)}) copy-start(bf16[640]{0:T(1024)(128)(2,1)} %param.20) | copy-start | bytes 3844
  7.0 5.0 %copy-start.13 = (bf16[640]{0:T(1024)(128)(2,1)S(1)}, bf16[640]{0:T(1024)(128)(2,1)}, u32[]{:S(2)}) copy-start(bf16[640]{0:T(1024)(128)(2,1)} %param.19) | copy-start | bytes 3844
  9.0 3.8 copy-start.4
  455.8 6.6 %copy-start = (bf16[24,320,1280]{2,1,0:T(8,128)(2,1)S(1)}, bf16[24,320,1280]{2,1,0:T(8,128)(2,1)}, u32[]{:S(2)}) copy-start(bf16[24,320,1280]{2,1,0:T(8,128)(2,1)} %get-tuple-element.41.part) | copy-start | bytes 58982404
  474.1 5.6 %copy-start.6 = (f32[1,16640]{1,0:T(1,128)S(1)}, f32[1,16640]{1,0:T(1,128)}, u32[]{:S(2)}) copy-start(f32[1,16640]{1,0:T(1,128)} %get-tuple-element.40) | copy-start | bytes 199684
  474.1 7.5 %copy-start.3 = (bf16[512,1280]{1,0:T(8,128)(2,1)S(1)}, bf16[512,1280]{1,0:T(8,128)(2,1)}, u32[]{:S(2)}) copy-start(bf16[512,1280]{1,0:T(8,128)(2,1)} %get-tuple-element.76) | copy-start | bytes 3932164
  479.8 3.0 copy-start.2

commit v6 on v5

--- a/solution.py
+++ b/solution.py
@@ -428,7 +428,7 @@
             out_shape=jax.ShapeDtypeStruct(
                 (self.shard_rows[w], self.across[w] * wide), jnp.float32
             ),
-            compiler_params=pltpu.CompilerParams(vmem_limit_bytes=24 << 20),
+            compiler_params=pltpu.CompilerParams(vmem_limit_bytes=60 << 20),
             cost_estimate=pl.CostEstimate(
                 flops=0,
                 transcendentals=0,
@@ -436,6 +436,10 @@
             ),
             name="widen",
         )(chunks)
+
+
+class LAGS:
+    x, z, step, end = 4, 6, 1, 2
 
 
 def backward_kernel(n_rep, cuts, n_heads, slots, score_scale, *refs):
@@ -838,11 +842,15 @@
     sums[...] = jnp.zeros_like(sums)
     sums[:, sums_of(3)] = down_sum[...]
     take_qkv.wait()
-    stages = [(0, push), (1, load), (2, product), (4, start_x), (6, start_z)]
-    stages += [(6 + depth, pass_in(depth)) for depth in range(1, half)]
-    stages += [(6 + half, middle)]
-    stages += [(6 + half + (half - 1 - depth), pass_out(depth)) for depth in range(half - 1)]
-    stages += [(slots + 2, sent), (7 + 2 * half, forward), (9 + 2 * half, finish)]
+    stages = [(0, push), (1, load), (2, product), (LAGS.x, start_x), (LAGS.z, start_z)]
+    stages += [(LAGS.z + LAGS.step * depth, pass_in(depth)) for depth in range(1, half)]
+    middle_lag = LAGS.z + LAGS.step * half
+    stages += [(middle_lag, middle)]
+    stages += [
+        (middle_lag + LAGS.step * (half - 1 - depth), pass_out(depth)) for depth in range(half - 1)
+    ]
+    forward_lag = middle_lag + LAGS.step * (half - 1) + 2
+    stages += [(slots + 2, sent), (forward_lag, forward), (forward_lag + LAGS.end, finish)]
     stages.sort(key=lambda item: -item[0])
     per_tick = 2
     at_norm = n_up // 2
@@ -864,7 +872,7 @@
     ):
         now += 1
         events[now] = [act]
-    last = count + 9 + 2 * half
+    last = count + forward_lag + LAGS.end
     assert now < last and at_norm < cuts.first[2] and at_qkv < cuts.first[3]
 
     def tick_body(tick, carry):
@@ -928,7 +936,7 @@
     sizes.append((model, qkv.shape[0]))
     cuts = Cuts(sizes, 2)
     half = n_rep // 8
-    slots = 3 + 2 * half
+    slots = LAGS.z + LAGS.step * half + 1 - 2
     count, rows, wide = cuts.count, cuts.rows, cuts.wide
     block, width = rows // 2, wide // 2
     n_sums = 6 * model + w_up.shape[1] + qkv.shape[0]
@@ -1246,12 +1254,16 @@
                 pre_turned[pl.ds(col, size), lanes] = grad.astype(jnp.bfloat16).T
                 out_sum[spot, :] += contract(act[spot, pl.ds(col, size)], weight, 1, 0)
 
-    offset = 2 * half + 2
+    gap = 2
+    across = 1 + gap * 2 * half
+    offset = across + 1
     stages = [(1, crossed)]
-    stages += [(1 + depth, pass_in(depth)) for depth in range(1, half)]
-    stages += [(1 + half, middle)]
-    stages += [(1 + half + (half - 1 - depth), pass_out(depth)) for depth in range(half - 1)]
-    stages += [(2 * half + 1, crossed_x)]
+    stages += [(1 + gap * depth, pass_in(depth)) for depth in range(1, half)]
+    stages += [(1 + gap * half, middle)]
+    stages += [
+        (1 + gap * (2 * half - 1 - depth), pass_out(depth)) for depth in range(half - 1)
+    ]
+    stages += [(across, crossed_x)]
     stages += [(offset - 2, take_own), (offset - 1, give_own), (offset, arrived)]
     stages.sort(key=lambda item: -item[0])
     n_up, n_down = cuts.across[2], cuts.down[3] // 2

time: 485 us -> 466 us (0.961)
  Pallas kernels: 453 us -> 440 us
  local copies, waits for them, and re-layouts: 21.5 us -> 14.9 us
    pallas_call x1, Pallas kernels: 164 us -> 139 us  [gather_forward(): pl.pallas_call(partial(forward_kernel, n_rep, cuts, n_heads, score_scale)...]
    pallas_call x4, Pallas kernels: 17.4 us -> 28 us  [whole(): pl.pallas_call(widen, grid=(down, self.across[w]), in_specs=[pl.BlockSpec...]
    unnamed x43 -> x41, local copies, waits for them, and re-layouts: 16.6 us -> 10 us
  transfers between devices with their start and end apart: 1 -> 1, of which waited for: 0 -> 0; matrix products, arithmetic and copies ran while one was open for 1% -> 2% of each run, Pallas kernels for 0% -> 0%
where the time goes in v6:
time: 466 us; the launch traced here: 465 us
  Pallas kernels  440 us (94%)
  local copies, waits for them, and re-layouts  14.9 us (3%)
  other arithmetic  5.54 us (1%)
    pallas_call x1, Pallas kernels, reduce_backward(): pl.pallas_call(partial(backward_kernel, n_rep, cuts, n_heads, slots, scor...  273 us
    pallas_call x1, Pallas kernels, gather_forward(): pl.pallas_call(partial(forward_kernel, n_rep, cuts, n_heads, score_scale)...  139 us
    pallas_call x4, Pallas kernels, whole(): pl.pallas_call(widen, grid=(down, self.across[w]), in_specs=[pl.BlockSpec...  28 us
    unnamed x41, local copies, waits for them, and re-layouts  10 us
  transfers between devices with their start and end apart: 1, of which 0 were waited for; matrix products, arithmetic and copies ran while one was open for 2% of the time, Pallas kernels for 0%

profile of v6, /device:TPU:0, one launch (start us, length us, event | category | flops | bytes accessed | tf_op | source)
XLA Modules:
  0.0 464.7 jit_solution(8945534752742400692)
XLA Ops:
  0.6 0.8 pad_add_fusion
  1.5 3.1 collective-permute-start
  4.5 1.7 copy.38
  6.3 0.2 convert_reduce_fusion
  6.5 0.4 fusion.2
  7.1 0.2 convert_reduce_fusion.1
  7.3 0.2 reduce_window_sum.11
  7.6 1.3 fusion.6
  9.0 1.5 copy.41
  10.4 0.9 copy.40.refs_13_.refs_14_
  11.3 0.6 broadcast_in_dim.2.refs_20_
  12.2 0.5 fusion.5
  12.7 1.6 fusion.9.refs_3_
  14.3 1.4 copy.39.refs_4_
  15.7 0.6 copy.43
  16.3 0.6 copy.44
  16.9 0.6 copy.45
  17.5 0.6 copy.46
  18.1 0.6 copy.47
  18.7 0.6 copy.48
  19.3 0.6 copy.49
  19.9 139.3 %gather_forward.1 = (bf16[1280,3840]{1,0:T(8,128)(2,1)}, bf16[1280,1280]{1,0:T(8,128)(2,1)}, bf16[1280,5120]{1,0:T(8,128)(2,1)}, bf16[5120,1280]{1,0:T(8,128)(2,...) custom-call(bf16[640,3840]{1,0:T(8,128)(2,1)} %refs_0_.1, ...), custom_call_target="tpu_custom_call" | custom-call | tf_op jit(solution)/shard_map/gather_forward/pallas_call | solution.py:1359
  159.3 272.9 %reduce_backward.1 = (bf16[24,320,1280]{2,1,0:T(8,128)(2,1)}, bf16[1280,512]{1,0:T(8,128)(2,1)}, bf16[3840,512]{1,0:T(8,128)(2,1)}, f32[512,1280]{1,0:T(8,128)},...) custom-call(bf16[5120,512]{1,0:T(8,128)(2,1)} %get-tuple-element.29.refs_0_, ...), custom_call_target="tpu_custom_call" | custom-call | tf_op jit(solution)/shard_map/reduce_backward/pallas_call | solution.py:946
  432.2 7.1 %widen.4 = f32[640,3840]{1,0:T(8,128)} custom-call(bf16[24,320,1280]{2,1,0:T(8,128)(2,1)} %get-tuple-element.41.part), custom_call_target="tpu_custom_call" | custom-call | bytes 14745600 | tf_op jit(solution)/shard_map/widen/pallas_call | solution.py:423
  439.3 3.0 widen.5
  442.3 9.0 %widen.6 = f32[640,5120]{1,0:T(8,128)} custom-call(bf16[24,320,1280]{2,1,0:T(8,128)(2,1)} %get-tuple-element.41.part), custom_call_target="tpu_custom_call" | custom-call | bytes 19660800 | tf_op jit(solution)/shard_map/widen/pallas_call | solution.py:423
  451.3 9.0 %widen.7 = f32[2560,1280]{1,0:T(8,128)} custom-call(bf16[24,320,1280]{2,1,0:T(8,128)(2,1)} %get-tuple-element.41.part), custom_call_target="tpu_custom_call" | custom-call | bytes 19660800 | tf_op jit(solution)/shard_map/widen/pallas_call | solution.py:423
  460.3 0.6 dynamic-slice_reduce_fusion.1
  460.9 0.6 dynamic-slice_reduce_fusion
  461.5 0.6 dynamic-slice_reduce_fusion.2
  462.2 1.1 copy.52
  463.2 1.5 copy.53
  (46 shorter events, 0.5 us)
Async XLA Ops:
  1.5 10.4 %collective-permute-start = (bf16[8320]{0:T(1024)(128)(2,1)S(1)}, bf16[8320]{0:T(1024)(128)(2,1)S(1)}, u32[]{:S(2)}, u32[]{:S(2)}) collective-permute-start(bf16[8320]{0:T(1024)(128)(2,1)S(1)} %pad_add_fusion), channel_id=1, source_target_pairs={{0,1},{1,0},{2,3},{3,2},{4,5},{5,4},{6,7},{7,6},{8,9},{9,8},{10,11... | collective-permute-start | bytes 49928 | tf_op jit(solution)/shard_map/ppermute | solution.py:1403
  4.5 2.5 copy-start.13
  4.5 2.5 copy-start
  6.3 1.0 copy-start.14
  6.9 5.0 %copy-start.4 = (bf16[2560]{0:T(1024)(128)(2,1)S(1)}, bf16[2560]{0:T(1024)(128)(2,1)}, u32[]{:S(2)}) copy-start(bf16[2560]{0:T(1024)(128)(2,1)} %param.28) | copy-start | bytes 15364
  6.9 5.0 %copy-start.6 = (bf16[1920]{0:T(1024)(128)(2,1)S(1)}, bf16[1920]{0:T(1024)(128)(2,1)}, u32[]{:S(2)}) copy-start(bf16[1920]{0:T(1024)(128)(2,1)} %param.22) | copy-start | bytes 11524
  7.0 5.0 %copy-start.7 = (bf16[640]{0:T(1024)(128)(2,1)S(1)}, bf16[640]{0:T(1024)(128)(2,1)}, u32[]{:S(2)}) copy-start(bf16[640]{0:T(1024)(128)(2,1)} %param.30) | copy-start | bytes 3844
  7.0 5.0 %copy-start.8 = (bf16[640]{0:T(1024)(128)(2,1)S(1)}, bf16[640]{0:T(1024)(128)(2,1)}, u32[]{:S(2)}) copy-start(bf16[640]{0:T(1024)(128)(2,1)} %param.26) | copy-start | bytes 3844
  7.0 5.0 %copy-start.9 = (bf16[640]{0:T(1024)(128)(2,1)S(1)}, bf16[640]{0:T(1024)(128)(2,1)}, u32[]{:S(2)}) copy-start(bf16[640]{0:T(1024)(128)(2,1)} %param.25) | copy-start | bytes 3844
  7.0 5.0 %copy-start.10 = (bf16[640]{0:T(1024)(128)(2,1)S(1)}, bf16[640]{0:T(1024)(128)(2,1)}, u32[]{:S(2)}) copy-start(bf16[640]{0:T(1024)(128)(2,1)} %param.24) | copy-start | bytes 3844
  7.0 5.0 %copy-start.11 = (bf16[640]{0:T(1024)(128)(2,1)S(1)}, bf16[640]{0:T(1024)(128)(2,1)}, u32[]{:S(2)}) copy-start(bf16[640]{0:T(1024)(128)(2,1)} %param.20) | copy-start | bytes 3844
  7.0 5.0 %copy-start.12 = (bf16[640]{0:T(1024)(128)(2,1)S(1)}, bf16[640]{0:T(1024)(128)(2,1)}, u32[]{:S(2)}) copy-start(bf16[640]{0:T(1024)(128)(2,1)} %param.19) | copy-start | bytes 3844
  9.0 3.8 copy-start.3
  451.3 9.0 %copy-start.5 = (f32[1,16640]{1,0:T(1,128)S(1)}, f32[1,16640]{1,0:T(1,128)}, u32[]{:S(2)}) copy-start(f32[1,16640]{1,0:T(1,128)} %get-tuple-element.40) | copy-start | bytes 199684
  451.3 10.9 %copy-start.2 = (bf16[512,1280]{1,0:T(8,128)(2,1)S(1)}, bf16[512,1280]{1,0:T(8,128)(2,1)}, u32[]{:S(2)}) copy-start(bf16[512,1280]{1,0:T(8,128)(2,1)} %get-tuple-element.76) | copy-start | bytes 3932164
  460.3 3.0 copy-start.1

commit v7 on v6

--- a/solution.py
+++ b/solution.py
@@ -417,14 +417,19 @@
     def whole(self, chunks, w):
         first, down, rows, wide = self.first[w], self.down[w], self.rows, self.wide
 
+        pair = 2
+
         def widen(part, dst):
-            dst[...] = part[0].astype(jnp.float32)
+            for i in range(pair):
+                dst[pl.ds(i * rows, rows), :] = part[i].astype(jnp.float32)
 
         return pl.pallas_call(
             widen,
-            grid=(down, self.across[w]),
-            in_specs=[pl.BlockSpec((1, rows, wide), lambda i, j: (first + j * down + i, 0, 0))],
-            out_specs=pl.BlockSpec((rows, wide), lambda i, j: (i, j)),
+            grid=(down // pair, self.across[w]),
+            in_specs=[
+                pl.BlockSpec((pair, rows, wide), lambda i, j: ((first + j * down) // pair + i, 0, 0))
+            ],
+            out_specs=pl.BlockSpec((pair * rows, wide), lambda i, j: (i, j)),
             out_shape=jax.ShapeDtypeStruct(
                 (self.shard_rows[w], self.across[w] * wide), jnp.float32
             ),
@@ -446,7 +451,7 @@
     (
         left_0, left_1, left_2, left_3, right_0, right_1, qkv, w_qkv, w_up, w_proj,
         hidden, cotangent, patches,
-        log_total, pic_key, pic_query, cosine, sine, gain_one, gain_two, down_sum,
+        log_total, pic_key, pic_query, cosine, sine, vectors,
         out, right_2, grad_qkv, d_rows, sums, lent_left, lent_right,
         op_left, op_right, held, got_y, got_x, got_in, got_mid, total, swap, w_block,
         pre_block, turned, branch, grad_heads, rows_in, got_sums,
@@ -665,6 +670,9 @@
     tokens = qkv.shape[1]
     wide_two = right_1.shape[0]
     n_up, n_qkv = wide_two // width, qkv.shape[0] // width
+    starts = [0]
+    for size in vector_sizes(model, wide_two):
+        starts.append(starts[-1] + size)
     ends = [0]
     for size in (model, model, wide_two, model, model, model, qkv.shape[0], model):
         ends.append(ends[-1] + size)
@@ -744,7 +752,7 @@
             grad = turned[:, lanes].T
             sums[:, sums_of(0)] += jnp.sum(grad * standard, axis=0, keepdims=True)
             sums[:, sums_of(1)] += jnp.sum(grad, axis=0, keepdims=True)
-            back = norm_gradient_step(grad, standard, inverse, gain_two[...])
+            back = norm_gradient_step(grad, standard, inverse, vectors[:, pl.ds(starts[4], model)])
             back = back + rows_in[spot, :].astype(jnp.float32)
             d_rows[spot, :] = back
             low = back.astype(jnp.bfloat16)
@@ -777,7 +785,7 @@
             grad = turned[:, lanes].T
             sums[:, sums_of(4)] += jnp.sum(grad * standard, axis=0, keepdims=True)
             sums[:, sums_of(5)] += jnp.sum(grad, axis=0, keepdims=True)
-            d_rows[spot, :] += norm_gradient_step(grad, standard, inverse, gain_one[...])
+            d_rows[spot, :] += norm_gradient_step(grad, standard, inverse, vectors[:, pl.ds(starts[0], model)])
 
     def sums_to(i, device):
         return remote(sums, got_sums.at[i], sum_sem, i, device)
@@ -840,7 +848,7 @@
     load_up(0)
     clear_turned()
     sums[...] = jnp.zeros_like(sums)
-    sums[:, sums_of(3)] = down_sum[...]
+    sums[:, sums_of(3)] = vectors[:, pl.ds(starts[-1], model)]
     take_qkv.wait()
     stages = [(0, push), (1, load), (2, product), (LAGS.x, start_x), (LAGS.z, start_z)]
     stages += [(LAGS.z + LAGS.step * depth, pass_in(depth)) for depth in range(1, half)]
@@ -853,7 +861,8 @@
     stages += [(slots + 2, sent), (forward_lag, forward), (forward_lag + LAGS.end, finish)]
     stages.sort(key=lambda item: -item[0])
     per_tick = 2
-    at_norm = n_up // 2
+    at_second = 2
+    at_norm = at_second + n_up // 2
     at_heads = at_norm + 1
     at_qkv = at_heads + -(-n_heads // per_tick)
     at_one = at_qkv + n_qkv // 2
@@ -882,13 +891,13 @@
             def _():
                 stage(tick - offset)
 
-        @pl.when(tick < at_norm)
-        def _():
-            up_step(tick)
-
-        @pl.when(tick < at_norm - 1)
-        def _():
-            load_up(tick + 1)
+        @pl.when((tick >= at_second) & (tick < at_norm))
+        def _():
+            up_step(tick - at_second)
+
+        @pl.when((tick >= at_second) & (tick < at_norm - 1))
+        def _():
+            load_up(tick - at_second + 1)
 
         @pl.when(tick == at_norm - 1)
         def _():
@@ -993,14 +1002,15 @@
     n_w = len(cuts.down)
     shards, refs = refs[:n_w], refs[n_w:]
     (
-        normed, patches, cotangent, qkv_bias, proj_bias, gain, bias, up_bias, down_bias,
-        pic_key, pic_query, cosine, sine,
-    ) = refs[:13]
-    fulls, refs = refs[13 : 13 + n_w], refs[13 + n_w :]
+        patches, cotangent, own_vectors, pic_key, pic_query, cosine, sine,
+    ) = refs[:7]
+    fulls, refs = refs[7 : 7 + n_w], refs[7 + n_w :]
     (
-        swap, heads_out, log_total, hidden, two_turned, act_turned, pre_turned, layer_out,
-        hold, w_block, turned, up_pre, act, out_sum, normed_two,
-        own_in, own_out, w_sem, y_sem, d_sem, in_sem, mid_sem, back_sem, x_sem, c_sem, cd_sem,
+        swap_out, heads_to, log_total, hidden_out, two_out, act_out, pre_out, layer_out,
+        one_out, cot_out, vectors,
+        swap, heads_out, hidden, two_turned, act_turned, pre_turned, one_turned, cot_turned,
+        hold, w_block, turned, up_pre, act, out_sum, normed_two, normed, got_vectors,
+        vec_sem, give_sem, pre_sem, own_in, own_out, w_sem, y_sem, d_sem, in_sem, mid_sem, back_sem, x_sem, c_sem, cd_sem,
     ) = refs
     at = Place(n_rep)
     nz, half = at.nz, at.half
@@ -1009,9 +1019,13 @@
     unit = plane // n_rep
     straight = (rows - plane) // 2
     mine, yours = at.y, 1 - at.y
-    model = normed.shape[1]
-    tokens = normed.shape[0]
+    tokens, model = patches.shape
     head = model // n_heads
+    sizes = vector_sizes(model, up_pre.shape[1])
+    starts = [sum(sizes[:i]) for i in range(len(sizes) + 1)]
+
+    def vector(i, start=0, size=model):
+        return vectors[:, pl.ds(pl.multiple_of(starts[i] + start, 128), size)]
 
     def shard(w, row, col, first, size):
         start = pl.multiple_of(row * rows + first, 16)
@@ -1175,8 +1189,8 @@
         @pl.loop(0, wide // step)
         def _(i):
             spot = pl.ds(pl.multiple_of(i * step, 128), step)
-            col = pl.ds(pl.multiple_of(b * wide + i * step, 128), step)
-            part = contract(normed[...], w_block[u % 2, :, spot], 1, 0) + qkv_bias[:, col]
+            part = contract(normed[...], w_block[u % 2, :, spot], 1, 0)
+            part = part + vector(2, b * wide + i * step, step)
             turned[pl.ds(pl.multiple_of(i * step, 16), step), :] = part.T
 
         @pl.loop(0, n_heads)
@@ -1214,11 +1228,11 @@
             spot = pl.ds(pl.multiple_of(i * step, 16), step)
             lanes = pl.ds(pl.multiple_of(i * step, 128), step)
             branch = contract(heads_out[:, lanes], w_block[u % 2], 0, 0)
-            rows_in = patches[spot, :].astype(jnp.float32) + branch + proj_bias[...]
+            rows_in = patches[spot, :].astype(jnp.float32) + branch + vector(3)
             hidden[spot, :] = rows_in
-            out_sum[spot, :] = rows_in + down_bias[...]
+            out_sum[spot, :] = rows_in + vector(7)
             standard, _ = apply_layer_norm(rows_in)
-            result = (standard * gain[...] + bias[...]).astype(jnp.bfloat16)
+            result = (standard * vector(4) + vector(5)).astype(jnp.bfloat16)
             normed_two[spot, :] = result
             two_turned[:, lanes] = result.T
 
@@ -1230,7 +1244,8 @@
             spot = pl.ds(pl.multiple_of(i * step, 128), step)
             col = pl.multiple_of(c * wide + i * step, 128)
             cols = pl.ds(col, step)
-            pre = contract(normed_two[...], w_block[u % 2, :, spot], 1, 0) + up_bias[:, cols]
+            pre = contract(normed_two[...], w_block[u % 2, :, spot], 1, 0)
+            pre = pre + vector(6, c * wide + i * step, step)
             up_pre[:, cols] = pre
             result = (pre / (1.0 + jnp.exp(-quick_slope * pre))).astype(jnp.bfloat16)
             act[:, cols] = result
@@ -1253,6 +1268,47 @@
                 grad = contract(cotangent[spot, :], weight, 1, 1) * slope
                 pre_turned[pl.ds(col, size), lanes] = grad.astype(jnp.bfloat16).T
                 out_sum[spot, :] += contract(act[spot, pl.ds(col, size)], weight, 1, 0)
+
+            pre_give(i, owner).start()
+
+    pairs = [
+        (one_turned, one_out), (cot_turned, cot_out), (swap, swap_out),
+        (heads_out, heads_to), (hidden, hidden_out), (two_turned, two_out),
+        (act_turned, act_out),
+    ]
+    gives = [pltpu.make_async_copy(a, b, give_sem.at[i]) for i, (a, b) in enumerate(pairs)]
+
+    def pre_give(i, owner):
+        start = owner * cuts.shard_rows[3] + i * (wide // 2)
+        spot = pl.ds(pl.multiple_of(start, 16), wide // 2)
+        return pltpu.make_async_copy(
+            pre_turned.at[spot, :], pre_out.at[spot, :], pre_sem.at[owner, i]
+        )
+
+    vector_copy = remote(own_vectors, got_vectors, vec_sem, 0, at.to_y)
+    slab = 128
+
+    def join_vectors():
+        vector_copy.wait()
+        for i, size in enumerate(sizes):
+            own, spot = size // 2, pl.ds(starts[i] // 2, size // 2)
+            for y, part in ((mine, own_vectors), (yours, got_vectors)):
+                start = pl.multiple_of(starts[i] + y * own, 128)
+                vectors[:, pl.ds(start, own)] = part[:, spot]
+
+    def norm_step(i):
+        spot = pl.ds(pl.multiple_of(i * slab, 16), slab)
+        lanes = pl.ds(pl.multiple_of(i * slab, 128), slab)
+        standard, _ = apply_layer_norm(patches[spot, :].astype(jnp.float32))
+        result = (standard * vector(0) + vector(1)).astype(jnp.bfloat16)
+        normed[spot, :] = result
+        one_turned[:, lanes] = result.T
+        cot_turned[:, lanes] = cotangent[spot, :].T
+
+    def cotangent_sums():
+        ones = jnp.ones((8, tokens), jnp.bfloat16)
+        sums = contract(ones, cot_turned[...], 1, 1)[0:1, :]
+        vectors[:, pl.ds(starts[-1], model)] = sums
 
     gap = 2
     across = 1 + gap * 2 * half
@@ -1275,6 +1331,7 @@
     n_steps = 4 + n_up + n_down
 
     at.meet(True)
+    vector_copy.start()
 
     @pl.loop(0, count)
     def _(k):
@@ -1287,6 +1344,18 @@
             def _():
                 stage(tick - lag)
 
+        @pl.when(tick == 0)
+        def _():
+            join_vectors()
+
+        @pl.when((tick >= 2) & (tick % 2 == 0) & (tick <= tokens // slab * 2))
+        def _():
+            norm_step(tick // 2 - 1)
+
+        @pl.when(tick == offset)
+        def _():
+            cotangent_sums()
+
         now = tick - offset
 
         @pl.when((now >= 2) & (now < first_head) & (now % 2 == 0))
@@ -1317,6 +1386,13 @@
         def _():
             down_step(down_i, down_i + 4 + n_up)
 
+        for when, group in ((first_head, gives[:3]), (at_up, gives[3:6]), (at_down, gives[6:])):
+
+            @pl.when(now == when)
+            def _():
+                for copy in group:
+                    copy.start()
+
         soon = now + 1
 
         @pl.when((soon >= 2) & (soon < first_head) & (soon % 2 == 0))
@@ -1342,6 +1418,15 @@
 
     lax.fori_loop(0, offset + at_down + 2 * n_down - 1, tick_body, 0)
     layer_out[...] = out_sum[...].astype(jnp.bfloat16)
+    for copy in gives:
+        copy.wait()
+    for i in range(n_down):
+        for owner in range(2):
+            pre_give(i, owner).wait()
+
+
+def vector_sizes(model, wide_two):
+    return [model, model, 3 * model, model, model, model, wide_two, model]
 
 
 def gather_forward(shards, inputs, n_rep, n_heads, score_scale):
@@ -1352,6 +1437,7 @@
     low, dma = jnp.bfloat16, pltpu.SemaphoreType.DMA
     anywhere, local = pl.BlockSpec(memory_space=pl.ANY), pl.BlockSpec(memory_space=pltpu.VMEM)
     n_steps = 4 + cuts.across[2] + cuts.down[3] // 2
+    n_vectors = sum(vector_sizes(model, wide_two))
 
     def shape(*sizes, kind=low):
         return jax.ShapeDtypeStruct(sizes, kind)
@@ -1368,10 +1454,22 @@
             shape(wide_two, tokens),
             shape(wide_two, tokens),
             shape(tokens, model),
+            shape(model, tokens),
+            shape(model, tokens),
+            shape(1, n_vectors + model, kind=jnp.float32),
         ],
         in_specs=[anywhere] * len(shards) + [local] * len(inputs),
-        out_specs=[anywhere] * len(shards) + [local] * 8,
+        out_specs=[anywhere] * len(shards)
+        + [anywhere] * 2 + [local] + [anywhere] * 4 + [local] + [anywhere] * 2 + [local],
         scratch_shapes=[
+            pltpu.VMEM((3 * model, tokens), low),
+            pltpu.VMEM((model, tokens), low),
+            pltpu.VMEM((tokens, model), jnp.float32),
+            pltpu.VMEM((model, tokens), low),
+            pltpu.VMEM((wide_two, tokens), low),
+            pltpu.VMEM((wide_two, tokens), low),
+            pltpu.VMEM((model, tokens), low),
+            pltpu.VMEM((model, tokens), low),
             pltpu.VMEM((3, rows, wide), low),
             pltpu.VMEM((2, model, wide), low),
             pltpu.VMEM((model, tokens), jnp.float32),
@@ -1379,6 +1477,11 @@
             pltpu.VMEM((tokens, wide_two), low),
             pltpu.VMEM((tokens, model), jnp.float32),
             pltpu.VMEM((tokens, model), low),
+            pltpu.VMEM((tokens, model), low),
+            pltpu.VMEM((1, n_vectors // 2), jnp.float32),
+            dma((2, 1)),
+            dma((7,)),
+            dma((2, cuts.down[3] // 2)),
             dma((count,)),
             dma((count,)),
             dma((2, n_steps)),
@@ -1398,11 +1501,7 @@
         self.y = lax.axis_index("shard")
 
     def gather_vector(self, vector):
-        if self.ny != 2:
-            return lax.all_gather(vector, "shard", axis=0, tiled=False)
-        other = lax.ppermute(vector, "shard", [(0, 1), (1, 0)])
-        low, high = jnp.where(self.y == 0, vector, other), jnp.where(self.y == 0, other, vector)
-        return jnp.stack([low, high])
+        return lax.all_gather(vector, "shard", axis=0, tiled=False)
 
     def sum_all(self, vector):
         for flip in (1, 2):
@@ -1457,50 +1556,46 @@
     idents = (idents + pack_index[:, None] * lengths.shape[1]).reshape(-1)
     cosine, sine = rotary_tables(positions, head_size)
 
+    shards = [qkv_weight, proj_weight, fc1_weight, fc2_weight]
+    qkv_shape = (3 * model_width, row_count)
     small = [ln1_gain, ln1_bias, qkv_bias, proj_bias, ln2_gain, ln2_bias, fc1_bias, fc2_bias]
-    sizes = [item.shape[0] for item in small]
-    spots = [sum(sizes[:i]) for i in range(len(sizes) + 1)]
+    spots = [0]
+    for item in small:
+        spots.append(spots[-1] + item.shape[0])
     packed = sum(
         jnp.pad(item, (spots[i], spots[-1] - spots[i + 1])) for i, item in enumerate(small)
     )
-    gathered = links.gather_vector(packed)
-    (
-        first_norm_gain, first_norm_bias, b_qkv, b_proj,
-        second_norm_gain, second_norm_bias, b_up, b_down,
-    ) = [
-        gathered[:, spots[i] : spots[i + 1]].reshape(-1).astype(jnp.float32)
-        for i in range(len(sizes))
-    ]
-
-    input_rows = patches.astype(jnp.float32)
-    first_centered_standard, first_inverse_spread = apply_layer_norm(input_rows)
-    first_normalized = (first_centered_standard * first_norm_gain + first_norm_bias).astype(
-        jnp.bfloat16
-    )
-    shards = [qkv_weight, proj_weight, fc1_weight, fc2_weight]
-    qkv_shape = (3 * model_width, row_count)
-    grad_out = cotangent.astype(jnp.float32)
-    d_b_down = jnp.sum(grad_out, axis=0)
     if n_shard == 2:
-        rows_in = [
-            item[None, :]
-            for item in (b_qkv, b_proj, second_norm_gain, second_norm_bias, b_up, b_down)
-        ]
-        inputs = [first_normalized, patches, cotangent] + rows_in
-        inputs += [idents[:, None], idents[None, :], cosine, sine]
+        pictures = [idents[:, None], idents[None, :]]
+        inputs = [patches, cotangent, packed.astype(jnp.float32)[None, :]]
+        inputs += pictures + [cosine, sine]
         weights, results = gather_forward(shards, inputs, n_rep, head_count, score_scale)
         w_qkv, w_proj, w_up, w_down = weights
         qkv, heads_out, log_total, hidden_rows, second_turned = results[:5]
-        activation, grad_pre, layer_out = results[5:]
+        activation, grad_pre, layer_out, first_turned, cotangent_turned, vectors = results[5:]
         others = [qkv, w_qkv, w_up, w_proj, hidden_rows, cotangent, patches]
-        row_args = [first_norm_gain[None, :], second_norm_gain[None, :], d_b_down[None, :]]
-        small_args = [log_total, idents[:, None], idents[None, :], cosine, sine] + row_args
-        lefts = [activation, second_turned, heads_out, first_normalized.T]
-        rights = [cotangent.T, grad_pre]
+        small_args = [log_total] + pictures + [cosine, sine, vectors]
+        lefts = [activation, second_turned, heads_out, first_turned]
+        rights = [cotangent_turned, grad_pre]
         products, d_patches, total = reduce_backward(
             lefts, rights, others, small_args, n_rep, head_count, score_scale
         )
     else:
+        gathered = links.gather_vector(packed)
+        (
+            first_norm_gain, first_norm_bias, b_qkv, b_proj,
+            second_norm_gain, second_norm_bias, b_up, b_down,
+        ) = [
+            gathered[:, spots[i] : spots[i + 1]].reshape(-1).astype(jnp.float32)
+            for i in range(len(small))
+        ]
+        grad_out = cotangent.astype(jnp.float32)
+        d_b_down = jnp.sum(grad_out, axis=0)
+        input_rows = patches.astype(jnp.float32)
+        first_centered_standard, first_inverse_spread = apply_layer_norm(input_rows)
+        first_normalized = (first_centered_standard * first_norm_gain + first_norm_bias).astype(
+            jnp.bfloat16
+        )
         w_qkv, w_proj, w_up, w_down = [
             lax.all_gather(shard, "shard", axis=0, tiled=True) for shard in shards
         ]

time: 466 us -> 446 us (0.957)
  Pallas kernels: 440 us -> 432 us
  local copies, waits for them, and re-layouts: 14.9 us -> 9.21 us
    pallas_call x1, Pallas kernels: 273 us -> 264 us  [reduce_backward(): pl.pallas_call(partial(backward_kernel, n_rep, cuts, n_heads, slots, scor...]
    unnamed x41 -> x8, local copies, waits for them, and re-layouts: 10 us -> 3.71 us
  transfers between devices with their start and end apart: 1 -> 0, of which waited for: 0 -> 0; matrix products, arithmetic and copies ran while one was open for 2% -> 0% of each run, Pallas kernels for 0% -> 0%
where the time goes in v7:
time: 446 us; the launch traced here: 445 us
  Pallas kernels  432 us (97%)
  local copies, waits for them, and re-layouts  9.21 us (2%)
    pallas_call x1, Pallas kernels, reduce_backward(): pl.pallas_call(partial(backward_kernel, n_rep, cuts, n_heads, slots, scor...  264 us
    pallas_call x1, Pallas kernels, gather_forward(): pl.pallas_call(partial(forward_kernel, n_rep, cuts, n_heads, score_scale)...  141 us
    pallas_call x4, Pallas kernels, whole(): pl.pallas_call(widen, grid=(down // pair, self.across[w]), in_specs=[pl.B...  25.9 us

profile of v7, /device:TPU:0, one launch (start us, length us, event | category | flops | bytes accessed | tf_op | source)
XLA Modules:
  0.0 445.5 jit_solution(8518321656363224343)
XLA Ops:
  0.6 0.8 add_convert_fusion
  1.5 0.6 reshape.89.refs_6_
  2.1 0.8 reduce_window_sum.11
  2.9 0.1 fusion.2
  3.0 0.0 copy-start.2
  3.0 0.9 copy.32.refs_7_.refs_14_
  3.9 0.8 slice_convert_fusion.1
  4.7 0.1 broadcast_multiply_fusion.1
  4.7 1.3 fusion
  6.1 0.0 copy-done.2
  6.1 141.4 %gather_forward.1 = (bf16[1280,3840]{1,0:T(8,128)(2,1)}, bf16[1280,1280]{1,0:T(8,128)(2,1)}, bf16[1280,5120]{1,0:T(8,128)(2,1)}, bf16[5120,1280]{1,0:T(8,128)(2,...) custom-call(bf16[640,3840]{1,0:T(8,128)(2,1)} %refs_0_.1, ...), custom_call_target="tpu_custom_call" | custom-call | tf_op jit(solution)/shard_map/gather_forward/pallas_call | solution.py:1445
  147.5 264.4 %reduce_backward.1 = (bf16[24,320,1280]{2,1,0:T(8,128)(2,1)}, bf16[1280,512]{1,0:T(8,128)(2,1)}, bf16[3840,512]{1,0:T(8,128)(2,1)}, f32[512,1280]{1,0:T(8,128)},...) custom-call(bf16[5120,512]{1,0:T(8,128)(2,1)} %get-tuple-element.32.refs_0_, ...), custom_call_target="tpu_custom_call" | custom-call | tf_op jit(solution)/shard_map/reduce_backward/pallas_call | solution.py:955
  411.9 1.4 dynamic-slice_reduce_fusion.2
  413.3 6.3 %widen.4 = f32[640,3840]{1,0:T(8,128)} custom-call(bf16[24,320,1280]{2,1,0:T(8,128)(2,1)} %get-tuple-element.47.part), custom_call_target="tpu_custom_call" | custom-call | bytes 14745600 | tf_op jit(solution)/shard_map/widen/pallas_call | solution.py:426
  419.6 1.3 dynamic-slice_reduce_fusion.1
  420.9 3.3 widen.5
  424.2 8.1 %widen.6 = f32[640,5120]{1,0:T(8,128)} custom-call(bf16[24,320,1280]{2,1,0:T(8,128)(2,1)} %get-tuple-element.47.part), custom_call_target="tpu_custom_call" | custom-call | bytes 19660800 | tf_op jit(solution)/shard_map/widen/pallas_call | solution.py:426
  432.3 1.3 dynamic-slice_reduce_fusion
  433.6 0.0 copy-start.1
  433.6 8.1 %widen.7 = f32[2560,1280]{1,0:T(8,128)} custom-call(bf16[24,320,1280]{2,1,0:T(8,128)(2,1)} %get-tuple-element.47.part), custom_call_target="tpu_custom_call" | custom-call | bytes 19660800 | tf_op jit(solution)/shard_map/widen/pallas_call | solution.py:426
  441.8 0.0 copy-start
  441.8 0.0 copy-done.1
  441.8 1.1 copy.36
  442.8 1.2 copy-done
  444.0 1.5 copy.37
  (1 shorter events, 0.0 us)
Async XLA Ops:
  3.0 3.0 copy-start.2
  433.6 8.2 %copy-start.1 = (bf16[512,1280]{1,0:T(8,128)(2,1)S(1)}, bf16[512,1280]{1,0:T(8,128)(2,1)}, u32[]{:S(2)}) copy-start(bf16[512,1280]{1,0:T(8,128)(2,1)} %get-tuple-element.74) | copy-start | bytes 3932164
  441.8 2.2 copy-start

commit v8 on v7

--- a/solution.py
+++ b/solution.py
@@ -417,7 +417,7 @@
     def whole(self, chunks, w):
         first, down, rows, wide = self.first[w], self.down[w], self.rows, self.wide
 
-        pair = 2
+        pair = min(down, 4)
 
         def widen(part, dst):
             for i in range(pair):
@@ -444,7 +444,7 @@
 
 
 class LAGS:
-    x, z, step, end = 4, 6, 1, 2
+    x, z, step, end = 4, 6, 1, 1
 
 
 def backward_kernel(n_rep, cuts, n_heads, slots, score_scale, *refs):
@@ -845,11 +845,6 @@
     once(2, hidden, d_rows).start()
     once(3, cotangent, rows_in).start()
     at.meet(True)
-    load_up(0)
-    clear_turned()
-    sums[...] = jnp.zeros_like(sums)
-    sums[:, sums_of(3)] = vectors[:, pl.ds(starts[-1], model)]
-    take_qkv.wait()
     stages = [(0, push), (1, load), (2, product), (LAGS.x, start_x), (LAGS.z, start_z)]
     stages += [(LAGS.z + LAGS.step * depth, pass_in(depth)) for depth in range(1, half)]
     middle_lag = LAGS.z + LAGS.step * half
@@ -890,6 +885,14 @@
             @pl.when((tick >= offset) & (tick < count + offset))
             def _():
                 stage(tick - offset)
+
+        @pl.when(tick == at_second - 1)
+        def _():
+            load_up(0)
+            clear_turned()
+            sums[...] = jnp.zeros_like(sums)
+            sums[:, sums_of(3)] = vectors[:, pl.ds(starts[-1], model)]
+            take_qkv.wait()
 
         @pl.when((tick >= at_second) & (tick < at_norm))
         def _():

time: 446 us -> 445 us (level)
  no operation moved by 1% of the time
where the time goes in v8:
time: 445 us; the launch traced here: 444 us
  Pallas kernels  430 us (97%)
  local copies, waits for them, and re-layouts  9.21 us (2%)
    pallas_call x1, Pallas kernels, reduce_backward(): pl.pallas_call(partial(backward_kernel, n_rep, cuts, n_heads, slots, scor...  264 us
    pallas_call x1, Pallas kernels, gather_forward(): pl.pallas_call(partial(forward_kernel, n_rep, cuts, n_heads, score_scale)...  141 us
    pallas_call x4, Pallas kernels, whole(): pl.pallas_call(widen, grid=(down // pair, self.across[w]), in_specs=[pl.B...  25.1 us

profile of v8, /device:TPU:0, one launch (start us, length us, event | category | flops | bytes accessed | tf_op | source)
XLA Modules:
  0.0 444.3 jit_solution(8955880694737017761)
XLA Ops:
  0.6 0.8 add_convert_fusion
  1.5 0.6 reshape.89.refs_6_
  2.1 0.8 reduce_window_sum.11
  2.9 0.1 fusion.2
  3.0 0.0 copy-start.2
  3.0 0.9 copy.32.refs_7_.refs_14_
  3.9 0.8 slice_convert_fusion.1
  4.7 0.1 broadcast_multiply_fusion.1
  4.7 1.3 fusion
  6.1 0.0 copy-done.2
  6.1 141.4 %gather_forward.1 = (bf16[1280,3840]{1,0:T(8,128)(2,1)}, bf16[1280,1280]{1,0:T(8,128)(2,1)}, bf16[1280,5120]{1,0:T(8,128)(2,1)}, bf16[5120,1280]{1,0:T(8,128)(2,...) custom-call(bf16[640,3840]{1,0:T(8,128)(2,1)} %refs_0_.1, ...), custom_call_target="tpu_custom_call" | custom-call | tf_op jit(solution)/shard_map/gather_forward/pallas_call | solution.py:1448
  147.5 263.9 %reduce_backward.1 = (bf16[24,320,1280]{2,1,0:T(8,128)(2,1)}, bf16[1280,512]{1,0:T(8,128)(2,1)}, bf16[3840,512]{1,0:T(8,128)(2,1)}, f32[512,1280]{1,0:T(8,128)},...) custom-call(bf16[5120,512]{1,0:T(8,128)(2,1)} %get-tuple-element.32.refs_0_, ...), custom_call_target="tpu_custom_call" | custom-call | tf_op jit(solution)/shard_map/reduce_backward/pallas_call | solution.py:958
  411.4 1.4 dynamic-slice_reduce_fusion.2
  412.8 6.3 %widen.4 = f32[640,3840]{1,0:T(8,128)} custom-call(bf16[24,320,1280]{2,1,0:T(8,128)(2,1)} %get-tuple-element.47.part), custom_call_target="tpu_custom_call" | custom-call | bytes 14745600 | tf_op jit(solution)/shard_map/widen/pallas_call | solution.py:426
  419.1 1.3 dynamic-slice_reduce_fusion.1
  420.4 3.3 widen.5
  423.8 8.1 %widen.6 = f32[640,5120]{1,0:T(8,128)} custom-call(bf16[24,320,1280]{2,1,0:T(8,128)(2,1)} %get-tuple-element.47.part), custom_call_target="tpu_custom_call" | custom-call | bytes 19660800 | tf_op jit(solution)/shard_map/widen/pallas_call | solution.py:426
  431.8 1.3 dynamic-slice_reduce_fusion
  433.2 0.0 copy-start.1
  433.2 7.4 %widen.7 = f32[2560,1280]{1,0:T(8,128)} custom-call(bf16[24,320,1280]{2,1,0:T(8,128)(2,1)} %get-tuple-element.47.part), custom_call_target="tpu_custom_call" | custom-call | bytes 19660800 | tf_op jit(solution)/shard_map/widen/pallas_call | solution.py:426
  440.6 0.0 copy-start
  440.6 0.0 copy-done.1
  440.6 1.1 copy.36
  441.6 1.2 copy-done
  442.8 1.5 copy.37
  (1 shorter events, 0.0 us)
Async XLA Ops:
  3.0 3.0 copy-start.2
  433.2 7.4 %copy-start.1 = (bf16[512,1280]{1,0:T(8,128)(2,1)S(1)}, bf16[512,1280]{1,0:T(8,128)(2,1)}, u32[]{:S(2)}) copy-start(bf16[512,1280]{1,0:T(8,128)(2,1)} %get-tuple-element.74) | copy-start | bytes 3932164
  440.6 2.2 copy-start
